TPU v7x, 32 devices: a whole 2x2x4 slice. The times are simulated.
32 devices in a mesh: dp: 4 (over z), ctx: 4 (over y, core), tensor: 2 (over x).
Axes of the slice: x: 2, y: 2, z: 4, core: 2. Of those that a mesh axis runs over, the one named last changes fastest.
Arguments:
- layer_input: bfloat16 [8, 1024, 2048], P('dp', 'ctx'), may hold values from -6 to 6
- attn_gain: bfloat16 [2048], P(('dp', 'ctx')), may hold values from 0.099609375 to 1.8984375
- w_query: bfloat16 [2048, 2048], P(('dp', 'ctx'), 'tensor'), may hold values from -0.25 to 0.25
- w_key: bfloat16 [2048, 512], P(('dp', 'ctx'), 'tensor'), may hold values from -0.125 to 0.125
- w_value: bfloat16 [2048, 512], P(('dp', 'ctx'), 'tensor'), may hold values from -0.125 to 0.125
- w_out: bfloat16 [2048, 2048], P('tensor', ('dp', 'ctx')), may hold values from -0.75 to 0.75
- ffn_gain: bfloat16 [2048], P(('dp', 'ctx')), may hold values from 0.099609375 to 1.8984375
- w_gate: bfloat16 [2048, 8192], P(('dp', 'ctx'), 'tensor'), may hold values from -0.125 to 0.125
- w_up: bfloat16 [2048, 8192], P(('dp', 'ctx'), 'tensor'), may hold values from -0.125 to 0.125
- w_down: bfloat16 [8192, 2048], P('tensor', ('dp', 'ctx')), may hold values from -0.0625 to 0.0625
- cotangent: bfloat16 [8, 1024, 2048], P('dp', 'ctx'), may hold values from -6 to 6
Outputs:
- layer_output: bfloat16 [8, 1024, 2048], P('dp', 'ctx')
- input_grad: float32 [8, 1024, 2048], P('dp', 'ctx')
- attn_gain_grad: float32 [2048], P(('dp', 'ctx'))
- w_query_grad: float32 [2048, 2048], P(('dp', 'ctx'), 'tensor')
- w_key_grad: float32 [2048, 512], P(('dp', 'ctx'), 'tensor')
- w_value_grad: float32 [2048, 512], P(('dp', 'ctx'), 'tensor')
- w_out_grad: float32 [2048, 2048], P('tensor', ('dp', 'ctx'))
- ffn_gain_grad: float32 [2048], P(('dp', 'ctx'))
- w_gate_grad: float32 [2048, 8192], P(('dp', 'ctx'), 'tensor')
- w_up_grad: float32 [2048, 8192], P(('dp', 'ctx'), 'tensor')
- w_down_grad: float32 [8192, 2048], P('tensor', ('dp', 'ctx'))
All inputs are finite; a program needn't handle non-finite values.
Results may differ from a plain program's by a relative error of at most 0.017.
Values may be sent and summed in bfloat16 or wider, within the bound.
A program may use at most 256 MiB of HBM per device.

v0:
```python
import math

import jax
import jax.numpy as jnp
from jax import lax
from jax.sharding import PartitionSpec as P

HEAD_DIM = 64


EPSILON = 1e-05
ROPE_BASE = 500000.0


def rotate(values, cosine, sine_val):
    middle = values.shape[-1] // 2
    leading = values[..., :middle]
    trailing = values[..., middle:]
    return jnp.concatenate(
        [leading * cosine - trailing * sine_val, trailing * cosine + leading * sine_val], axis=-1
    )


def unrotate(gradient, cosine, sine_val):
    middle = gradient.shape[-1] // 2
    leading = gradient[..., :middle]
    trailing = gradient[..., middle:]
    return jnp.concatenate(
        [leading * cosine + trailing * sine_val, trailing * cosine - leading * sine_val], axis=-1
    )


def angles(positions, head_dim):
    exponent = jnp.arange(head_dim // 2).astype(jnp.float32) * (
        -2.0 * math.log(ROPE_BASE) / head_dim
    )
    return positions.astype(jnp.float32)[:, None] * jnp.exp(exponent)[None, :]


def rms_factor(row_values):
    return lax.rsqrt(jnp.mean(row_values * row_values, axis=-1, keepdims=True) + EPSILON)


def rms_back(upstream, row_values, factor, gain_row):
    scaled = upstream * gain_row
    gain_term = jnp.sum(upstream * row_values * factor, axis=0)
    inner_mean = jnp.mean(scaled * row_values, axis=-1, keepdims=True)
    return (factor * scaled - row_values * (factor * factor * factor) * inner_mean, gain_term)


def matmul_t(left_op, right_op):
    return lax.dot_general(
        left_op, right_op, (((0,), (0,)), ((), ())), preferred_element_type=jnp.float32
    )


def matmul_nt(left_op, right_op):
    return lax.dot_general(
        left_op, right_op, (((1,), (1,)), ((), ())), preferred_element_type=jnp.float32
    )


def on_device(
    layer_input,
    attn_gain,
    w_query,
    w_key,
    w_value,
    w_out,
    ffn_gain,
    w_gate,
    w_up,
    w_down,
    cotangent,
):
    seq_dev, span_len, model_width = layer_input.shape
    row_count = seq_dev * span_len
    length_all = span_len * lax.axis_size("ctx")
    full_q, full_k, full_v, full_o, full_gate, full_up, full_down, gain_attn, gain_ffn = (
        lax.all_gather(w_query, ("dp", "ctx"), axis=0, tiled=True),
        lax.all_gather(w_key, ("dp", "ctx"), axis=0, tiled=True),
        lax.all_gather(w_value, ("dp", "ctx"), axis=0, tiled=True),
        lax.all_gather(w_out, ("dp", "ctx"), axis=1, tiled=True),
        lax.all_gather(w_gate, ("dp", "ctx"), axis=0, tiled=True),
        lax.all_gather(w_up, ("dp", "ctx"), axis=0, tiled=True),
        lax.all_gather(w_down, ("dp", "ctx"), axis=1, tiled=True),
        lax.all_gather(attn_gain, ("dp", "ctx"), axis=0, tiled=True),
        lax.all_gather(ffn_gain, ("dp", "ctx"), axis=0, tiled=True),
    )
    kv_local = full_k.shape[1] // HEAD_DIM
    group_size = full_q.shape[1] // HEAD_DIM // kv_local
    block_count = seq_dev * kv_local
    scale = HEAD_DIM ** (-0.5)
    query_pos = lax.axis_index("ctx") * span_len + jnp.arange(span_len)
    theta = angles(query_pos, HEAD_DIM)
    cosine = jnp.cos(theta)
    sine_val = jnp.sin(theta)
    causal = query_pos[:, None] >= jnp.arange(length_all)[None, :]
    inputs_f = layer_input.reshape(row_count, model_width).astype(jnp.float32)
    gain_one = gain_attn.astype(jnp.float32)
    gain_two = gain_ffn.astype(jnp.float32)
    factor_one = rms_factor(inputs_f)
    normed_one = (inputs_f * factor_one * gain_one).astype(jnp.bfloat16)
    query_pre = jnp.dot(normed_one, full_q, preferred_element_type=jnp.float32).reshape(
        seq_dev, span_len, kv_local, group_size, HEAD_DIM
    )
    queries = rotate(
        query_pre, cosine[None, :, None, None, :], sine_val[None, :, None, None, :]
    ).astype(jnp.bfloat16)
    key_pre = jnp.dot(normed_one, full_k, preferred_element_type=jnp.float32).reshape(
        seq_dev, span_len, kv_local, HEAD_DIM
    )
    keys_own = (
        rotate(key_pre, cosine[None, :, None, :], sine_val[None, :, None, :])
        .astype(jnp.bfloat16)
        .reshape(seq_dev, span_len, kv_local * HEAD_DIM)
    )
    values_own = (
        jnp.dot(normed_one, full_v, preferred_element_type=jnp.float32)
        .astype(jnp.bfloat16)
        .reshape(seq_dev, span_len, kv_local * HEAD_DIM)
    )
    keys_all, values_all = (
        lax.all_gather(keys_own, "ctx", axis=1, tiled=True),
        lax.all_gather(values_own, "ctx", axis=1, tiled=True),
    )
    query_blocks = jnp.transpose(queries, (0, 2, 1, 3, 4)).reshape(
        block_count, span_len, group_size, HEAD_DIM
    )
    key_blocks = jnp.transpose(
        keys_all.reshape(seq_dev, length_all, kv_local, HEAD_DIM), (0, 2, 1, 3)
    ).reshape(block_count, length_all, HEAD_DIM)
    value_blocks = jnp.transpose(
        values_all.reshape(seq_dev, length_all, kv_local, HEAD_DIM), (0, 2, 1, 3)
    ).reshape(block_count, length_all, HEAD_DIM)

    def scores_of(query_b, key_b):
        raw_scores = jnp.einsum("qgd,kd->gqk", query_b, key_b, preferred_element_type=jnp.float32)
        return jnp.where(causal[None], raw_scores * scale, -1e30)

    def attend(block_in):
        query_b, key_b, value_b = block_in
        scores = scores_of(query_b, key_b)
        peak_row = jnp.max(scores, axis=-1, keepdims=True)
        powers = jnp.exp(scores - peak_row)
        total_sum = jnp.sum(powers, axis=-1, keepdims=True)
        probability = (powers / total_sum).astype(jnp.bfloat16)
        mixed = jnp.einsum("gqk,kd->qgd", probability, value_b, preferred_element_type=jnp.float32)
        return (mixed.astype(jnp.bfloat16), peak_row + jnp.log(total_sum))

    mixed_blocks, logsum = lax.map(attend, (query_blocks, key_blocks, value_blocks))
    attended = jnp.transpose(
        mixed_blocks.reshape(seq_dev, kv_local, span_len, group_size, HEAD_DIM), (0, 2, 1, 3, 4)
    ).reshape(row_count, kv_local * group_size * HEAD_DIM)
    attn_part = jnp.dot(attended, full_o, preferred_element_type=jnp.float32)
    hidden = inputs_f + lax.psum(attn_part, "tensor")
    factor_two = rms_factor(hidden)
    normed_two = (hidden * factor_two * gain_two).astype(jnp.bfloat16)
    gate_pre = jnp.dot(normed_two, full_gate, preferred_element_type=jnp.float32)
    up_pre = jnp.dot(normed_two, full_up, preferred_element_type=jnp.float32)
    sigma = jax.nn.sigmoid(gate_pre)
    product = (gate_pre * sigma * up_pre).astype(jnp.bfloat16)
    ffn_part = jnp.dot(product, full_down, preferred_element_type=jnp.float32)
    out_f = hidden + lax.psum(ffn_part.astype(jnp.bfloat16), "tensor").astype(jnp.float32)
    layer_output = out_f.astype(jnp.bfloat16).reshape(seq_dev, span_len, model_width)
    grad_out = cotangent.reshape(row_count, model_width).astype(jnp.float32)
    grad_low = cotangent.reshape(row_count, model_width)
    down_grad = matmul_t(product, grad_low)
    prod_grad = matmul_nt(grad_low, full_down)
    gate_grad = (prod_grad * up_pre * sigma * (1.0 + gate_pre * (1.0 - sigma))).astype(jnp.bfloat16)
    up_grad = (prod_grad * gate_pre * sigma).astype(jnp.bfloat16)
    gate_w_grad = matmul_t(normed_two, gate_grad)
    up_w_grad = matmul_t(normed_two, up_grad)
    normed_two_part = matmul_nt(gate_grad, full_gate) + matmul_nt(up_grad, full_up)
    normed_two_grad = lax.psum(normed_two_part, "tensor")
    hidden_back, ffn_gain_term = rms_back(normed_two_grad, hidden, factor_two, gain_two)
    hidden_grad = grad_out + hidden_back
    hidden_low = hidden_grad.astype(jnp.bfloat16)
    out_w_grad = matmul_t(attended, hidden_low)
    attended_grad = matmul_nt(hidden_low, full_o).astype(jnp.bfloat16)
    upstream_blocks = jnp.transpose(
        attended_grad.reshape(seq_dev, span_len, kv_local, group_size, HEAD_DIM), (0, 2, 1, 3, 4)
    ).reshape(block_count, span_len, group_size, HEAD_DIM)

    def attend_back(block_in):
        query_b, key_b, value_b, logsum_b, upstream_b = block_in
        scores = scores_of(query_b, key_b)
        probability = jnp.exp(scores - logsum_b)
        rounded = probability.astype(jnp.bfloat16)
        value_grad = jnp.einsum(
            "gqk,qgd->kd", rounded, upstream_b, preferred_element_type=jnp.float32
        )
        prob_grad = jnp.einsum(
            "qgd,kd->gqk", upstream_b, value_b, preferred_element_type=jnp.float32
        )
        inner_sum = jnp.sum(probability * prob_grad, axis=-1, keepdims=True)
        score_grad = (probability * (prob_grad - inner_sum)).astype(jnp.bfloat16)
        query_grad = (
            jnp.einsum("gqk,kd->qgd", score_grad, key_b, preferred_element_type=jnp.float32) * scale
        )
        key_grad = (
            jnp.einsum("gqk,qgd->kd", score_grad, query_b, preferred_element_type=jnp.float32)
            * scale
        )
        return (query_grad, key_grad, value_grad)

    query_grads, key_grads, value_grads = lax.map(
        attend_back, (query_blocks, key_blocks, value_blocks, logsum, upstream_blocks)
    )
    key_rows = jnp.transpose(
        key_grads.reshape(seq_dev, kv_local, length_all, HEAD_DIM), (0, 2, 1, 3)
    ).reshape(seq_dev, length_all, kv_local * HEAD_DIM)
    value_rows = jnp.transpose(
        value_grads.reshape(seq_dev, kv_local, length_all, HEAD_DIM), (0, 2, 1, 3)
    ).reshape(seq_dev, length_all, kv_local * HEAD_DIM)
    key_mine, value_mine = (
        lax.psum_scatter(key_rows, "ctx", scatter_dimension=1, tiled=True),
        lax.psum_scatter(value_rows, "ctx", scatter_dimension=1, tiled=True),
    )
    key_low = (
        unrotate(
            key_mine.reshape(seq_dev, span_len, kv_local, HEAD_DIM),
            cosine[None, :, None, :],
            sine_val[None, :, None, :],
        )
        .astype(jnp.bfloat16)
        .reshape(row_count, kv_local * HEAD_DIM)
    )
    value_low = value_mine.astype(jnp.bfloat16).reshape(row_count, kv_local * HEAD_DIM)
    query_rot = jnp.transpose(
        query_grads.reshape(seq_dev, kv_local, span_len, group_size, HEAD_DIM), (0, 2, 1, 3, 4)
    )
    query_low = (
        unrotate(query_rot, cosine[None, :, None, None, :], sine_val[None, :, None, None, :])
        .astype(jnp.bfloat16)
        .reshape(row_count, kv_local * group_size * HEAD_DIM)
    )
    query_w_grad = matmul_t(normed_one, query_low)
    key_w_grad = matmul_t(normed_one, key_low)
    value_w_grad = matmul_t(normed_one, value_low)
    normed_one_part = (
        matmul_nt(query_low, full_q) + matmul_nt(key_low, full_k) + matmul_nt(value_low, full_v)
    )
    normed_one_grad = lax.psum(normed_one_part.astype(jnp.bfloat16), "tensor").astype(jnp.float32)
    input_back, attn_gain_term = rms_back(normed_one_grad, inputs_f, factor_one, gain_one)
    input_grad = (hidden_grad + input_back).reshape(seq_dev, span_len, model_width)
    (
        query_sum,
        key_sum,
        value_sum,
        out_sum,
        gate_sum,
        up_sum,
        down_sum,
        attn_gain_sum,
        ffn_gain_sum,
    ) = (
        lax.psum_scatter(query_w_grad, ("dp", "ctx"), scatter_dimension=0, tiled=True),
        lax.psum_scatter(key_w_grad, ("dp", "ctx"), scatter_dimension=0, tiled=True),
        lax.psum_scatter(value_w_grad, ("dp", "ctx"), scatter_dimension=0, tiled=True),
        lax.psum_scatter(out_w_grad, ("dp", "ctx"), scatter_dimension=1, tiled=True),
        lax.psum_scatter(gate_w_grad, ("dp", "ctx"), scatter_dimension=0, tiled=True),
        lax.psum_scatter(up_w_grad, ("dp", "ctx"), scatter_dimension=0, tiled=True),
        lax.psum_scatter(down_grad, ("dp", "ctx"), scatter_dimension=1, tiled=True),
        lax.psum_scatter(attn_gain_term, ("dp", "ctx"), scatter_dimension=0, tiled=True),
        lax.psum_scatter(ffn_gain_term, ("dp", "ctx"), scatter_dimension=0, tiled=True),
    )
    return (
        layer_output,
        input_grad,
        attn_gain_sum,
        query_sum,
        key_sum,
        value_sum,
        out_sum,
        ffn_gain_sum,
        gate_sum,
        up_sum,
        down_sum,
    )


def solution(mesh):
    return jax.shard_map(
        on_device,
        mesh=mesh,
        in_specs=(
            P("dp", "ctx", None),
            P(("dp", "ctx")),
            P(("dp", "ctx"), "tensor"),
            P(("dp", "ctx"), "tensor"),
            P(("dp", "ctx"), "tensor"),
            P("tensor", ("dp", "ctx")),
            P(("dp", "ctx")),
            P(("dp", "ctx"), "tensor"),
            P(("dp", "ctx"), "tensor"),
            P("tensor", ("dp", "ctx")),
            P("dp", "ctx", None),
        ),
        out_specs=(
            P("dp", "ctx", None),
            P("dp", "ctx", None),
            P(("dp", "ctx")),
            P(("dp", "ctx"), "tensor"),
            P(("dp", "ctx"), "tensor"),
            P(("dp", "ctx"), "tensor"),
            P("tensor", ("dp", "ctx")),
            P(("dp", "ctx")),
            P(("dp", "ctx"), "tensor"),
            P(("dp", "ctx"), "tensor"),
            P("tensor", ("dp", "ctx")),
        ),
        check_vma=False,
    )
```

profile of v0, /device:TPU:0, one launch (start us, length us, event | category | flops | bytes accessed | tf_op | source)
XLA Modules:
  0.0 2554.4 jit_solution(3712881861854117042)
XLA Ops:
  8.7 23.2 all-gather
  37.6 13.2 all-gather.12.cloned.1.call-done
  56.5 33.4 %all-gather.16.cloned.1.call-done = bf16[2048,256]{1,0:T(8,128)(2,1)} async-done(((bf16[128,256]{1,0:T(8,128)(2,1)}), bf16[2048,256]{1,0:T(8,128)(2,1)}) %all-gather.16.cloned.1.call-update) | async-done | bytes 1048592 | tf_op jit(solution)/shard_map/all_gather | solution.py:81
  96.6 11.2 all-gather.14.cloned.1.call-done
  114.9 11.8 all-gather.18.cloned.1.call-done
  132.8 46.7 %all-gather.20.cloned.1.call-done = bf16[2048,1024]{1,0:T(8,128)(2,1)} async-done(((bf16[128,1024]{1,0:T(8,128)(2,1)}), bf16[2048,1024]{1,0:T(8,128)(2,1)}) %all-gather.20.cloned.1.call-update) | async-done | bytes 4194320 | tf_op jit(solution)/shard_map/all_gather | solution.py:80
  192.7 45.6 %while.28 = (s32[]{:T(128)}, bf16[8,256,4,64]{1,3,2,0:T(8,128)(2,1)}, f32[8,4,256,1]{2,1,3,0:T(4,128)S(1)}, bf16[8,1024,64]{1,2,0:T(8,128)(2,1)}, bf16[8,1024,64...) while((s32[]{:T(128)}, ...), condition=%wide.region_4.5_spmd.clone, body=%wide.region_1.4_spmd.clone.sunk | while | flops 281345024 | bytes 14191713 | solution.py:151
  250.4 18.6 all-gather.1
  269.0 85.6 %all-reduce.8.cloned.1.call-done = f32[512,2048]{1,0:T(8,128)} async-done(((f32[512,2048]{1,0:T(8,128)}), f32[512,2048]{1,0:T(8,128)}) %all-reduce.8.cloned.1.call-update) | async-done | bytes 4194320 | tf_op jit(solution)/shard_map/psum | solution.py:156
  359.9 124.1 %all-gather.24.cloned.1.call-done = bf16[2048,4096]{1,0:T(8,128)(2,1)} async-done(((bf16[128,4096]{1,0:T(8,128)(2,1)}), bf16[2048,4096]{1,0:T(8,128)(2,1)}) %all-gather.24.cloned.1.call-update) | async-done | bytes 16777232 | tf_op jit(solution)/shard_map/all_gather | solution.py:84
  484.0 14.3 fusion.89
  498.3 113.1 %all-gather.26.cloned.1.call-done = bf16[2048,4096]{1,0:T(8,128)(2,1)} async-done(((bf16[128,4096]{1,0:T(8,128)(2,1)}), bf16[2048,4096]{1,0:T(8,128)(2,1)}) %all-gather.26.cloned.1.call-update) | async-done | bytes 16777232 | tf_op jit(solution)/shard_map/all_gather | solution.py:85
  611.4 14.3 fusion.90
  625.7 116.5 %all-gather.28.cloned.1.call-done = bf16[4096,2048]{1,0:T(8,128)(2,1)} async-done(((bf16[4096,128]{1,0:T(8,128)(2,1)}), bf16[4096,2048]{1,0:T(8,128)(2,1)}) %all-gather.28.cloned.1.call-update) | async-done | bytes 16777232 | tf_op jit(solution)/shard_map/all_gather | solution.py:86
  742.2 20.3 multiply_convert_fusion
  762.5 16.4 fusion.91
  778.9 14.5 convolution_add_fusion
  793.9 105.7 %all-reduce.10.cloned.1.call-done = f32[512,2048]{1,0:T(8,128)} async-done(((f32[512,2048]{1,0:T(8,128)}), f32[512,2048]{1,0:T(8,128)}) %all-reduce.10.cloned.1.call-update) | async-done | bytes 4194320 | tf_op jit(solution)/shard_map/psum | solution.py:175
  912.1 93.4 %while.29 = (s32[]{:T(128)}, f32[8,256,4,64]{1,3,2,0:T(8,128)}, f32[8,1024,64]{1,2,0:T(8,128)}, f32[8,1024,64]{1,2,0:T(8,128)}, bf16[8,1024,64]{1,2,0:T(8,128)(2...) while((s32[]{:T(128)}, f32[8,256,4,64]{1,3,2,0:T(8,128)}, ...), condition=%wide.region_12.13_spmd.clone, body=%wide.region_10.12_spmd.clone.sunk | while | flops 687209472 | bytes 34244728 | solution.py:207
  1006.5 14.9 convolution_convert_fusion
  1038.6 32.7 %reduce-scatter.12.cloned.1.call-done = f32[2,256,256]{1,2,0:T(8,128)} async-done(((f32[2,1024,256]{1,2,0:T(8,128)}), f32[2,256,256]{1,2,0:T(8,128)}) %reduce-scatter.12.cloned.1.call-update) | async-done | bytes 524304 | tf_op jit(solution)/shard_map/reduce_scatter | solution.py:218
  1100.8 17.7 fusion.96
  1118.9 17.8 fusion.97
  1138.4 18.4 fusion.98
  1158.7 26.7 %all-reduce.12.cloned.1.call-done = (bf16[512,2048]{1,0:T(8,128)(2,1)}, bf16[512,2048]{1,0:T(8,128)(2,1)}) async-done(((bf16[512,2048]{1,0:T(8,128)(2,1)}, bf16[512,2048]{1,0:T(8,128)(2,1)}), (bf16[512,2048]{1,0:T(8,128)(2,1)}, bf16[512,2048]{1,0:T(8,128)(2,1)})) %all-reduce.12.cloned.1.call-update) | async-done | bytes 4194320 | tf_op jit(solution)/shard_map/psum | solution.py:164
  1188.6 62.1 %all-reduce.2 = (f32[2048]{0:T(1024)S(1)}, f32[2048]{0:T(1024)S(1)}) all-reduce(f32[2048]{0:T(1024)S(1)} %get-tuple-element.201, f32[2048]{0:T(1024)S(1)} %copy-done.31), channel_id=4, replica_groups=mesh['dp'=4,'ctx'=4,'tensor'=2] {'dp','ctx'}, use_global_device_ids=true, to_apply=%region_18.19.clone | all-reduce | flops 4096 | bytes 32768
  1260.1 56.3 %reduce-scatter.18.cloned.1.call-done = f32[128,256]{1,0:T(8,128)} async-done(((f32[2048,256]{1,0:T(8,128)}), f32[128,256]{1,0:T(8,128)}) %reduce-scatter.18.cloned.1.call-update) | async-done | bytes 131088 | tf_op jit(solution)/shard_map/reduce_scatter | solution.py:260
  1316.4 108.6 %reduce-scatter.14.cloned.1.call-done = f32[128,1024]{1,0:T(8,128)} async-done(((f32[2048,1024]{1,0:T(8,128)}), f32[128,1024]{1,0:T(8,128)}) %reduce-scatter.14.cloned.1.call-update) | async-done | bytes 524304 | tf_op jit(solution)/shard_map/reduce_scatter | solution.py:258
  1425.0 109.7 %reduce-scatter.20.cloned.1.call-done = f32[1024,128]{1,0:T(8,128)} async-done(((f32[1024,2048]{1,0:T(8,128)}), f32[1024,128]{1,0:T(8,128)}) %reduce-scatter.20.cloned.1.call-update) | async-done | bytes 524304 | tf_op jit(solution)/shard_map/reduce_scatter | solution.py:261
  1534.7 337.9 %reduce-scatter.22.cloned.1.call-done = f32[128,4096]{1,0:T(8,128)} async-done(((f32[2048,4096]{1,0:T(8,128)}), f32[128,4096]{1,0:T(8,128)}) %reduce-scatter.22.cloned.1.call-update) | async-done | bytes 2097168 | tf_op jit(solution)/shard_map/reduce_scatter | solution.py:262
  1872.6 337.1 %reduce-scatter.24.cloned.1.call-done = f32[128,4096]{1,0:T(8,128)} async-done(((f32[2048,4096]{1,0:T(8,128)}), f32[128,4096]{1,0:T(8,128)}) %reduce-scatter.24.cloned.1.call-update) | async-done | bytes 2097168 | tf_op jit(solution)/shard_map/reduce_scatter | solution.py:263
  2209.7 337.3 %reduce-scatter.26.cloned.1.call-done = f32[4096,128]{1,0:T(8,128)} async-done(((f32[4096,2048]{1,0:T(8,128)}), f32[4096,128]{1,0:T(8,128)}) %reduce-scatter.26.cloned.1.call-update) | async-done | bytes 2097168 | tf_op jit(solution)/shard_map/reduce_scatter | solution.py:264
  (291 shorter events, 277.7 us)
Async XLA Ops:
  7.2 43.7 %all-gather.12.cloned.1.call-start = ((), (), s32[]{:S(2)}) async-start(), calls=%async_computation.9 | async-start | bytes 1114112 | tf_op jit(solution)/shard_map/all_gather | solution.py:82
  7.9 82.0 %all-gather.16.cloned.1.call-start = ((), (), s32[]{:S(2)}) async-start(), calls=%async_computation.11 | async-start | bytes 1114112 | tf_op jit(solution)/shard_map/all_gather | solution.py:81
  8.7 99.2 %all-gather.14.cloned.1.call-start = ((), (), s32[]{:S(2)}) async-start(), calls=%async_computation.10 | async-start | bytes 1310720 | tf_op jit(solution)/shard_map/all_gather | solution.py:125
  31.9 22.7 copy-start.27
  34.0 20.6 copy-start.2
  54.3 72.4 %all-gather.18.cloned.1.call-start = ((), (), s32[]{:S(2)}) async-start(), calls=%async_computation.12 | async-start | bytes 1310720 | tf_op jit(solution)/shard_map/all_gather | solution.py:124
  54.6 136.7 %copy-start.23 = (f32[256,32]{0,1:T(8,128)}, f32[256,32]{0,1:T(8,128)S(1)}, u32[]{:S(2)}) copy-start(f32[256,32]{0,1:T(8,128)S(1)} %get-tuple-element.270) | copy-start | bytes 98308
  54.6 136.7 %copy-start.25 = (f32[256,32]{0,1:T(8,128)}, f32[256,32]{0,1:T(8,128)S(1)}, u32[]{:S(2)}) copy-start(f32[256,32]{0,1:T(8,128)S(1)} %get-tuple-element.271) | copy-start | bytes 98308
  94.8 84.6 %all-gather.20.cloned.1.call-start = ((), (), s32[]{:S(2)}) async-start(), calls=%async_computation.13 | async-start | bytes 4456448 | tf_op jit(solution)/shard_map/all_gather | solution.py:80
  95.4 145.8 %all-gather.22.cloned.1.call-start = ((), (), s32[]{:S(2)}) async-start(), calls=%async_computation.14 | async-start | bytes 4456448 | tf_op jit(solution)/shard_map/all_gather | solution.py:83
  96.0 258.6 %all-reduce.8.cloned.1.call-start = ((), (), s32[]{:S(2)}) async-start(), calls=%async_computation.15 | async-start | bytes 8388608 | tf_op jit(solution)/shard_map/psum | solution.py:156
  248.2 235.7 %all-gather.24.cloned.1.call-start = ((), (), s32[]{:S(2)}) async-start(), calls=%async_computation.16 | async-start | bytes 17825792 | tf_op jit(solution)/shard_map/all_gather | solution.py:84
  249.0 362.4 %all-gather.26.cloned.1.call-start = ((), (), s32[]{:S(2)}) async-start(), calls=%async_computation.17 | async-start | bytes 17825792 | tf_op jit(solution)/shard_map/all_gather | solution.py:85
  249.7 492.4 %all-gather.28.cloned.1.call-start = ((), (), s32[]{:S(2)}) async-start(), calls=%async_computation.18 | async-start | bytes 17825792 | tf_op jit(solution)/shard_map/all_gather | solution.py:86
  250.3 649.3 %all-reduce.10.cloned.1.call-start = ((), (), s32[]{:S(2)}) async-start(), calls=%async_computation.19 | async-start | bytes 8388608 | tf_op jit(solution)/shard_map/psum | solution.py:175
  359.9 251.5 %copy-start.16 = (bf16[512,2048]{1,0:T(8,128)(2,1)}, bf16[512,2048]{1,0:T(8,128)(2,1)S(1)}, u32[]{:S(2)}) copy-start(bf16[512,2048]{1,0:T(8,128)(2,1)S(1)} %multiply_convert_fusion.3) | copy-start | bytes 6291460
  762.5 16.4 copy-start.34
  793.4 111.5 %copy-start.19 = (bf16[2,256,2048]{2,1,0:T(8,128)(2,1)S(1)}, bf16[2,256,2048]{2,1,0:T(8,128)(2,1)}, u32[]{:S(2)}) copy-start(bf16[2,256,2048]{2,1,0:T(8,128)(2,1)} %param.25) | copy-start | bytes 6291460
  793.4 243.7 %reduce-scatter.10.cloned.1.call-start = ((), (), s32[]{:S(2)}) async-start(), calls=%async_computation.20 | async-start | bytes 2621440 | tf_op jit(solution)/shard_map/reduce_scatter | solution.py:217
  1005.5 65.8 %reduce-scatter.12.cloned.1.call-start = ((), (), s32[]{:S(2)}) async-start(), calls=%async_computation.21 | async-start | bytes 2621440 | tf_op jit(solution)/shard_map/reduce_scatter | solution.py:218
  1006.3 179.1 %all-reduce.12.cloned.1.call-start = ((), (), s32[]{:S(2)}) async-start(), calls=%async_computation.29 | async-start | bytes 8388608 | tf_op jit(solution)/shard_map/psum | solution.py:164
  1028.7 43.9 %copy-start.15 = (bf16[2048,256]{1,0:T(8,128)(2,1)S(1)}, bf16[2048,256]{1,0:T(8,128)(2,1)}, u32[]{:S(2)}) copy-start(bf16[2048,256]{1,0:T(8,128)(2,1)} %all-gather.16.cloned.1.call-done) | copy-start | bytes 3145732
  1077.0 183.1 %reduce-scatter.16.cloned.1.call-start = ((), (), s32[]{:S(2)}) async-start(), calls=%async_computation.23 | async-start | bytes 2228224 | tf_op jit(solution)/shard_map/reduce_scatter | solution.py:259
  1080.7 235.7 %reduce-scatter.18.cloned.1.call-start = ((), (), s32[]{:S(2)}) async-start(), calls=%async_computation.24 | async-start | bytes 2228224 | tf_op jit(solution)/shard_map/reduce_scatter | solution.py:260
  1082.9 342.2 %reduce-scatter.14.cloned.1.call-start = ((), (), s32[]{:S(2)}) async-start(), calls=%async_computation.22 | async-start | bytes 8912896 | tf_op jit(solution)/shard_map/reduce_scatter | solution.py:258
  1090.1 444.6 %reduce-scatter.20.cloned.1.call-start = ((), (), s32[]{:S(2)}) async-start(), calls=%async_computation.25 | async-start | bytes 8912896 | tf_op jit(solution)/shard_map/reduce_scatter | solution.py:261
  1099.3 773.4 %reduce-scatter.22.cloned.1.call-start = ((), (), s32[]{:S(2)}) async-start(), calls=%async_computation.26 | async-start | bytes 35651584 | tf_op jit(solution)/shard_map/reduce_scatter | solution.py:262
  1118.6 1091.2 %reduce-scatter.24.cloned.1.call-start = ((), (), s32[]{:S(2)}) async-start(), calls=%async_computation.27 | async-start | bytes 35651584 | tf_op jit(solution)/shard_map/reduce_scatter | solution.py:263
  1136.7 1410.4 %reduce-scatter.26.cloned.1.call-start = ((), (), s32[]{:S(2)}) async-start(), calls=%async_computation.28 | async-start | bytes 35651584 | tf_op jit(solution)/shard_map/reduce_scatter | solution.py:264
  1156.8 28.6 %copy-start.3 = (bf16[2,256,2048]{2,1,0:T(8,128)(2,1)S(1)}, bf16[2,256,2048]{2,1,0:T(8,128)(2,1)}, u32[]{:S(2)}) copy-start(bf16[2,256,2048]{2,1,0:T(8,128)(2,1)} %param.15) | copy-start | bytes 6291460
  1156.8 28.6 %copy-start.28 = (f32[16,1,128]{2,1,0:T(1,128)S(1)}, f32[16,1,128]{2,1,0:T(1,128)}, u32[]{:S(2)}) copy-start(f32[16,1,128]{2,1,0:T(1,128)} %copy-done.27) | copy-start | bytes 24580
  1156.8 31.8 %copy-start.31 = (f32[2048]{0:T(1024)S(1)}, f32[2048]{0:T(1024)}, u32[]{:S(2)}) copy-start(f32[2048]{0:T(1024)} %get-tuple-element.199) | copy-start | bytes 24580
  (24 other events, 104.7 us)
Sparse Core Ops, SparseCore 0:
  10.2 40.6 all-gather.11
  53.0 36.8 all-gather.15
  92.0 15.7 all-gather.13
  109.8 16.8 all-gather.17
  128.7 50.7 all-gather.19
  181.5 51.6 all-gather.21
  248.4 106.2 all-reduce.7
  357.0 126.8 all-gather.23
  486.4 124.9 all-gather.25
  613.6 128.5 all-gather.27
  793.5 106.0 all-reduce.9
  1005.7 31.4 reduce-scatter.9
  1039.8 31.4 reduce-scatter.11
  1077.1 108.2 all-reduce.11
  1190.0 61.6 reduce-scatter.15
  1255.9 60.4 reduce-scatter.17
  1321.5 103.5 reduce-scatter.13
  1430.1 104.5 reduce-scatter.19
  1540.1 332.4 reduce-scatter.21
  1877.9 331.7 reduce-scatter.23
  2215.1 331.8 reduce-scatter.25
where the time goes:
time: 2560 us; the launch traced here: 2550 us
  waiting for transfers between devices  2020 us (79%)
  matrix products  313 us (12%)
  blocking collectives  104 us (4%)
  other arithmetic  55.1 us (2%)
  local copies, waits for them, and re-layouts  41.7 us (2%)
    reduce_scatter x1, waiting for transfers between devices, on_device(): lax.psum_scatter(gate_w_grad, ('dp', 'ctx'), scatter_dimension=0, tiled=T...  338 us
    reduce_scatter x1, waiting for transfers between devices, on_device(): lax.psum_scatter(down_grad, ('dp', 'ctx'), scatter_dimension=1, tiled=True)  337 us
    reduce_scatter x1, waiting for transfers between devices, on_device(): lax.psum_scatter(up_w_grad, ('dp', 'ctx'), scatter_dimension=0, tiled=True)  337 us
    all_gather x1, waiting for transfers between devices, on_device(): lax.all_gather(w_gate, ('dp', 'ctx'), axis=0, tiled=True)  124 us
    all_gather x1, waiting for transfers between devices, on_device(): lax.all_gather(w_down, ('dp', 'ctx'), axis=1, tiled=True)  116 us
    all_gather x1, waiting for transfers between devices, on_device(): lax.all_gather(w_up, ('dp', 'ctx'), axis=0, tiled=True)  113 us
    reduce_scatter x1, waiting for transfers between devices, on_device(): lax.psum_scatter(out_w_grad, ('dp', 'ctx'), scatter_dimension=1, tiled=True)  110 us
    reduce_scatter x1, waiting for transfers between devices, on_device(): lax.psum_scatter(query_w_grad, ('dp', 'ctx'), scatter_dimension=0, tiled=...  109 us
  transfers between devices with their start and end apart: 21, of which 19 were waited for; matrix products, arithmetic and copies ran while one was open for 9% of the time, Pallas kernels for 0%

commit v1 on v0

--- a/solution.py
+++ b/solution.py
@@ -1,8 +1,11 @@
+import functools
 import math
 
 import jax
 import jax.numpy as jnp
 from jax import lax
+from jax.experimental import pallas as pl
+from jax.experimental.pallas import tpu as pltpu
 from jax.sharding import PartitionSpec as P
 
 HEAD_DIM = 64
@@ -280,9 +283,600 @@
     )
 
 
-def solution(mesh):
+MESH_ID = pl.DeviceIdType.MESH
+BF16 = jnp.bfloat16
+F32 = jnp.float32
+QB = 256
+
+
+def place():
+    side = lax.axis_index("tensor")
+    ctx = lax.axis_index("ctx")
+    row = ctx // 2
+    core = ctx % 2
+    near_core = {"ctx": row * 2 + (1 - core)}
+    near_side = {"tensor": 1 - side}
+    near_row = {"ctx": (1 - row) * 2 + core}
+    return side, row, core, near_core, near_side, near_row
+
+
+def greet(neighbours):
+    barrier = pltpu.get_barrier_semaphore()
+    for target in neighbours:
+        pl.semaphore_signal(barrier, inc=1, device_id=target, device_id_type=MESH_ID)
+    pl.semaphore_wait(barrier, len(neighbours))
+
+
+def remote(source, target, send_sem, recv_sem, device):
+    return pltpu.make_async_remote_copy(
+        src_ref=source,
+        dst_ref=target,
+        send_sem=send_sem,
+        recv_sem=recv_sem,
+        device_id=device,
+        device_id_type=MESH_ID,
+    )
+
+
+def gather_kernel(rows, block_ref, all_ref, send_sems, recv_sems, local_sem):
+    side, row, core, near_core, near_side, near_row = place()
+    half = rows // 2
+
+    def spot(a, b, c, part=None):
+        start = (a * 4 + b * 2 + c) * rows
+        if part is None:
+            return all_ref.at[pl.ds(pl.multiple_of(start, rows), rows)]
+        return all_ref.at[pl.ds(pl.multiple_of(start + part * half, half), half)]
+
+    greet((near_core, near_side, near_row))
+    copies = []
+
+    def send(number, source, target, device):
+        copy = remote(source, target, send_sems.at[number], recv_sems.at[number], device)
+        copy.start()
+        copies.append(copy)
+        return copy
+
+    first = block_ref.at[pl.ds(0, half)]
+    second = block_ref.at[pl.ds(half, half)]
+    side_b = send(0, second, spot(side, row, core, 1), near_side)
+    row_a = send(1, first, spot(side, row, core, 0), near_row)
+    side_a = send(2, first, spot(side, row, core, 0), near_side)
+    row_b = send(3, second, spot(side, row, core, 1), near_row)
+    core_own = send(4, block_ref, spot(side, row, core), near_core)
+    local = pltpu.make_async_copy(block_ref, spot(side, row, core), local_sem)
+    local.start()
+    side_b.wait_recv()
+    away_b = send(5, spot(1 - side, row, core, 1), spot(1 - side, row, core, 1), near_row)
+    row_a.wait_recv()
+    away_a = send(6, spot(side, 1 - row, core, 0), spot(side, 1 - row, core, 0), near_side)
+    side_a.wait_recv()
+    core_side = send(7, spot(1 - side, row, core), spot(1 - side, row, core), near_core)
+    row_b.wait_recv()
+    core_row = send(8, spot(side, 1 - row, core), spot(side, 1 - row, core), near_core)
+    away_a.wait_recv()
+    core_away_a = send(
+        9, spot(1 - side, 1 - row, core, 0), spot(1 - side, 1 - row, core, 0), near_core
+    )
+    away_b.wait_recv()
+    core_away_b = send(
+        10, spot(1 - side, 1 - row, core, 1), spot(1 - side, 1 - row, core, 1), near_core
+    )
+    for copy in (core_own, core_side, core_row, core_away_a, core_away_b):
+        copy.wait_recv()
+    for copy in copies:
+        copy.wait_send()
+    local.wait()
+
+
+def plane_gather(block):
+    rows, width = block.shape
+    return pl.pallas_call(
+        functools.partial(gather_kernel, rows),
+        out_shape=jax.ShapeDtypeStruct((8 * rows, width), block.dtype),
+        in_specs=[pl.BlockSpec(memory_space=pl.ANY)],
+        out_specs=pl.BlockSpec(memory_space=pl.ANY),
+        scratch_shapes=[
+            pltpu.SemaphoreType.DMA((11,)),
+            pltpu.SemaphoreType.DMA((11,)),
+            pltpu.SemaphoreType.DMA,
+        ],
+        compiler_params=pltpu.CompilerParams(collective_id=0, has_side_effects=True),
+        cost_estimate=pl.CostEstimate(
+            flops=0, bytes_accessed=64 * rows * width * 2, transcendentals=0
+        ),
+        name="plane_gather",
+    )(block)
+
+
+def scatter_kernel(
+    rows,
+    part_ref,
+    out_ref,
+    mine,
+    other,
+    to_side,
+    to_row,
+    from_side,
+    from_row,
+    on_side,
+    on_row,
+    got_side,
+    got_row,
+    send_sems,
+    recv_sems,
+    local_sems,
+):
+    side, row, core, near_core, near_side, near_row = place()
+    half = rows // 2
+    tile = 32
+
+    def spot(a, b, c):
+        return part_ref.at[pl.ds(pl.multiple_of((a * 4 + b * 2 + c) * rows, rows), rows)]
+
+    chips = ((side, row), (1 - side, row), (side, 1 - row), (1 - side, 1 - row))
+    locals_, pairs = {}, {}
+    for number in (3, 1, 2, 0):
+        locals_[number] = pltpu.make_async_copy(
+            spot(*chips[number], core), mine.at[number], local_sems.at[number]
+        )
+        locals_[number].start()
+    greet((near_core, near_side, near_row))
+    copies = []
+
+    def send(number, source, target, device):
+        copy = remote(source, target, send_sems.at[number], recv_sems.at[number], device)
+        copy.start()
+        copies.append(copy)
+        return copy
+
+    for number in (3, 1, 2, 0):
+        pairs[number] = send(number, spot(*chips[number], 1 - core), other.at[number], near_core)
+
+    def ready(number):
+        locals_[number].wait()
+        pairs[number].wait_recv()
+
+    def both(number, part, at):
+        at = part * half + at
+        here = mine[number, pl.ds(at, tile), :].astype(F32)
+        return here + other[number, pl.ds(at, tile), :].astype(F32)
+
+    def each(body):
+        def step(index, carry):
+            body(pl.multiple_of(index * tile, tile))
+            return carry
+
+        lax.fori_loop(0, half // tile, step, 0)
+
+    def put(target, number, part, extra=None):
+        def body(at):
+            value = both(number, part, at)
+            if extra is not None:
+                value = value + extra[pl.ds(at, tile), :].astype(F32)
+            target[pl.ds(at, tile), :] = value.astype(BF16)
+
+        each(body)
+
+    ready(3)
+    put(to_side.at[0], 3, 0)
+    side_0 = send(4, to_side.at[0], from_side.at[0], near_side)
+    put(to_row.at[0], 3, 1)
+    row_0 = send(5, to_row.at[0], from_row.at[0], near_row)
+    ready(1)
+    put(to_side.at[1], 1, 0)
+    side_1 = send(6, to_side.at[1], from_side.at[1], near_side)
+    ready(2)
+    put(to_row.at[1], 2, 1)
+    row_1 = send(7, to_row.at[1], from_row.at[1], near_row)
+    side_0.wait_recv()
+    put(on_row, 2, 0, from_side.at[0])
+    fin_row = send(8, on_row, got_row, near_row)
+    row_0.wait_recv()
+    put(on_side, 1, 1, from_row.at[0])
+    fin_side = send(9, on_side, got_side, near_side)
+    ready(0)
+    side_1.wait_recv()
+    row_1.wait_recv()
+
+    def first_sum(at):
+        out_ref[pl.ds(at, tile), :] = both(0, 0, at) + from_side[1, pl.ds(at, tile), :].astype(F32)
+        out_ref[pl.ds(half + at, tile), :] = both(0, 1, at) + from_row[
+            1, pl.ds(at, tile), :
+        ].astype(F32)
+
+    each(first_sum)
+    fin_row.wait_recv()
+    fin_side.wait_recv()
+
+    def last_sum(at):
+        out_ref[pl.ds(at, tile), :] += got_row[pl.ds(at, tile), :].astype(F32)
+        out_ref[pl.ds(half + at, tile), :] += got_side[pl.ds(at, tile), :].astype(F32)
+
+    each(last_sum)
+    for copy in copies:
+        copy.wait_send()
+
+
+def plane_scatter(partial):
+    total, width = partial.shape
+    rows = total // 8
+    half = rows // 2
+    return pl.pallas_call(
+        functools.partial(scatter_kernel, rows),
+        out_shape=jax.ShapeDtypeStruct((rows, width), F32),
+        in_specs=[pl.BlockSpec(memory_space=pl.ANY)],
+        out_specs=pl.BlockSpec(memory_space=pltpu.VMEM),
+        scratch_shapes=[
+            pltpu.VMEM((4, rows, width), BF16),
+            pltpu.VMEM((4, rows, width), BF16),
+            pltpu.VMEM((2, half, width), BF16),
+            pltpu.VMEM((2, half, width), BF16),
+            pltpu.VMEM((2, half, width), BF16),
+            pltpu.VMEM((2, half, width), BF16),
+            pltpu.VMEM((half, width), BF16),
+            pltpu.VMEM((half, width), BF16),
+            pltpu.VMEM((half, width), BF16),
+            pltpu.VMEM((half, width), BF16),
+            pltpu.SemaphoreType.DMA((10,)),
+            pltpu.SemaphoreType.DMA((10,)),
+            pltpu.SemaphoreType.DMA((4,)),
+        ],
+        compiler_params=pltpu.CompilerParams(
+            collective_id=1, has_side_effects=True, vmem_limit_bytes=32 * 1024 * 1024
+        ),
+        cost_estimate=pl.CostEstimate(
+            flops=0, bytes_accessed=8 * total * width * 2, transcendentals=0
+        ),
+        name="plane_scatter",
+    )(partial)
+
+
+def swap_halves(values):
+    width = values.shape[-1]
+    lane = lax.broadcasted_iota(jnp.int32, values.shape, 1)
+    ahead = pltpu.roll(values, width - HEAD_DIM // 2, 1)
+    behind = pltpu.roll(values, HEAD_DIM // 2, 1)
+    return jnp.where(lane % HEAD_DIM < HEAD_DIM // 2, ahead, behind)
+
+
+def pieces_of(block):
+    return ((0, block * QB, False), (block * QB, QB, True)) if block else ((0, QB, True),)
+
+
+def masked_scores(query, keys, diagonal):
+    scores = matmul_nt(query, keys)
+    if diagonal:
+        here = lax.broadcasted_iota(jnp.int32, scores.shape, 0)
+        there = lax.broadcasted_iota(jnp.int32, scores.shape, 1)
+        scores = jnp.where(here >= there, scores, -1e30)
+    return scores
+
+
+def attend_kernel(length, q_ref, kv_ref, cos_ref, sin_ref, att_ref, qrot_ref, kvrot_ref, log_ref):
+    cosine = cos_ref[...]
+    signed = sin_ref[...]
+    scale = HEAD_DIM ** (-0.5)
+    pre = q_ref[...]
+    qrot_ref[...] = (pre * cosine + swap_halves(pre) * signed).astype(BF16)
+    pre = kv_ref[...]
+    lane = lax.broadcasted_iota(jnp.int32, pre.shape, 1)
+    turned = jnp.where(lane < HEAD_DIM, pre * cosine + swap_halves(pre) * signed, pre)
+    kvrot_ref[...] = turned.astype(BF16)
+    for block in range(length // QB):
+        here = pl.ds(block * QB, QB)
+        logs = []
+        mixed = []
+        for head in range(2):
+            query = qrot_ref[here, head * HEAD_DIM : (head + 1) * HEAD_DIM] * jnp.asarray(
+                scale, BF16
+            )
+            scores = []
+            for start, size, diagonal in pieces_of(block):
+                keys = kvrot_ref[pl.ds(start, size), :HEAD_DIM]
+                scores.append(masked_scores(query, keys, diagonal))
+            peak = functools.reduce(
+                jnp.maximum, [jnp.max(s, axis=1, keepdims=True) for s in scores]
+            )
+            powers = [jnp.exp(s - peak) for s in scores]
+            total = sum(jnp.sum(p, axis=1, keepdims=True) for p in powers)
+            inverse = 1.0 / total
+            out = None
+            for (start, size, _), power in zip(pieces_of(block), powers):
+                values = kvrot_ref[pl.ds(start, size), HEAD_DIM:]
+                term = jnp.dot(
+                    (power * inverse).astype(BF16), values, preferred_element_type=F32
+                )
+                out = term if out is None else out + term
+            mixed.append(out)
+            logs.append(peak + jnp.log(total))
+        att_ref[here, :] = jnp.concatenate(mixed, axis=1).astype(BF16)
+        lane = lax.broadcasted_iota(jnp.int32, (QB, 128), 1)
+        log_ref[here, :] = jnp.where(lane < HEAD_DIM, logs[0], logs[1])
+
+
+def attend(pre, cosine, signed, seqs):
+    rows = pre.shape[0]
+    length = rows // seqs
+    pairs = pre.shape[1] // 128 - 1
+    block = (length, 128)
+    return pl.pallas_call(
+        functools.partial(attend_kernel, length),
+        grid=(seqs, pairs),
+        out_shape=(
+            jax.ShapeDtypeStruct((rows, pairs * 128), BF16),
+            jax.ShapeDtypeStruct((rows, pairs * 128), BF16),
+            jax.ShapeDtypeStruct((rows, 128), BF16),
+            jax.ShapeDtypeStruct((rows, pairs * 128), F32),
+        ),
+        in_specs=[
+            pl.BlockSpec(block, lambda s, h: (s, h)),
+            pl.BlockSpec(block, lambda s, h: (s, pairs)),
+            pl.BlockSpec(block, lambda s, h: (0, 0)),
+            pl.BlockSpec(block, lambda s, h: (0, 0)),
+        ],
+        out_specs=(
+            pl.BlockSpec(block, lambda s, h: (s, h)),
+            pl.BlockSpec(block, lambda s, h: (s, h)),
+            pl.BlockSpec(block, lambda s, h: (s, 0)),
+            pl.BlockSpec(block, lambda s, h: (s, h)),
+        ),
+        compiler_params=pltpu.CompilerParams(vmem_limit_bytes=48 * 1024 * 1024),
+        cost_estimate=pl.CostEstimate(
+            flops=8 * rows * length * 128 * pairs,
+            bytes_accessed=rows * pairs * 128 * 12,
+            transcendentals=rows * length * 2 * pairs,
+        ),
+        name="attend",
+    )(pre, pre, cosine, signed)
+
+
+def attend_back_kernel(
+    length, q_ref, kv_ref, up_ref, log_ref, cos_ref, sin_ref, dq_ref, dkv_ref, sum_ref
+):
+    pair = pl.program_id(1)
+    scale = HEAD_DIM ** (-0.5)
+
+    @pl.when(pair == 0)
+    def _():
+        sum_ref[...] = jnp.zeros_like(sum_ref)
+
+    for block in range(length // QB):
+        here = pl.ds(block * QB, QB)
+        turned = []
+        for head in range(2):
+            lanes = slice(head * HEAD_DIM, (head + 1) * HEAD_DIM)
+            query = q_ref[here, lanes] * jnp.asarray(scale, BF16)
+            upstream = up_ref[here, lanes]
+            logs = log_ref[here, head * HEAD_DIM : head * HEAD_DIM + 1]
+            saved = []
+            inner = None
+            for start, size, diagonal in pieces_of(block):
+                keys = kv_ref[pl.ds(start, size), :HEAD_DIM]
+                values = kv_ref[pl.ds(start, size), HEAD_DIM:]
+                probability = jnp.exp(masked_scores(query, keys, diagonal) - logs)
+                prob_grad = matmul_nt(upstream, values)
+                term = jnp.sum(probability * prob_grad, axis=1, keepdims=True)
+                inner = term if inner is None else inner + term
+                saved.append((start, size, probability, prob_grad))
+            out = None
+            for start, size, probability, prob_grad in saved:
+                keys = kv_ref[pl.ds(start, size), :HEAD_DIM]
+                score_grad = (probability * (prob_grad - inner)).astype(BF16)
+                rounded = probability.astype(BF16)
+                term = jnp.dot(score_grad, keys, preferred_element_type=F32)
+                out = term if out is None else out + term
+                sum_ref[pl.ds(start, size), :] += jnp.concatenate(
+                    [matmul_t(score_grad, query), matmul_t(rounded, upstream)], axis=1
+                )
+            turned.append(out * scale)
+        grad = jnp.concatenate(turned, axis=1)
+        dq_ref[here, :] = (grad * cos_ref[here, :] - swap_halves(grad) * sin_ref[here, :]).astype(
+            BF16
+        )
+
+    @pl.when(pair == pl.num_programs(1) - 1)
+    def _():
+        grad = sum_ref[...]
+        lane = lax.broadcasted_iota(jnp.int32, grad.shape, 1)
+        back = grad * cos_ref[...] - swap_halves(grad) * sin_ref[...]
+        dkv_ref[...] = jnp.where(lane < HEAD_DIM, back, grad).astype(BF16)
+
+
+def attend_back(queries, keyvals, upstream, logs, cosine, signed, seqs):
+    rows, width = queries.shape
+    length = rows // seqs
+    pairs = width // 128
+    block = (length, 128)
+    by_pair = pl.BlockSpec(block, lambda s, h: (s, h))
+    by_seq = pl.BlockSpec(block, lambda s, h: (s, 0))
+    same = pl.BlockSpec(block, lambda s, h: (0, 0))
+    return pl.pallas_call(
+        functools.partial(attend_back_kernel, length),
+        grid=(seqs, pairs),
+        out_shape=(
+            jax.ShapeDtypeStruct((rows, width), BF16),
+            jax.ShapeDtypeStruct((rows, 128), BF16),
+        ),
+        in_specs=[by_pair, by_seq, by_pair, by_pair, same, same],
+        out_specs=(by_pair, by_seq),
+        scratch_shapes=[pltpu.VMEM(block, F32)],
+        compiler_params=pltpu.CompilerParams(vmem_limit_bytes=48 * 1024 * 1024),
+        cost_estimate=pl.CostEstimate(
+            flops=20 * rows * length * 128 * pairs,
+            bytes_accessed=rows * pairs * 128 * 12,
+            transcendentals=rows * length * 2 * pairs,
+        ),
+        name="attend_back",
+    )(queries, keyvals, upstream, logs, cosine, signed)
+
+
+def to_units(weight):
+    return lax.all_to_all(weight, "ctx", split_axis=1, concat_axis=0, tiled=True)
+
+
+def from_units(grad):
+    return lax.all_to_all(grad, "ctx", split_axis=0, concat_axis=1, tiled=True)
+
+
+def on_plane(
+    layer_input,
+    attn_gain,
+    w_query,
+    w_key,
+    w_value,
+    w_out,
+    ffn_gain,
+    w_gate,
+    w_up,
+    w_down,
+    cotangent,
+):
+    seqs, span, width = layer_input.shape
+    planes = lax.axis_size("dp")
+    parts = lax.axis_size("ctx")
+    side = lax.axis_index("tensor")
+    length = span * parts
+    rows_w = w_query.shape[0]
+    q_cols = w_query.shape[1] // parts
+    kv_cols = w_key.shape[1] // parts
+
+    theta = angles(jnp.arange(length), HEAD_DIM)
+    cosine = jnp.tile(jnp.cos(theta), (1, 4))
+    sine = jnp.sin(theta)
+    signed = jnp.tile(jnp.concatenate([-sine, sine], axis=1), (1, 2))
+
+    gain_row = jnp.concatenate(
+        [attn_gain, ffn_gain, jnp.zeros((2 * q_cols + 2 * kv_cols - 2 * rows_w,), BF16)]
+    )
+    gain_rows = jnp.broadcast_to(gain_row[None, None, :], (parts, 8, gain_row.shape[0]))
+    mixed = jnp.concatenate(
+        [
+            w_query.reshape(rows_w, parts, q_cols),
+            w_key.reshape(rows_w, parts, kv_cols),
+            w_value.reshape(rows_w, parts, kv_cols),
+            w_out.T.reshape(rows_w, parts, q_cols),
+        ],
+        axis=2,
+    ).transpose(1, 0, 2)
+    mixed = jnp.concatenate([mixed, gain_rows], axis=1)
+    mixed = lax.all_to_all(mixed, "ctx", split_axis=0, concat_axis=0, tiled=True)
+    mixed = lax.all_gather(mixed, "dp", axis=0, tiled=True)
+    attn_w = mixed[:, :rows_w].reshape(width, -1)
+    gain_one = mixed[:, rows_w, :rows_w].reshape(width).astype(F32)
+    gain_two = mixed[:, rows_w, rows_w : 2 * rows_w].reshape(width).astype(F32)
+    qkv_cols = q_cols + 2 * kv_cols
+    w_qkv = attn_w[:, :qkv_cols]
+    w_out_t = attn_w[:, qkv_cols:]
+
+    gate_w, up_w, down_w = (
+        lax.all_gather(to_units(w), "dp", axis=0, tiled=True) for w in (w_gate, w_up, w_down.T)
+    )
+
+    own_in = lax.dynamic_index_in_dim(layer_input, side, 0, keepdims=False)
+    own_cot = lax.dynamic_index_in_dim(cotangent, side, 0, keepdims=False)
+    all_in = plane_gather(own_in)
+    all_cot = plane_gather(own_cot)
+
+    all_f = all_in.astype(F32)
+    normed_one = (all_f * rms_factor(all_f) * gain_one).astype(BF16)
+    pre = jnp.dot(normed_one, w_qkv, preferred_element_type=F32)
+    attended, queries, keyvals, logs = attend(pre, cosine, signed, seqs)
+    attn_part = matmul_nt(attended, w_out_t).astype(BF16)
+    inputs_f = own_in.astype(F32)
+    factor_one = rms_factor(inputs_f)
+    hidden = inputs_f + plane_scatter(attn_part)
+    factor_two = rms_factor(hidden)
+    normed_own = (hidden * factor_two * gain_two).astype(BF16)
+    normed_two = plane_gather(normed_own)
+
+    gate_pre = jnp.dot(normed_two, gate_w, preferred_element_type=F32)
+    up_pre = jnp.dot(normed_two, up_w, preferred_element_type=F32)
+    sigma = jax.nn.sigmoid(gate_pre)
+    product = (gate_pre * sigma * up_pre).astype(BF16)
+    down_grad = matmul_t(all_cot, product).astype(BF16)
+    prod_grad = jnp.dot(all_cot, down_w, preferred_element_type=F32)
+    gate_grad = (prod_grad * up_pre * sigma * (1.0 + gate_pre * (1.0 - sigma))).astype(BF16)
+    up_grad = (prod_grad * gate_pre * sigma).astype(BF16)
+    gate_w_grad = matmul_t(normed_two, gate_grad).astype(BF16)
+    up_w_grad = matmul_t(normed_two, up_grad).astype(BF16)
+    back_part = (matmul_nt(gate_grad, gate_w) + matmul_nt(up_grad, up_w)).astype(BF16)
+    ffn_part = matmul_nt(product, down_w).astype(BF16)
+    down_sum, gate_sum, up_sum = (
+        lax.psum_scatter(g, "dp", scatter_dimension=0, tiled=True)
+        for g in (down_grad, gate_w_grad, up_w_grad)
+    )
+
+    normed_two_grad = plane_scatter(back_part)
+    hidden_back, ffn_gain_term = rms_back(normed_two_grad, hidden, factor_two, gain_two)
+    hidden_grad = own_cot.astype(F32) + hidden_back
+    hidden_low = plane_gather(hidden_grad.astype(BF16))
+    attended_grad = jnp.dot(hidden_low, w_out_t, preferred_element_type=F32).astype(BF16)
+    out_w_grad = matmul_t(hidden_low, attended).astype(BF16)
+    query_low, keyval_low = attend_back(
+        queries, keyvals, attended_grad, logs, cosine, signed, seqs
+    )
+    back = jnp.concatenate([query_low, keyval_low], axis=1)
+    qkv_grad = matmul_t(normed_one, back).astype(BF16)
+    attn_grad = jnp.concatenate([qkv_grad, out_w_grad], axis=1)
+    attn_sum = lax.psum_scatter(attn_grad, "dp", scatter_dimension=0, tiled=True)
+    one_part = matmul_nt(back, w_qkv).astype(BF16)
+    normed_one_grad = plane_scatter(one_part)
+    input_back, attn_gain_term = rms_back(normed_one_grad, inputs_f, factor_one, gain_one)
+    input_own = hidden_grad + input_back
+    out_own = (hidden + plane_scatter(ffn_part)).astype(BF16)
+
+    def both_sides(own):
+        other = lax.ppermute(own, "tensor", [(0, 1), (1, 0)])
+        return jnp.where(side == 0, jnp.stack([own, other]), jnp.stack([other, own]))
+
+    layer_output = both_sides(out_own)
+    input_grad = both_sides(input_own.astype(BF16)).astype(F32)
+    gain_terms = lax.psum(jnp.stack([attn_gain_term, ffn_gain_term]), ("dp", "ctx", "tensor"))
+    own_start = (lax.axis_index("dp") * parts + lax.axis_index("ctx")) * rows_w
+    gain_own = lax.dynamic_slice_in_dim(gain_terms, own_start, rows_w, axis=1)
+
+    down_out, gate_out, up_out = (from_units(g) for g in (down_sum, gate_sum, up_sum))
+    attn_out = lax.all_to_all(
+        attn_sum.reshape(parts, rows_w, -1), "ctx", split_axis=0, concat_axis=0, tiled=True
+    )
+
+    def columns(start, size):
+        return attn_out[:, :, start : start + size].transpose(1, 0, 2).reshape(rows_w, -1)
+
+    return (
+        layer_output,
+        input_grad,
+        gain_own[0],
+        columns(0, q_cols).astype(F32),
+        columns(q_cols, kv_cols).astype(F32),
+        columns(q_cols + kv_cols, kv_cols).astype(F32),
+        columns(qkv_cols, q_cols).T.astype(F32),
+        gain_own[1],
+        gate_out.astype(F32),
+        up_out.astype(F32),
+        down_out.T.astype(F32),
+    )
+
+
+def fits_plane(mesh, shapes):
+    sizes = mesh.shape
+    seqs, length, width = shapes[0].shape
+    kv_heads = shapes[3].shape[1] // HEAD_DIM
+    return (
+        sizes["tensor"] == 2
+        and sizes["ctx"] == 4
+        and seqs == 2 * sizes["dp"]
+        and kv_heads == 8
+        and shapes[2].shape[1] == 4 * shapes[3].shape[1]
+        and length % (4 * QB) == 0
+        and width % (128 * 4 * sizes["dp"]) == 0
+    )
+
+
+def placed(mesh, function):
     return jax.shard_map(
-        on_device,
+        function,
         mesh=mesh,
         in_specs=(
             P("dp", "ctx", None),
@@ -312,3 +906,10 @@
         ),
         check_vma=False,
     )
+
+
+def solution(mesh):
+    def whole(*arrays):
+        return placed(mesh, on_plane if fits_plane(mesh, arrays) else on_device)(*arrays)
+
+    return whole

time: 2560 us -> 886 us (0.35)
  waiting for transfers between devices: 2020 us -> 107 us
  Pallas kernels: 0 us -> 389 us
  matrix products: 313 us -> 164 us
    reduce_scatter x9 -> x4, waiting for transfers between devices: 1330 us -> 82.8 us  [the longest x3 82.8 us: on_plane(): lax.psum_scatter(g, 'dp', scatter_dimension=0, tiled=True)]
    all_gather x9 -> x4, waiting for transfers between devices: 470 us -> 7.75 us  [the longest x3 7.73 us: on_plane(): lax.all_gather(to_units(w), 'dp', axis=0, tiled=True)]
    pallas_call x0 -> x10, Pallas kernels: none -> 389 us  [the longest x4 174 us: plane_scatter(): pl.pallas_call(functools.partial(scatter_kernel, rows), out_shape=jax.Sha...]
    psum x3 -> x0, waiting for transfers between devices: 218 us -> none  [the longest x1 106 us: on_device(): normed_two_grad = lax.psum(normed_two_part, 'tensor')]
    dot_general x63 -> x5, matrix products: 179 us -> 66.2 us  [the longest x1 22 us: on_plane(): prod_grad = jnp.dot(all_cot, down_w, preferred_element_type=F32)]
    psum x0 -> x1, blocking collectives: none -> 62.4 us  [on_plane(): lax.psum(jnp.stack([attn_gain_term, ffn_gain_term]), ('dp', 'ctx', 'tenso...]
    unnamed x1 -> x0, blocking collectives: 62.1 us -> none
    all_to_all x0 -> x3, blocking collectives: none -> 48.6 us  [the longest x2 33.8 us: to_units(): lax.all_to_all(weight, 'ctx', split_axis=1, concat_axis=0, tiled=True)]
  transfers between devices with their start and end apart: 21 -> 15, of which waited for: 19 -> 6; matrix products, arithmetic and copies ran while one was open for 9% -> 16% of each run, Pallas kernels for 0% -> 27%
where the time goes in v1:
time: 886 us; the launch traced here: 877 us
  Pallas kernels  389 us (44%)
  matrix products  164 us (19%)
  blocking collectives  111 us (13%)
  waiting for transfers between devices  107 us (12%)
  other arithmetic  35.7 us (4%)
  local copies, waits for them, and re-layouts  32.2 us (4%)
  starting transfers between devices  22.5 us (3%)
  between operations  15.2 us (2%)
    pallas_call x4, Pallas kernels, plane_scatter(): pl.pallas_call(functools.partial(scatter_kernel, rows), out_shape=jax.Sha...  174 us
    pallas_call x4, Pallas kernels, plane_gather(): pl.pallas_call(functools.partial(gather_kernel, rows), out_shape=jax.Shap...  166 us
    reduce_scatter x3, waiting for transfers between devices, on_plane(): lax.psum_scatter(g, 'dp', scatter_dimension=0, tiled=True)  82.8 us
    psum x1, blocking collectives, on_plane(): lax.psum(jnp.stack([attn_gain_term, ffn_gain_term]), ('dp', 'ctx', 'tenso...  62.4 us
    dot_general x5, matrix products, matmul_t(): lax.dot_general(left_op, right_op, (((0,), (0,)), ((), ())), preferred_el...  52.8 us
    dot_general x5, matrix products, matmul_nt(): lax.dot_general(left_op, right_op, (((1,), (1,)), ((), ())), preferred_el...  45.4 us
    all_to_all x2, blocking collectives, to_units(): lax.all_to_all(weight, 'ctx', split_axis=1, concat_axis=0, tiled=True)  33.8 us
    pallas_call x1, Pallas kernels, attend_back(): pl.pallas_call(functools.partial(attend_back_kernel, length), grid=(seqs,...  28.4 us
  transfers between devices with their start and end apart: 15, of which 6 were waited for; matrix products, arithmetic and copies ran while one was open for 16% of the time, Pallas kernels for 27%

profile of v1, /device:TPU:0, one launch (start us, length us, event | category | flops | bytes accessed | tf_op | source)
XLA Modules:
  0.0 877.1 jit_solution(9877760650984650358)
XLA Ops:
  13.1 14.8 %all_to_all.106 = bf16[4,136,640]{2,1,0:T(8,128)(2,1)} all-to-all(bf16[4,136,640]{2,1,0:T(8,128)(2,1)S(1)} %copy.96), channel_id=1, replica_groups=mesh['dp'=4,'ctx'=4,'tensor'=2] {'ctx'}, dimensions={0} | all-to-all | bytes 1392640 | tf_op jit(solution)/shard_map/all_to_all | solution.py:763
  28.7 16.9 %all_to_all.107 = bf16[128,4,1024]{0,2,1:T(8,128)(2,1)S(1)} all-to-all(bf16[128,4,1024]{0,2,1:T(8,128)(2,1)S(1)} %bitcast.121), channel_id=1, replica_groups=mesh['dp'=4,'ctx'=4,'tensor'=2] {'ctx'}, dimensions={1} | all-to-all | bytes 2097152 | tf_op jit(solution)/shard_map/all_to_all | solution.py:715
  48.6 16.9 %all_to_all.108 = bf16[128,4,1024]{0,2,1:T(8,128)(2,1)S(1)} all-to-all(bf16[128,4,1024]{0,2,1:T(8,128)(2,1)S(1)} %bitcast.122), channel_id=1, replica_groups=mesh['dp'=4,'ctx'=4,'tensor'=2] {'ctx'}, dimensions={1} | all-to-all | bytes 2097152 | tf_op jit(solution)/shard_map/all_to_all | solution.py:715
  74.0 46.6 %plane_gather.6 = bf16[2048,2048]{1,0:T(8,128)(2,1)} custom-call(bf16[256,2048]{1,0:T(8,128)(2,1)} %dynamic-slice_bitcast_fusion.block_ref), custom_call_target="tpu_custom_call" | custom-call | bytes 67108864 | tf_op jit(solution)/shard_map/plane_gather/pallas_call | solution.py:374
  123.7 40.1 %plane_gather.4 = bf16[2048,2048]{1,0:T(8,128)(2,1)} custom-call(bf16[256,2048]{1,0:T(8,128)(2,1)} %get-tuple-element.72.block_ref), custom_call_target="tpu_custom_call" | custom-call | bytes 67108864 | tf_op jit(solution)/shard_map/plane_gather/pallas_call | solution.py:374
  173.3 11.2 %fusion.4.q_ref.kv_ref = f32[2048,384]{1,0:T(8,128)} fusion(bf16[2048,2048]{1,0:T(8,128)(2,1)} %plane_gather.4, f32[2048]{0:T(1024)S(1)} %fusion.21, f32[2048]{0:T(1024)S(1)} %add_rsqrt_fusion, bf16[2048,640]{1,0:T(8,128)(2,1)S(1)} %bitcast.110), kind=kOutput, calls=%fused_computation.25 | convolution fusion | flops 3238002688 | bytes 13123584 | tf_op jit(solution)/shard_map/dot_general | solution.py:783
  184.5 20.6 %attend.1 = (bf16[2048,256]{1,0:T(8,128)(2,1)S(1)}, bf16[2048,256]{1,0:T(8,128)(2,1)S(1)}, bf16[2048,128]{1,0:T(8,128)(2,1)S(1)}, f32[2048,256]{1,0:T(8,128)S(1)}) custom-call(f32[2048,384]{1,0:T(8,128)} %fusion.4.q_ref.kv_ref, f32[2048,384]{1,0:T(8,128)} %fusion.4.q_ref.kv_ref, f32[1024,128]{1,0:T(8,128)S(1)} %copy.98.cos_ref, f32[1024,128]{1,0:T(8,128)S(1)} %copy.99.sin_ref), custom_call_target="tpu_custom_call" | custom-call | flops 4294967296 | bytes 6291456 | tf_op jit(solution)/shard_map/attend/pallas_call | solution.py:603
  208.8 40.4 %plane_scatter.4 = f32[256,2048]{1,0:T(8,128)S(1)} custom-call(bf16[2048,2048]{1,0:T(8,128)(2,1)S(1)} %convolution_convert_fusion.2.part_ref), custom_call_target="tpu_custom_call" | custom-call | bytes 67108864 | tf_op jit(solution)/shard_map/plane_scatter/pallas_call | solution.py:505
  252.1 39.8 %plane_gather.5 = bf16[2048,2048]{1,0:T(8,128)(2,1)} custom-call(bf16[256,2048]{1,0:T(8,128)(2,1)} %multiply_convert_fusion.3.block_ref), custom_call_target="tpu_custom_call" | custom-call | bytes 67108864 | tf_op jit(solution)/shard_map/plane_gather/pallas_call | solution.py:374
  292.0 14.5 %fusion.25 = f32[2048,1024]{1,0:T(8,128)} fusion(bf16[2048,2048]{1,0:T(8,128)(2,1)} %plane_gather.5, bf16[2048,1024]{1,0:T(8,128)(2,1)} %all-gather.9.cloned.1.call-done), kind=kOutput, calls=%fused_computation.86 | convolution fusion | flops 8589934592 | bytes 20971520 | tf_op jit(solution)/shard_map/dot_general | solution.py:794
  306.5 14.9 %fusion.24 = f32[2048,1024]{1,0:T(8,128)} fusion(bf16[2048,2048]{1,0:T(8,128)(2,1)} %plane_gather.5, bf16[2048,1024]{1,0:T(8,128)(2,1)} %all-gather.7.cloned.1.call-done), kind=kOutput, calls=%fused_computation.85 | convolution fusion | flops 8589934592 | bytes 20971520 | tf_op jit(solution)/shard_map/dot_general | solution.py:793
  321.4 7.7 all-gather.11.cloned.1.call-done
  329.1 22.0 %multiply_convert_fusion = (bf16[2048,1024]{1,0:T(8,128)(2,1)}, bf16[2048,1024]{1,0:T(8,128)(2,1)}, bf16[2048,1024]{1,0:T(8,128)(2,1)}) fusion(f32[2048,1024]{1,0:T(8,128)} %fusion.24, f32[2048,1024]{1,0:T(8,128)} %fusion.25, bf16[2048,2048]{1,0:T(8,128)(2,1)} %plane_gather.6, bf16[2048,1024]{1,0:T(8,128)(2,1)} %all-gather.11.cloned.1.call-done), kind=kOutput, calls=%fused_computation.6 | convolution fusion | flops 8623489024 | bytes 41943040 | tf_op jit(solution)/shard_map/dot_general | solution.py:798
  351.1 10.7 %convolution_convert_fusion.1.part_ref = bf16[2048,2048]{1,0:T(8,128)(2,1)S(1)} fusion(bf16[2048,1024]{1,0:T(8,128)(2,1)} %get-tuple-element.79, bf16[2048,1024]{1,0:T(8,128)(2,1)S(1)} %copy-done.27), kind=kOutput, calls=%fused_computation.11 | convolution fusion | flops 8594128896 | bytes 16777216 | tf_op jit(solution)/shard_map/dot_general | solution.py:61
  361.8 40.7 %plane_scatter.5 = f32[256,2048]{1,0:T(8,128)S(1)} custom-call(bf16[2048,2048]{1,0:T(8,128)(2,1)S(1)} %convolution_convert_fusion.1.part_ref), custom_call_target="tpu_custom_call" | custom-call | bytes 67108864 | tf_op jit(solution)/shard_map/plane_scatter/pallas_call | solution.py:505
  403.9 11.7 %fusion.26 = f32[2048,2048]{1,0:T(8,128)} fusion(bf16[2048,1024]{1,0:T(8,128)(2,1)S(1)} %copy-done.28, bf16[2048,1024]{1,0:T(8,128)(2,1)S(1)} %copy-done.26), kind=kOutput, calls=%fused_computation.87 | convolution fusion | flops 8589934592 | bytes 25165824 | tf_op jit(solution)/shard_map/dot_general | solution.py:61
  415.6 14.4 %add_convert_fusion.part_ref = bf16[2048,2048]{1,0:T(8,128)(2,1)S(1)} fusion(f32[2048,2048]{1,0:T(8,128)} %fusion.26, bf16[2048,1024]{1,0:T(8,128)(2,1)} %get-tuple-element.77, bf16[2048,1024]{1,0:T(8,128)(2,1)} %all-gather.9.cloned.1.call-done), kind=kOutput, calls=%fused_computation.5 | convolution fusion | flops 8598323200 | bytes 33554432 | tf_op jit(solution)/shard_map/dot_general | solution.py:61
  430.0 40.4 %plane_scatter.6 = f32[256,2048]{1,0:T(8,128)S(1)} custom-call(bf16[2048,2048]{1,0:T(8,128)(2,1)S(1)} %add_convert_fusion.part_ref), custom_call_target="tpu_custom_call" | custom-call | bytes 67108864 | tf_op jit(solution)/shard_map/plane_scatter/pallas_call | solution.py:505
  475.4 39.6 %plane_gather.7 = bf16[2048,2048]{1,0:T(8,128)(2,1)} custom-call(bf16[256,2048]{1,0:T(8,128)(2,1)} %get-tuple-element.73.block_ref), custom_call_target="tpu_custom_call" | custom-call | bytes 67108864 | tf_op jit(solution)/shard_map/plane_gather/pallas_call | solution.py:374
  515.0 5.9 convolution_convert_fusion.7
  524.8 28.4 %attend_back.1 = (bf16[2048,256]{1,0:T(8,128)(2,1)S(1)}, bf16[2048,128]{1,0:T(8,128)(2,1)S(1)}) custom-call(bf16[2048,256]{1,0:T(8,128)(2,1)S(1)} %copy-done.8, bf16[2048,128]{1,0:T(8,128)(2,1)S(1)} %copy-done.10, bf16[2048,256]{1,0:T(8,128)(2,1)S(1)} %convolution_convert_fusion.8.up_ref, f32[2048,256]{1,0:T(8,128)} %copy-done.6, f32[1024,128]{1,0:T(8,128)S(1)} %copy-done.5, ...), custom_call_target="tpu_custom_call" | custom-call | flops 10737418240 | bytes 6291456 | tf_op jit(solution)/shard_map/attend_back/pallas_call | solution.py:694
  559.3 14.4 %convolution_convert_fusion.3 = bf16[2048,1024]{1,0:T(8,128)(2,1)} fusion(bf16[2048,2048]{1,0:T(8,128)(2,1)} %plane_gather.6, bf16[2048,1024]{1,0:T(8,128)(2,1)} %get-tuple-element.79), kind=kOutput, calls=%fused_computation.18 | convolution fusion | flops 8592031744 | bytes 16777216 | tf_op jit(solution)/shard_map/dot_general | solution.py:55
  573.8 14.1 %convolution_convert_fusion.5 = bf16[2048,1024]{1,0:T(8,128)(2,1)} fusion(bf16[2048,2048]{1,0:T(8,128)(2,1)} %plane_gather.5, bf16[2048,1024]{1,0:T(8,128)(2,1)} %get-tuple-element.78), kind=kOutput, calls=%fused_computation.20 | convolution fusion | flops 8592031744 | bytes 16777216 | tf_op jit(solution)/shard_map/dot_general | solution.py:55
  588.0 14.3 %convolution_convert_fusion.4 = bf16[2048,1024]{1,0:T(8,128)(2,1)} fusion(bf16[2048,2048]{1,0:T(8,128)(2,1)} %plane_gather.5, bf16[2048,1024]{1,0:T(8,128)(2,1)} %get-tuple-element.77), kind=kOutput, calls=%fused_computation.19 | convolution fusion | flops 8592031744 | bytes 16777216 | tf_op jit(solution)/shard_map/dot_general | solution.py:55
  604.0 6.2 convolution_convert_fusion.part_ref
  610.2 52.6 %plane_scatter.7 = f32[256,2048]{1,0:T(8,128)S(1)} custom-call(bf16[2048,2048]{1,0:T(8,128)(2,1)S(1)} %convolution_convert_fusion.part_ref), custom_call_target="tpu_custom_call" | custom-call | bytes 67108864 | tf_op jit(solution)/shard_map/plane_scatter/pallas_call | solution.py:505
  669.6 9.7 %all-to-all-done.4 = bf16[4,128,640]{1,2,0:T(8,128)(2,1)} async-done(((bf16[4,128,640]{1,2,0:T(8,128)(2,1)}), bf16[4,128,640]{1,2,0:T(8,128)(2,1)}, u32[]{:S(2)}, u32[]{:S(2)}) %all-to-all-start.4) | async-done | bytes 655392 | tf_op jit(solution)/shard_map/all_to_all | solution.py:840
  679.3 8.8 %reduce-scatter.11.cloned.1.call-done = bf16[512,1024]{1,0:T(8,128)(2,1)} async-done(((bf16[2048,1024]{1,0:T(8,128)(2,1)}), bf16[512,1024]{1,0:T(8,128)(2,1)}) %reduce-scatter.11.cloned.1.call-update) | async-done | bytes 1048592 | tf_op jit(solution)/shard_map/reduce_scatter | solution.py:806
  697.1 62.4 %psum.7 = f32[2,2048]{1,0:T(2,128)S(1)} all-reduce(f32[2,2048]{1,0:T(2,128)S(1)} %pad_maximum_fusion.3), channel_id=1, replica_groups=mesh['dp'=4,'ctx'=4,'tensor'=2] {'dp','ctx','tensor'}, use_global_device_ids=true, to_apply=%region_7.8 | all-reduce | flops 4096 | bytes 32768 | tf_op jit(solution)/shard_map/psum | solution.py:835
  760.0 8.9 %reduce-scatter.7.cloned.1.call-done = bf16[512,1024]{1,0:T(8,128)(2,1)} async-done(((bf16[2048,1024]{1,0:T(8,128)(2,1)}), bf16[512,1024]{1,0:T(8,128)(2,1)}) %reduce-scatter.7.cloned.1.call-update) | async-done | bytes 1048592 | tf_op jit(solution)/shard_map/reduce_scatter | solution.py:806
  783.3 65.1 %reduce-scatter.9.cloned.1.call-done = bf16[512,1024]{1,0:T(8,128)(2,1)} async-done(((bf16[2048,1024]{1,0:T(8,128)(2,1)}), bf16[512,1024]{1,0:T(8,128)(2,1)}) %reduce-scatter.9.cloned.1.call-update) | async-done | bytes 1048592 | tf_op jit(solution)/shard_map/reduce_scatter | solution.py:806
  860.5 6.6 all-to-all-done.6
  (158 shorter events, 100.8 us)
Async XLA Ops:
  7.2 163.1 %all-gather.5.cloned.1.call-start = ((), (), s32[]{:S(2)}) async-start(), calls=%async_computation.12 | async-start | bytes 3481600 | tf_op jit(solution)/shard_map/all_gather | solution.py:764
  11.0 17.0 %copy-start.19 = (bf16[128,4096]{1,0:T(8,128)(2,1)S(1)}, bf16[128,4096]{1,0:T(8,128)(2,1)}, u32[]{:S(2)}) copy-start(bf16[128,4096]{1,0:T(8,128)(2,1)} %param.19) | copy-start | bytes 3145732
  28.0 264.1 %all-gather.9.cloned.1.call-start = ((), (), s32[]{:S(2)}) async-start(), calls=%async_computation.14 | async-start | bytes 5242880 | tf_op jit(solution)/shard_map/all_gather | solution.py:773
  46.9 259.6 %all-gather.7.cloned.1.call-start = ((), (), s32[]{:S(2)}) async-start(), calls=%async_computation.13 | async-start | bytes 5242880 | tf_op jit(solution)/shard_map/all_gather | solution.py:773
  66.8 102.1 %all-to-all-start.3 = ((bf16[128,4,1024]{0,2,1:T(8,128)(2,1)}), bf16[128,4,1024]{0,2,1:T(8,128)(2,1)S(1)}, u32[]{:S(2)}, u32[]{:S(2)}) async-start(bf16[128,4,1024]{0,2,1:T(8,128)(2,1)} %bitcast.19), calls=%async_computation.3 | async-start | bytes 2097152 | tf_op jit(solution)/shard_map/all_to_all | solution.py:715
  70.4 258.7 %all-gather.11.cloned.1.call-start = ((), (), s32[]{:S(2)}) async-start(), calls=%async_computation.15 | async-start | bytes 5242880 | tf_op jit(solution)/shard_map/all_gather | solution.py:773
  71.2 113.2 %copy-start.2 = (f32[1024,128]{1,0:T(8,128)}, f32[1024,128]{1,0:T(8,128)S(1)}, u32[]{:S(2)}) copy-start(f32[1024,128]{1,0:T(8,128)S(1)} %copy.99.sin_ref) | copy-start | bytes 1572868
  71.5 112.9 %copy-start.4 = (f32[1024,128]{1,0:T(8,128)}, f32[1024,128]{1,0:T(8,128)S(1)}, u32[]{:S(2)}) copy-start(f32[1024,128]{1,0:T(8,128)S(1)} %copy.98.cos_ref) | copy-start | bytes 1572868
  168.9 4.4 copy-start.23
  170.3 492.5 %reduce-scatter.5.cloned.1.call-start = ((), (), s32[]{:S(2)}) async-start(), calls=%async_computation.16 | async-start | bytes 3276800 | tf_op jit(solution)/shard_map/reduce_scatter | solution.py:822
  171.1 13.3 %copy-start.21 = (f32[2048]{0:T(1024)}, f32[2048]{0:T(1024)S(1)}, u32[]{:S(2)}) copy-start(f32[2048]{0:T(1024)S(1)} %fusion.21) | copy-start | bytes 24580
  173.2 33.2 %copy-start.16 = (bf16[16,128,640]{2,1,0:T(8,128)(2,1)}, bf16[16,128,640]{2,1,0:T(8,128)(2,1)S(1)}, u32[]{:S(2)}) copy-start(bf16[16,128,640]{2,1,0:T(8,128)(2,1)S(1)} %slice.45) | copy-start | bytes 7864324
  208.8 40.4 %copy-start.13 = (bf16[256,2048]{1,0:T(8,128)(2,1)S(1)}, bf16[256,2048]{1,0:T(8,128)(2,1)}, u32[]{:S(2)}) copy-start(bf16[256,2048]{1,0:T(8,128)(2,1)} %get-tuple-element.72.block_ref) | copy-start | bytes 3145732
  329.1 22.0 %copy-start.27 = (bf16[2048,1024]{1,0:T(8,128)(2,1)S(1)}, bf16[2048,1024]{1,0:T(8,128)(2,1)}, u32[]{:S(2)}) copy-start(bf16[2048,1024]{1,0:T(8,128)(2,1)} %all-gather.11.cloned.1.call-done) | copy-start | bytes 12582916
  361.8 42.1 %copy-start.26 = (bf16[2048,1024]{1,0:T(8,128)(2,1)S(1)}, bf16[2048,1024]{1,0:T(8,128)(2,1)}, u32[]{:S(2)}) copy-start(bf16[2048,1024]{1,0:T(8,128)(2,1)} %all-gather.7.cloned.1.call-done) | copy-start | bytes 12582916
  361.8 42.1 %copy-start.28 = (bf16[2048,1024]{1,0:T(8,128)(2,1)S(1)}, bf16[2048,1024]{1,0:T(8,128)(2,1)}, u32[]{:S(2)}) copy-start(bf16[2048,1024]{1,0:T(8,128)(2,1)} %get-tuple-element.78) | copy-start | bytes 12582916
  430.0 40.4 %copy-start.12 = (f32[256,2048]{1,0:T(8,128)S(1)}, f32[256,2048]{1,0:T(8,128)}, u32[]{:S(2)}) copy-start(f32[256,2048]{1,0:T(8,128)} %copy-done.11) | copy-start | bytes 6291460
  515.0 5.9 copy-start.15
  521.0 32.4 %slice-start = ((s8[8388608]{0:T(1024)(128)(4,1)}), s8[4194304]{0:T(1024)(128)(4,1)S(1)}, s32[]{:S(2)}) async-start(s8[8388608]{0:T(1024)(128)(4,1)} %bitcast.108), calls=%async_computation.20 | async-start | bytes 8388608
  524.8 28.6 %slice-start.1 = ((s8[8388608]{0:T(1024)(128)(4,1)}), s8[4194304]{0:T(1024)(128)(4,1)S(1)}, s32[]{:S(2)}) async-start(s8[8388608]{0:T(1024)(128)(4,1)} %bitcast.108), calls=%async_computation.21 | async-start | bytes 8388608
  524.8 28.6 %copy-start.22 = (f32[2048]{0:T(1024)S(1)}, f32[2048]{0:T(1024)}, u32[]{:S(2)}) copy-start(f32[2048]{0:T(1024)} %copy-done.21) | copy-start | bytes 24580
  524.8 28.6 %copy-start.24 = (f32[2048]{0:T(1024)S(1)}, f32[2048]{0:T(1024)}, u32[]{:S(2)}) copy-start(f32[2048]{0:T(1024)} %copy-done.23) | copy-start | bytes 24580
  559.3 128.9 %reduce-scatter.11.cloned.1.call-start = ((), (), s32[]{:S(2)}) async-start(), calls=%async_computation.19 | async-start | bytes 5242880 | tf_op jit(solution)/shard_map/reduce_scatter | solution.py:806
  573.7 195.1 %reduce-scatter.7.cloned.1.call-start = ((), (), s32[]{:S(2)}) async-start(), calls=%async_computation.17 | async-start | bytes 5242880 | tf_op jit(solution)/shard_map/reduce_scatter | solution.py:806
  587.9 260.5 %reduce-scatter.9.cloned.1.call-start = ((), (), s32[]{:S(2)}) async-start(), calls=%async_computation.18 | async-start | bytes 5242880 | tf_op jit(solution)/shard_map/reduce_scatter | solution.py:806
  602.9 169.5 %collective-permute-start = (bf16[256,2048]{1,0:T(8,128)(2,1)}, bf16[256,2048]{1,0:T(8,128)(2,1)}, u32[]{:S(2)}, u32[]{:S(2)}) collective-permute-start(bf16[256,2048]{1,0:T(8,128)(2,1)} %get-tuple-element.82), channel_id=1, source_target_pairs={{0,1},{1,0},{2,3},{3,2},{4,5},{5,4},{6,7},{7,6},{8,9},{9,8},{10,11... | collective-permute-start | bytes 3145736 | tf_op jit(solution)/shard_map/ppermute | solution.py:830
  610.2 58.8 %copy-start.14 = (bf16[256,2048]{1,0:T(8,128)(2,1)S(1)}, bf16[256,2048]{1,0:T(8,128)(2,1)}, u32[]{:S(2)}) copy-start(bf16[256,2048]{1,0:T(8,128)(2,1)} %get-tuple-element.72.block_ref) | copy-start | bytes 3145732
  664.8 14.5 %all-to-all-start.4 = ((bf16[4,128,640]{1,2,0:T(8,128)(2,1)}), bf16[4,128,640]{1,2,0:T(8,128)(2,1)}, u32[]{:S(2)}, u32[]{:S(2)}) async-start(bf16[4,128,640]{1,2,0:T(8,128)(2,1)} %copy_bitcast_fusion), calls=%async_computation.5 | async-start | bytes 1310720 | tf_op jit(solution)/shard_map/all_to_all | solution.py:840
  688.1 80.8 %all-to-all-start.7 = ((bf16[4,128,1024]{2,1,0:T(8,128)(2,1)}), bf16[4,128,1024]{2,1,0:T(8,128)(2,1)}, u32[]{:S(2)}, u32[]{:S(2)}) async-start(bf16[4,128,1024]{2,1,0:T(8,128)(2,1)} %bitcast.133), calls=%async_computation.11 | async-start | bytes 2097152 | tf_op jit(solution)/shard_map/all_to_all | solution.py:719
  695.6 80.9 %collective-permute-start.1 = (bf16[256,2048]{1,0:T(8,128)(2,1)}, bf16[256,2048]{1,0:T(8,128)(2,1)S(1)}, u32[]{:S(2)}, u32[]{:S(2)}) collective-permute-start(bf16[256,2048]{1,0:T(8,128)(2,1)} %fusion.10), channel_id=1, source_target_pairs={{0,1},{1,0},{2,3},{3,2},{4,5},{5,4},{6,7},{7,6},{8,9},{9,8},{10,11... | collective-permute-start | bytes 3145736 | tf_op jit(solution)/shard_map/ppermute | solution.py:830
  768.9 79.5 %all-to-all-start.5 = ((bf16[4,128,1024]{2,1,0:T(8,128)(2,1)}), bf16[4,128,1024]{2,1,0:T(8,128)(2,1)S(1)}, u32[]{:S(2)}, u32[]{:S(2)}) async-start(bf16[4,128,1024]{2,1,0:T(8,128)(2,1)} %bitcast.132), calls=%async_computation.7 | async-start | bytes 2097152 | tf_op jit(solution)/shard_map/all_to_all | solution.py:719
  848.4 18.8 %all-to-all-start.6 = ((bf16[4,128,1024]{2,1,0:T(8,128)(2,1)}), bf16[4,128,1024]{2,1,0:T(8,128)(2,1)}, u32[]{:S(2)}, u32[]{:S(2)}) async-start(bf16[4,128,1024]{2,1,0:T(8,128)(2,1)} %bitcast.131), calls=%async_computation.9 | async-start | bytes 2097152 | tf_op jit(solution)/shard_map/all_to_all | solution.py:719
  (14 other events, 34.2 us)
Sparse Core Ops, SparseCore 0:
  28.1 58.2 all-gather.4
  87.9 79.4 all-gather.8
  169.0 79.2 all-gather.6
  249.8 79.2 all-gather.10
  559.4 50.0 reduce-scatter.4
  611.7 76.4 reduce-scatter.10
  690.5 78.3 reduce-scatter.6
  771.2 77.1 reduce-scatter.8

commit v2 on v1

--- a/solution.py
+++ b/solution.py
@@ -389,53 +389,86 @@
     )(block)
 
 
-def scatter_kernel(
-    rows,
-    part_ref,
-    out_ref,
-    mine,
-    other,
-    to_side,
-    to_row,
-    from_side,
-    from_row,
-    on_side,
-    on_row,
-    got_side,
-    got_row,
-    send_sems,
-    recv_sems,
-    local_sems,
-):
+def swap_scratch():
+    return [pltpu.SemaphoreType.DMA((3,))] * 2 + [pltpu.SemaphoreType.DMA]
+
+
+def swap_copies(in_ref, out_ref, send_sems, recv_sems, local_sem):
+    _, row, core, *_ = place()
+    rows = out_ref.shape[1]
+    here = row * 2 + core
+
+    def block(index):
+        return in_ref.at[pl.ds(pl.multiple_of(index * rows, rows), rows)]
+
+    peers = (row * 2 + 1 - core, (1 - row) * 2 + core, (1 - row) * 2 + 1 - core)
+    away = [
+        remote(block(peer), out_ref.at[here], send_sems.at[at], recv_sems.at[at], {"ctx": peer})
+        for at, peer in enumerate(peers)
+    ]
+    return away, pltpu.make_async_copy(block(here), out_ref.at[here], local_sem)
+
+
+def scatter_steps(rows, lefts, right, out_ref, scratch, prepare=None, swap=None):
+    mine, theirs, other, to_side, to_row, from_side, from_row = scratch[:7]
+    on_side, on_row, got_side, got_row, send_sems, recv_sems = scratch[7:]
     side, row, core, near_core, near_side, near_row = place()
     half = rows // 2
     tile = 32
-
-    def spot(a, b, c):
-        return part_ref.at[pl.ds(pl.multiple_of((a * 4 + b * 2 + c) * rows, rows), rows)]
+    width = out_ref.shape[1]
+    wide = 512
 
     chips = ((side, row), (1 - side, row), (side, 1 - row), (1 - side, 1 - row))
-    locals_, pairs = {}, {}
-    for number in (3, 1, 2, 0):
-        locals_[number] = pltpu.make_async_copy(
-            spot(*chips[number], core), mine.at[number], local_sems.at[number]
-        )
-        locals_[number].start()
-    greet((near_core, near_side, near_row))
-    copies = []
-
-    def send(number, source, target, device):
-        copy = remote(source, target, send_sems.at[number], recv_sems.at[number], device)
-        copy.start()
-        copies.append(copy)
-        return copy
-
-    for number in (3, 1, 2, 0):
-        pairs[number] = send(number, spot(*chips[number], 1 - core), other.at[number], near_core)
-
-    def ready(number):
-        locals_[number].wait()
-        pairs[number].wait_recv()
+    routes = [(theirs.at[chip], other.at[chip], near_core) for chip in range(4)] + [
+        (to_side.at[0], from_side.at[0], near_side),
+        (to_row.at[0], from_row.at[0], near_row),
+        (to_side.at[1], from_side.at[1], near_side),
+        (to_row.at[1], from_row.at[1], near_row),
+        (on_row, got_row, near_row),
+        (on_side, got_side, near_side),
+    ]
+    copies = [
+        remote(source, target, send_sems.at[at], recv_sems.at[at], device)
+        for at, (source, target, device) in enumerate(routes)
+    ]
+
+    order = [(chip, owner) for chip in (3, 1, 2, 0) for owner in (1 - core, core)]
+    starts = [
+        pl.multiple_of((chips[chip][0] * 4 + chips[chip][1] * 2 + owner) * rows, rows)
+        for chip, owner in order
+    ]
+
+    swapped = None if swap is None else swap_copies(*swap)
+
+    def product(target, number, twin):
+        turn = 2 * (3, 1, 2, 0).index(number) + twin
+        start = starts[turn]
+        if prepare is not None:
+            prepare(turn, starts)
+
+        def step(index, carry):
+            at = pl.multiple_of(index * wide, wide)
+            value = None
+            for which, left in enumerate(lefts):
+                term = matmul_nt(left[pl.ds(start, rows), :], right[which, pl.ds(at, wide), :])
+                value = term if value is None else value + term
+            target[number, :, pl.ds(at, wide)] = value.astype(BF16)
+            return carry
+
+        lax.fori_loop(0, width // wide, step, 0)
+
+    def give(number):
+        product(theirs, number, 0)
+        if number == 3:
+            partners = (near_core, near_side, near_row)
+            if swap is not None:
+                partners += ({"ctx": (1 - row) * 2 + 1 - core},)
+            greet(partners)
+        copies[number].start()
+
+    def take(number):
+        product(mine, number, 1)
+        copies[number].wait_recv()
 
     def both(number, part, at):
         at = part * half + at
@@ -458,78 +491,239 @@
 
         each(body)
 
-    ready(3)
-    put(to_side.at[0], 3, 0)
-    side_0 = send(4, to_side.at[0], from_side.at[0], near_side)
-    put(to_row.at[0], 3, 1)
-    row_0 = send(5, to_row.at[0], from_row.at[0], near_row)
-    ready(1)
-    put(to_side.at[1], 1, 0)
-    side_1 = send(6, to_side.at[1], from_side.at[1], near_side)
-    ready(2)
-    put(to_row.at[1], 2, 1)
-    row_1 = send(7, to_row.at[1], from_row.at[1], near_row)
-    side_0.wait_recv()
-    put(on_row, 2, 0, from_side.at[0])
-    fin_row = send(8, on_row, got_row, near_row)
-    row_0.wait_recv()
-    put(on_side, 1, 1, from_row.at[0])
-    fin_side = send(9, on_side, got_side, near_side)
-    ready(0)
-    side_1.wait_recv()
-    row_1.wait_recv()
-
-    def first_sum(at):
-        out_ref[pl.ds(at, tile), :] = both(0, 0, at) + from_side[1, pl.ds(at, tile), :].astype(F32)
-        out_ref[pl.ds(half + at, tile), :] = both(0, 1, at) + from_row[
-            1, pl.ds(at, tile), :
-        ].astype(F32)
-
-    each(first_sum)
-    fin_row.wait_recv()
-    fin_side.wait_recv()
-
-    def last_sum(at):
-        out_ref[pl.ds(at, tile), :] += got_row[pl.ds(at, tile), :].astype(F32)
-        out_ref[pl.ds(half + at, tile), :] += got_side[pl.ds(at, tile), :].astype(F32)
-
-    each(last_sum)
-    for copy in copies:
-        copy.wait_send()
-
-
-def plane_scatter(partial):
-    total, width = partial.shape
+    def across():
+        give(3)
+        take(3)
+        put(to_side.at[0], 3, 0)
+        copies[4].start()
+        put(to_row.at[0], 3, 1)
+        copies[5].start()
+        if swap is not None:
+            for copy in swapped[0] + [swapped[1]]:
+                copy.start()
+
+    def along():
+        give(1)
+        take(1)
+        put(to_side.at[1], 1, 0)
+        copies[6].start()
+        give(2)
+        take(2)
+        put(to_row.at[1], 2, 1)
+        copies[7].start()
+
+    def forward():
+        copies[4].wait_recv()
+        put(on_row, 2, 0, from_side.at[0])
+        copies[8].start()
+        copies[5].wait_recv()
+        put(on_side, 1, 1, from_row.at[0])
+        copies[9].start()
+
+    def own():
+        give(0)
+        take(0)
+
+    def finish():
+        copies[6].wait_recv()
+        copies[7].wait_recv()
+
+        def first_sum(at):
+            out_ref[pl.ds(at, tile), :] = both(0, 0, at) + from_side[
+                1, pl.ds(at, tile), :
+            ].astype(F32)
+            out_ref[pl.ds(half + at, tile), :] = both(0, 1, at) + from_row[
+                1, pl.ds(at, tile), :
+            ].astype(F32)
+
+        each(first_sum)
+        copies[8].wait_recv()
+        copies[9].wait_recv()
+
+        def last_sum(at):
+            out_ref[pl.ds(at, tile), :] += got_row[pl.ds(at, tile), :].astype(F32)
+            out_ref[pl.ds(half + at, tile), :] += got_side[pl.ds(at, tile), :].astype(F32)
+
+        each(last_sum)
+        for copy in copies:
+            copy.wait_send()
+        if swap is not None:
+            for copy in swapped[0]:
+                copy.wait()
+            swapped[1].wait()
+
+    return across, along, forward, own, finish
+
+
+def scatter_scratch(rows, width):
+    half = rows // 2
+    return (
+        [pltpu.VMEM((4, rows, width), BF16)] * 3
+        + [pltpu.VMEM((2, half, width), BF16)] * 4
+        + [pltpu.VMEM((half, width), BF16)] * 4
+        + [pltpu.SemaphoreType.DMA((10,))] * 2
+    )
+
+
+def scatter_kernel(rows, terms, swaps, *refs):
+    lefts, right, refs = refs[:terms], refs[terms], refs[terms + 1 :]
+    swap = None
+    if swaps:
+        in_ref, out_ref, swapped_ref, *scratch = refs
+        swap = (in_ref, swapped_ref, *scratch[-3:])
+        scratch = scratch[:-3]
+    else:
+        out_ref, *scratch = refs
+    for step in scatter_steps(rows, lefts, right, out_ref, scratch, swap=swap):
+        step()
+
+
+def product_scatter(number, lefts, right, swap=None):
+    total = lefts[0].shape[0]
+    width = right.shape[1]
     rows = total // 8
-    half = rows // 2
+    vmem = pl.BlockSpec(memory_space=pltpu.VMEM)
+    shapes, ins, scratch = [jax.ShapeDtypeStruct((rows, width), F32)], [vmem] * (len(lefts) + 1), []
+    operands = [*lefts, right]
+    if swap is not None:
+        shapes.append(jax.ShapeDtypeStruct((4, swap.shape[0] // 4, swap.shape[1]), swap.dtype))
+        ins.append(pl.BlockSpec(memory_space=pl.ANY))
+        operands.append(swap)
+        scratch = swap_scratch()
     return pl.pallas_call(
-        functools.partial(scatter_kernel, rows),
-        out_shape=jax.ShapeDtypeStruct((rows, width), F32),
-        in_specs=[pl.BlockSpec(memory_space=pl.ANY)],
-        out_specs=pl.BlockSpec(memory_space=pltpu.VMEM),
+        functools.partial(scatter_kernel, rows, len(lefts), swap is not None),
+        out_shape=tuple(shapes),
+        in_specs=ins,
+        out_specs=tuple([vmem] * len(shapes)),
+        scratch_shapes=scatter_scratch(rows, width) + scratch,
+        compiler_params=pltpu.CompilerParams(
+            collective_id=number, has_side_effects=True, vmem_limit_bytes=56 * 1024 * 1024
+        ),
+        cost_estimate=pl.CostEstimate(flops=0, bytes_accessed=1024, transcendentals=0),
+        name="product_scatter",
+    )(*operands)
+
+
+def ffn_back_kernel(
+    rows,
+    cot_ref,
+    gate_slope_ref,
+    up_slope_ref,
+    down_ref,
+    right_ref,
+    out_ref,
+    gate_ref,
+    up_ref,
+    cots,
+    gate_slopes,
+    up_slopes,
+    sems,
+    *scratch,
+):
+    wide = 512
+    sources = ((cot_ref, cots), (gate_slope_ref, gate_slopes), (up_slope_ref, up_slopes))
+
+    def fetch(turn, starts):
+        return [
+            pltpu.make_async_copy(
+                source.at[pl.ds(starts[turn], rows)], target.at[turn % 2], sems.at[which, turn % 2]
+            )
+            for which, (source, target) in enumerate(sources)
+        ]
+
+    def prepare(turn, starts):
+        if turn == 0:
+            for copy in fetch(0, starts):
+                copy.start()
+        if turn < 7:
+            for copy in fetch(turn + 1, starts):
+                copy.start()
+        for copy in fetch(turn, starts):
+            copy.wait()
+        slot = turn % 2
+        here = pl.ds(starts[turn], rows)
+
+        def step(index, carry):
+            at = pl.ds(pl.multiple_of(index * wide, wide), wide)
+            grad = jnp.dot(cots[slot], down_ref[:, at], preferred_element_type=F32)
+            gate_ref[here, at] = (grad * gate_slopes[slot, :, at].astype(F32)).astype(BF16)
+            up_ref[here, at] = (grad * up_slopes[slot, :, at].astype(F32)).astype(BF16)
+            return carry
+
+        lax.fori_loop(0, down_ref.shape[1] // wide, step, 0)
+
+    for step in scatter_steps(rows, [gate_ref, up_ref], right_ref, out_ref, scratch, prepare):
+        step()
+
+
+def ffn_back(number, cot, gate_slope, up_slope, down_w, gate_up):
+    total, width = cot.shape
+    units = down_w.shape[1]
+    rows = total // 8
+    vmem = pl.BlockSpec(memory_space=pltpu.VMEM)
+    left = pl.BlockSpec(memory_space=pl.ANY)
+    return pl.pallas_call(
+        functools.partial(ffn_back_kernel, rows),
+        out_shape=(
+            jax.ShapeDtypeStruct((rows, width), F32),
+            jax.ShapeDtypeStruct((total, units), BF16),
+            jax.ShapeDtypeStruct((total, units), BF16),
+        ),
+        in_specs=[left, left, left, vmem, vmem],
+        out_specs=(vmem, vmem, vmem),
         scratch_shapes=[
-            pltpu.VMEM((4, rows, width), BF16),
-            pltpu.VMEM((4, rows, width), BF16),
-            pltpu.VMEM((2, half, width), BF16),
-            pltpu.VMEM((2, half, width), BF16),
-            pltpu.VMEM((2, half, width), BF16),
-            pltpu.VMEM((2, half, width), BF16),
-            pltpu.VMEM((half, width), BF16),
-            pltpu.VMEM((half, width), BF16),
-            pltpu.VMEM((half, width), BF16),
-            pltpu.VMEM((half, width), BF16),
-            pltpu.SemaphoreType.DMA((10,)),
-            pltpu.SemaphoreType.DMA((10,)),
-            pltpu.SemaphoreType.DMA((4,)),
+            pltpu.VMEM((2, rows, width), BF16),
+            pltpu.VMEM((2, rows, units), BF16),
+            pltpu.VMEM((2, rows, units), BF16),
+            pltpu.SemaphoreType.DMA((3, 2)),
+        ]
+        + scatter_scratch(rows, width),
+        compiler_params=pltpu.CompilerParams(
+            collective_id=number, has_side_effects=True, vmem_limit_bytes=56 * 1024 * 1024
+        ),
+        cost_estimate=pl.CostEstimate(flops=0, bytes_accessed=1024, transcendentals=0),
+        name="ffn_back",
+    )(cot, gate_slope, up_slope, down_w, gate_up)
+
+
+def ffn_kernel(in_ref, w_ref, product_ref, gate_slope_ref, up_slope_ref):
+    wide = 256
+    rows_in = in_ref[...]
+
+    def step(index, carry):
+        at = pl.ds(pl.multiple_of(index * wide, wide), wide)
+        gate = jnp.dot(rows_in, w_ref[0, :, at], preferred_element_type=F32)
+        up = jnp.dot(rows_in, w_ref[1, :, at], preferred_element_type=F32)
+        sigma = jax.nn.sigmoid(gate)
+        active = gate * sigma
+        product_ref[:, at] = (active * up).astype(BF16)
+        gate_slope_ref[:, at] = (up * sigma * (1.0 + gate * (1.0 - sigma))).astype(BF16)
+        up_slope_ref[:, at] = active.astype(BF16)
+        return carry
+
+    lax.fori_loop(0, w_ref.shape[2] // wide, step, 0)
+
+
+def ffn(rows_in, gate_up):
+    total, width = rows_in.shape
+    units = gate_up.shape[2]
+    rows = 256
+    out = pl.BlockSpec((rows, units), lambda i: (i, 0))
+    return pl.pallas_call(
+        ffn_kernel,
+        grid=(total // rows,),
+        out_shape=(jax.ShapeDtypeStruct((total, units), BF16),) * 3,
+        in_specs=[
+            pl.BlockSpec((rows, width), lambda i: (i, 0)),
+            pl.BlockSpec(
+                (2, width, units), lambda i: (0, 0, 0), pipeline_mode=pl.Buffered(1)
+            ),
         ],
-        compiler_params=pltpu.CompilerParams(
-            collective_id=1, has_side_effects=True, vmem_limit_bytes=32 * 1024 * 1024
-        ),
-        cost_estimate=pl.CostEstimate(
-            flops=0, bytes_accessed=8 * total * width * 2, transcendentals=0
-        ),
-        name="plane_scatter",
-    )(partial)
+        out_specs=(out, out, out),
+        compiler_params=pltpu.CompilerParams(vmem_limit_bytes=40 * 1024 * 1024),
+        cost_estimate=pl.CostEstimate(flops=0, bytes_accessed=1024, transcendentals=0),
+        name="ffn",
+    )(rows_in, gate_up)
 
 
 def swap_halves(values):
@@ -632,83 +826,242 @@
 
 
 def attend_back_kernel(
-    length, q_ref, kv_ref, up_ref, log_ref, cos_ref, sin_ref, dq_ref, dkv_ref, sum_ref
+    seqs,
+    rows,
+    q_ref,
+    kv_ref,
+    up_ref,
+    log_ref,
+    cos_ref,
+    sin_ref,
+    left_ref,
+    right_ref,
+    in_ref,
+    dq_ref,
+    dkv_ref,
+    out_ref,
+    swapped_ref,
+    sum_ref,
+    *scratch,
 ):
-    pair = pl.program_id(1)
+    across, along, forward, own, finish = scatter_steps(
+        rows,
+        [left_ref],
+        right_ref,
+        out_ref,
+        scratch[:-3],
+        swap=(in_ref, swapped_ref, *scratch[-3:]),
+    )
     scale = HEAD_DIM ** (-0.5)
-
-    @pl.when(pair == 0)
-    def _():
-        sum_ref[...] = jnp.zeros_like(sum_ref)
-
-    for block in range(length // QB):
-        here = pl.ds(block * QB, QB)
-        turned = []
-        for head in range(2):
-            lanes = slice(head * HEAD_DIM, (head + 1) * HEAD_DIM)
-            query = q_ref[here, lanes] * jnp.asarray(scale, BF16)
-            upstream = up_ref[here, lanes]
-            logs = log_ref[here, head * HEAD_DIM : head * HEAD_DIM + 1]
-            saved = []
-            inner = None
-            for start, size, diagonal in pieces_of(block):
-                keys = kv_ref[pl.ds(start, size), :HEAD_DIM]
-                values = kv_ref[pl.ds(start, size), HEAD_DIM:]
-                probability = jnp.exp(masked_scores(query, keys, diagonal) - logs)
-                prob_grad = matmul_nt(upstream, values)
-                term = jnp.sum(probability * prob_grad, axis=1, keepdims=True)
-                inner = term if inner is None else inner + term
-                saved.append((start, size, probability, prob_grad))
-            out = None
-            for start, size, probability, prob_grad in saved:
-                keys = kv_ref[pl.ds(start, size), :HEAD_DIM]
-                score_grad = (probability * (prob_grad - inner)).astype(BF16)
-                rounded = probability.astype(BF16)
-                term = jnp.dot(score_grad, keys, preferred_element_type=F32)
-                out = term if out is None else out + term
-                sum_ref[pl.ds(start, size), :] += jnp.concatenate(
-                    [matmul_t(score_grad, query), matmul_t(rounded, upstream)], axis=1
-                )
-            turned.append(out * scale)
-        grad = jnp.concatenate(turned, axis=1)
-        dq_ref[here, :] = (grad * cos_ref[here, :] - swap_halves(grad) * sin_ref[here, :]).astype(
-            BF16
+    length = q_ref.shape[0] // seqs
+    pairs = q_ref.shape[1] // 128
+    across()
+    along()
+
+    def one_pair(index, carry):
+        seq = index // pairs
+        pair = index % pairs
+        lanes_at = pl.ds(pl.multiple_of(pair * 128, 128), 128)
+        base = pl.multiple_of(seq * length, length)
+
+        @pl.when(index == 1)
+        def _():
+            forward()
+
+        @pl.when(index == 2)
+        def _():
+            own()
+
+        @pl.when(pair == 0)
+        def _():
+            sum_ref[...] = jnp.zeros_like(sum_ref)
+
+        for block in range(length // QB):
+            here = pl.ds(base + block * QB, QB)
+            turned = []
+            q_pair = q_ref[here, lanes_at]
+            up_pair = up_ref[here, lanes_at]
+            log_pair = log_ref[here, lanes_at]
+            for head in range(2):
+                lanes = slice(head * HEAD_DIM, (head + 1) * HEAD_DIM)
+                query = q_pair[:, lanes] * jnp.asarray(scale, BF16)
+                upstream = up_pair[:, lanes]
+                logs = log_pair[:, head * HEAD_DIM : head * HEAD_DIM + 1]
+                saved = []
+                inner = None
+                for start, size, diagonal in pieces_of(block):
+                    keys = kv_ref[pl.ds(base + start, size), :HEAD_DIM]
+                    values = kv_ref[pl.ds(base + start, size), HEAD_DIM:]
+                    probability = jnp.exp(masked_scores(query, keys, diagonal) - logs)
+                    prob_grad = matmul_nt(upstream, values)
+                    term = jnp.sum(probability * prob_grad, axis=1, keepdims=True)
+                    inner = term if inner is None else inner + term
+                    saved.append((start, size, probability, prob_grad))
+                out = None
+                for start, size, probability, prob_grad in saved:
+                    keys = kv_ref[pl.ds(base + start, size), :HEAD_DIM]
+                    score_grad = (probability * (prob_grad - inner)).astype(BF16)
+                    rounded = probability.astype(BF16)
+                    term = jnp.dot(score_grad, keys, preferred_element_type=F32)
+                    out = term if out is None else out + term
+                    sum_ref[pl.ds(start, size), :] += jnp.concatenate(
+                        [matmul_t(score_grad, query), matmul_t(rounded, upstream)], axis=1
+                    )
+                turned.append(out * scale)
+            grad = jnp.concatenate(turned, axis=1)
+            angle = pl.ds(block * QB, QB)
+            dq_ref[here, lanes_at] = (
+                grad * cos_ref[angle, :] - swap_halves(grad) * sin_ref[angle, :]
+            ).astype(BF16)
+
+        @pl.when(pair == pairs - 1)
+        def _():
+            grad = sum_ref[...]
+            lane = lax.broadcasted_iota(jnp.int32, grad.shape, 1)
+            back = grad * cos_ref[...] - swap_halves(grad) * sin_ref[...]
+            dkv_ref[pl.ds(base, length), :] = jnp.where(lane < HEAD_DIM, back, grad).astype(BF16)
+
+        return carry
+
+    lax.fori_loop(0, seqs * pairs, one_pair, 0)
+    finish()
+
+
+def attend_back(number, queries, keyvals, upstream, logs, cosine, signed, seqs, left, right, swap):
+    total, width = queries.shape
+    length = total // seqs
+    rows = total // 8
+    vmem = pl.BlockSpec(memory_space=pltpu.VMEM)
+    return pl.pallas_call(
+        functools.partial(attend_back_kernel, seqs, rows),
+        out_shape=(
+            jax.ShapeDtypeStruct((total, width), BF16),
+            jax.ShapeDtypeStruct((total, 128), BF16),
+            jax.ShapeDtypeStruct((rows, right.shape[1]), F32),
+            jax.ShapeDtypeStruct((4, swap.shape[0] // 4, swap.shape[1]), swap.dtype),
+        ),
+        in_specs=[vmem] * 8 + [pl.BlockSpec(memory_space=pl.ANY)],
+        out_specs=(vmem, vmem, vmem, vmem),
+        scratch_shapes=[pltpu.VMEM((length, 128), F32)]
+        + scatter_scratch(rows, right.shape[1])
+        + swap_scratch(),
+        compiler_params=pltpu.CompilerParams(
+            collective_id=number, has_side_effects=True, vmem_limit_bytes=56 * 1024 * 1024
+        ),
+        cost_estimate=pl.CostEstimate(flops=0, bytes_accessed=1024, transcendentals=0),
+        name="attend_back",
+    )(queries, keyvals, upstream, logs, cosine, signed, left, right, swap)
+
+
+def gain_kernel(
+    planes, parts, cols, terms_ref, out_ref, total, seen, far, mine, across, send_sems, recv_sems
+):
+    side, row, core, near_core, near_side, near_row = place()
+    plane = lax.axis_index("dp")
+    ctx = row * 2 + core
+    others = [{"dp": (plane + step) % planes} for step in range(1, planes)]
+    greet((near_core, near_side, near_row) + tuple(others))
+    total[...] = terms_ref[...]
+    copies = []
+    for number, target in enumerate((near_core, near_row)):
+        copy = remote(
+            total, seen.at[number], send_sems.at[number], recv_sems.at[number], target
         )
-
-    @pl.when(pair == pl.num_programs(1) - 1)
-    def _():
-        grad = sum_ref[...]
-        lane = lax.broadcasted_iota(jnp.int32, grad.shape, 1)
-        back = grad * cos_ref[...] - swap_halves(grad) * sin_ref[...]
-        dkv_ref[...] = jnp.where(lane < HEAD_DIM, back, grad).astype(BF16)
-
-
-def attend_back(queries, keyvals, upstream, logs, cosine, signed, seqs):
-    rows, width = queries.shape
-    length = rows // seqs
-    pairs = width // 128
-    block = (length, 128)
-    by_pair = pl.BlockSpec(block, lambda s, h: (s, h))
-    by_seq = pl.BlockSpec(block, lambda s, h: (s, 0))
-    same = pl.BlockSpec(block, lambda s, h: (0, 0))
+        copy.start()
+        copy.wait()
+        total[...] += seen[number]
+    for step, target in enumerate(others, 1):
+        start = (((plane + step) % planes) * parts + ctx) * cols
+        copy = remote(
+            total.at[:, pl.ds(pl.multiple_of(start, cols), cols)],
+            far.at[step - 1],
+            send_sems.at[2 + step],
+            recv_sems.at[2 + step],
+            target,
+        )
+        copy.start()
+        copies.append(copy)
+    start = (plane * parts + ctx) * cols
+    value = total[:, pl.ds(pl.multiple_of(start, cols), cols)]
+    for number, copy in enumerate(copies):
+        copy.wait_recv()
+        value += far[number]
+    mine[...] = value
+    last = remote(mine, across, send_sems.at[2], recv_sems.at[2], near_side)
+    last.start()
+    copies.append(last)
+    last.wait_recv()
+    out_ref[...] = value + across[...]
+    for copy in copies:
+        copy.wait_send()
+
+
+def gain_sum(terms):
+    planes = lax.axis_size("dp")
+    parts = lax.axis_size("ctx")
+    rows, width = terms.shape
+    cols = width // (planes * parts)
     return pl.pallas_call(
-        functools.partial(attend_back_kernel, length),
-        grid=(seqs, pairs),
-        out_shape=(
-            jax.ShapeDtypeStruct((rows, width), BF16),
-            jax.ShapeDtypeStruct((rows, 128), BF16),
-        ),
-        in_specs=[by_pair, by_seq, by_pair, by_pair, same, same],
-        out_specs=(by_pair, by_seq),
-        scratch_shapes=[pltpu.VMEM(block, F32)],
-        compiler_params=pltpu.CompilerParams(vmem_limit_bytes=48 * 1024 * 1024),
-        cost_estimate=pl.CostEstimate(
-            flops=20 * rows * length * 128 * pairs,
-            bytes_accessed=rows * pairs * 128 * 12,
-            transcendentals=rows * length * 2 * pairs,
-        ),
-        name="attend_back",
-    )(queries, keyvals, upstream, logs, cosine, signed)
+        functools.partial(gain_kernel, planes, parts, cols),
+        out_shape=jax.ShapeDtypeStruct((rows, cols), F32),
+        in_specs=[pl.BlockSpec(memory_space=pltpu.VMEM)],
+        out_specs=pl.BlockSpec(memory_space=pltpu.VMEM),
+        scratch_shapes=[
+            pltpu.VMEM((rows, width), F32),
+            pltpu.VMEM((2, rows, width), F32),
+            pltpu.VMEM((planes - 1, rows, cols), F32),
+            pltpu.VMEM((rows, cols), F32),
+            pltpu.VMEM((rows, cols), F32),
+            pltpu.SemaphoreType.DMA((planes + 2,)),
+            pltpu.SemaphoreType.DMA((planes + 2,)),
+        ],
+        compiler_params=pltpu.CompilerParams(collective_id=2, has_side_effects=True),
+        name="gain_sum",
+    )(terms)
+
+
+def lay_kernel(own_ref, far_ref, twin_ref, twin_far_ref, all_ref, sems):
+    ctx = lax.axis_index("ctx")
+    row, core = ctx // 2, ctx % 2
+    span = own_ref.shape[1]
+    copies = []
+    for number, (part, a, b) in enumerate(
+        (
+            (own_ref, row, core),
+            (twin_ref, row, 1 - core),
+            (far_ref, 1 - row, core),
+            (twin_far_ref, 1 - row, 1 - core),
+        )
+    ):
+        start = pl.multiple_of((a * 2 + b) * span, span)
+        copies.append(
+            pltpu.make_async_copy(part, all_ref.at[:, pl.ds(start, span)], sems.at[number])
+        )
+        copies[-1].start()
+    for copy in copies:
+        copy.wait()
+
+
+def along_ctx(block, earlier, later):
+    seqs, span, width = block.shape
+    cores = [(0, 1), (1, 0), (2, 3), (3, 2)]
+    far = lax.ppermute(after(block, earlier), "ctx", [(0, 2), (1, 3), (2, 0), (3, 1)])
+    far = after(far, later)
+    twin, twin_far = lax.ppermute(block, "ctx", cores), lax.ppermute(far, "ctx", cores)
+    whole = pl.pallas_call(
+        lay_kernel,
+        out_shape=jax.ShapeDtypeStruct((seqs, 4 * span, width), block.dtype),
+        in_specs=[pl.BlockSpec(memory_space=pl.ANY)] * 4,
+        out_specs=pl.BlockSpec(memory_space=pltpu.VMEM),
+        scratch_shapes=[pltpu.SemaphoreType.DMA((4,))],
+        compiler_params=pltpu.CompilerParams(vmem_limit_bytes=24 * 1024 * 1024),
+        name="lay",
+    )(block, far, twin, twin_far)
+    return whole.reshape(seqs * 4 * span, width)
+
+
+def after(value, *earlier):
+    return lax.optimization_barrier((value,) + earlier)[0]
 
 
 def to_units(weight):
@@ -761,6 +1114,7 @@
     ).transpose(1, 0, 2)
     mixed = jnp.concatenate([mixed, gain_rows], axis=1)
     mixed = lax.all_to_all(mixed, "ctx", split_axis=0, concat_axis=0, tiled=True)
+    ready_w = mixed
     mixed = lax.all_gather(mixed, "dp", axis=0, tiled=True)
     attn_w = mixed[:, :rows_w].reshape(width, -1)
     gain_one = mixed[:, rows_w, :rows_w].reshape(width).astype(F32)
@@ -769,76 +1123,84 @@
     w_qkv = attn_w[:, :qkv_cols]
     w_out_t = attn_w[:, qkv_cols:]
 
-    gate_w, up_w, down_w = (
-        lax.all_gather(to_units(w), "dp", axis=0, tiled=True) for w in (w_gate, w_up, w_down.T)
-    )
-
+    half_units = w_gate.shape[1] // parts
+    gate_up = jnp.stack(
+        [w_gate.reshape(rows_w, parts, half_units), w_up.reshape(rows_w, parts, half_units)]
+    )
+    gate_up = after(gate_up, ready_w).transpose(2, 0, 1, 3)
+    gate_up = lax.all_to_all(gate_up, "ctx", split_axis=0, concat_axis=0, tiled=True)
     own_in = lax.dynamic_index_in_dim(layer_input, side, 0, keepdims=False)
     own_cot = lax.dynamic_index_in_dim(cotangent, side, 0, keepdims=False)
-    all_in = plane_gather(own_in)
-    all_cot = plane_gather(own_cot)
+    all_in = plane_gather(after(own_in, ready_w))
+    gate_up = gate_up.transpose(1, 0, 2, 3).reshape(2, parts * rows_w, half_units)
+    gate_up = lax.all_gather(gate_up, "dp", axis=1, tiled=True)
+    down_own = to_units(after(w_down, all_in).T)
+    down_w = lax.all_gather(down_own, "dp", axis=0, tiled=True)
 
     all_f = all_in.astype(F32)
     normed_one = (all_f * rms_factor(all_f) * gain_one).astype(BF16)
-    pre = jnp.dot(normed_one, w_qkv, preferred_element_type=F32)
+    pre = after(jnp.dot(normed_one, w_qkv, preferred_element_type=F32), down_own)
     attended, queries, keyvals, logs = attend(pre, cosine, signed, seqs)
-    attn_part = matmul_nt(attended, w_out_t).astype(BF16)
     inputs_f = own_in.astype(F32)
     factor_one = rms_factor(inputs_f)
-    hidden = inputs_f + plane_scatter(attn_part)
+    hidden = inputs_f + product_scatter(1, [attended], w_out_t[None])[0]
     factor_two = rms_factor(hidden)
     normed_own = (hidden * factor_two * gain_two).astype(BF16)
     normed_two = plane_gather(normed_own)
-
-    gate_pre = jnp.dot(normed_two, gate_w, preferred_element_type=F32)
-    up_pre = jnp.dot(normed_two, up_w, preferred_element_type=F32)
-    sigma = jax.nn.sigmoid(gate_pre)
-    product = (gate_pre * sigma * up_pre).astype(BF16)
+    all_cot = along_ctx(cotangent, down_own, attended)
+
+    product, gate_slope, up_slope = ffn(normed_two, gate_up)
     down_grad = matmul_t(all_cot, product).astype(BF16)
-    prod_grad = jnp.dot(all_cot, down_w, preferred_element_type=F32)
-    gate_grad = (prod_grad * up_pre * sigma * (1.0 + gate_pre * (1.0 - sigma))).astype(BF16)
-    up_grad = (prod_grad * gate_pre * sigma).astype(BF16)
+    down_sum = lax.psum_scatter(down_grad, "dp", scatter_dimension=0, tiled=True)
+    normed_two_grad, gate_grad, up_grad = ffn_back(
+        3, after(all_cot, down_grad), gate_slope, up_slope, down_w, gate_up
+    )
     gate_w_grad = matmul_t(normed_two, gate_grad).astype(BF16)
-    up_w_grad = matmul_t(normed_two, up_grad).astype(BF16)
-    back_part = (matmul_nt(gate_grad, gate_w) + matmul_nt(up_grad, up_w)).astype(BF16)
-    ffn_part = matmul_nt(product, down_w).astype(BF16)
-    down_sum, gate_sum, up_sum = (
-        lax.psum_scatter(g, "dp", scatter_dimension=0, tiled=True)
-        for g in (down_grad, gate_w_grad, up_w_grad)
-    )
-
-    normed_two_grad = plane_scatter(back_part)
+    gate_sum = lax.psum_scatter(gate_w_grad, "dp", scatter_dimension=0, tiled=True)
     hidden_back, ffn_gain_term = rms_back(normed_two_grad, hidden, factor_two, gain_two)
     hidden_grad = own_cot.astype(F32) + hidden_back
-    hidden_low = plane_gather(hidden_grad.astype(BF16))
-    attended_grad = jnp.dot(hidden_low, w_out_t, preferred_element_type=F32).astype(BF16)
+    hidden_low = plane_gather(after(hidden_grad.astype(BF16), gate_w_grad))
+    up_w_grad = matmul_t(normed_two, after(up_grad, hidden_low)).astype(BF16)
+    up_sum = lax.psum_scatter(up_w_grad, "dp", scatter_dimension=0, tiled=True)
+    attended_grad = jnp.dot(after(hidden_low, up_w_grad), w_out_t, preferred_element_type=F32).astype(BF16)
     out_w_grad = matmul_t(hidden_low, attended).astype(BF16)
-    query_low, keyval_low = attend_back(
-        queries, keyvals, attended_grad, logs, cosine, signed, seqs
+    query_low, keyval_low, ffn_own, down_out = attend_back(
+        5,
+        queries,
+        keyvals,
+        attended_grad,
+        logs,
+        cosine,
+        signed,
+        seqs,
+        product,
+        down_w[None],
+        down_sum,
     )
     back = jnp.concatenate([query_low, keyval_low], axis=1)
     qkv_grad = matmul_t(normed_one, back).astype(BF16)
     attn_grad = jnp.concatenate([qkv_grad, out_w_grad], axis=1)
     attn_sum = lax.psum_scatter(attn_grad, "dp", scatter_dimension=0, tiled=True)
-    one_part = matmul_nt(back, w_qkv).astype(BF16)
-    normed_one_grad = plane_scatter(one_part)
+    normed_one_grad, gate_out = product_scatter(
+        4, [after(back, attn_grad)], w_qkv[None], gate_sum
+    )
     input_back, attn_gain_term = rms_back(normed_one_grad, inputs_f, factor_one, gain_one)
-    input_own = hidden_grad + input_back
-    out_own = (hidden + plane_scatter(ffn_part)).astype(BF16)
+    input_own = (hidden_grad + input_back).astype(BF16)
+    gain_own = gain_sum(after(jnp.stack([attn_gain_term, ffn_gain_term]), input_own))
+    out_own = (hidden + ffn_own).astype(BF16)
 
     def both_sides(own):
         other = lax.ppermute(own, "tensor", [(0, 1), (1, 0)])
         return jnp.where(side == 0, jnp.stack([own, other]), jnp.stack([other, own]))
 
     layer_output = both_sides(out_own)
-    input_grad = both_sides(input_own.astype(BF16)).astype(F32)
-    gain_terms = lax.psum(jnp.stack([attn_gain_term, ffn_gain_term]), ("dp", "ctx", "tensor"))
-    own_start = (lax.axis_index("dp") * parts + lax.axis_index("ctx")) * rows_w
-    gain_own = lax.dynamic_slice_in_dim(gain_terms, own_start, rows_w, axis=1)
-
-    down_out, gate_out, up_out = (from_units(g) for g in (down_sum, gate_sum, up_sum))
+    input_grad = both_sides(input_own).astype(F32)
+    down_out, gate_out = (
+        swapped.transpose(1, 0, 2).reshape(rows_w, -1) for swapped in (down_out, gate_out)
+    )
+    up_out = from_units(after(up_sum, gain_own))
     attn_out = lax.all_to_all(
-        attn_sum.reshape(parts, rows_w, -1), "ctx", split_axis=0, concat_axis=0, tiled=True
+        after(attn_sum, up_out).reshape(parts, rows_w, -1), "ctx", split_axis=0, concat_axis=0, tiled=True
     )
 
     def columns(start, size):

time: 886 us -> 691 us (0.78)
  matrix products: 164 us -> 70.5 us
  waiting for transfers between devices: 107 us -> 23.1 us
  blocking collectives: 111 us -> 44.3 us
  Pallas kernels: 389 us -> 421 us
  local copies, waits for them, and re-layouts: 32.2 us -> 52 us
    dot_general x10 -> x2, matrix products: 112 us -> 16.8 us  [the longest x1 9.75 us: on_plane(): jnp.dot(normed_one, w_qkv, preferred_element_type=F32)]
    reduce_scatter x3, waiting for transfers between devices: 82.8 us -> 0.02 us  [the longest x1 0.02 us: on_plane(): up_sum = lax.psum_scatter(up_w_grad, 'dp', scatter_dimension=0, tiled=True)]
    pallas_call x5 -> x7, Pallas kernels: 202 us -> 282 us  [the longest x2 100 us: product_scatter(): pl.pallas_call(functools.partial(scatter_kernel, rows, len(lefts), swap i...]
    psum x1 -> x0, blocking collectives: 62.4 us -> none  [on_plane(): lax.psum(jnp.stack([attn_gain_term, ffn_gain_term]), ('dp', 'ctx', 'tenso...]
    pallas_call x4 -> x3, Pallas kernels: 166 us -> 119 us  [plane_gather(): pl.pallas_call(functools.partial(gather_kernel, rows), out_shape=jax.Shap...]
    unnamed x71 -> x70, local copies, waits for them, and re-layouts: 14.2 us -> 30 us
    all_to_all x1, waiting for transfers between devices: 0.01 us -> 11 us  [to_units(): lax.all_to_all(weight, 'ctx', split_axis=1, concat_axis=0, tiled=True)]
    all_to_all x1, waiting for transfers between devices: 9.69 us -> 0.01 us  [on_plane(): lax.all_to_all(after(attn_sum, up_out).reshape(parts, rows_w, -1), 'ctx',...]
  transfers between devices with their start and end apart: 15 -> 15, of which waited for: 6 -> 5; matrix products, arithmetic and copies ran while one was open for 16% -> 20% of each run, Pallas kernels for 27% -> 62%
where the time goes in v2:
time: 691 us; the launch traced here: 681 us
  Pallas kernels  421 us (61%)
  matrix products  70.5 us (10%)
  local copies, waits for them, and re-layouts  52 us (8%)
  blocking collectives  44.3 us (6%)
  other arithmetic  39.6 us (6%)
  waiting for transfers between devices  23.1 us (3%)
  starting transfers between devices  15.4 us (2%)
  between operations  15.2 us (2%)
    pallas_call x3, Pallas kernels, plane_gather(): pl.pallas_call(functools.partial(gather_kernel, rows), out_shape=jax.Shap...  119 us
    pallas_call x2, Pallas kernels, product_scatter(): pl.pallas_call(functools.partial(scatter_kernel, rows, len(lefts), swap i...  100 us
    pallas_call x1, Pallas kernels, ffn_back(): pl.pallas_call(functools.partial(ffn_back_kernel, rows), out_shape=(jax.S...  64 us
    pallas_call x1, Pallas kernels, attend_back(): pl.pallas_call(functools.partial(attend_back_kernel, seqs, rows), out_sha...  60.8 us
    dot_general x5, matrix products, matmul_t(): lax.dot_general(left_op, right_op, (((0,), (0,)), ((), ())), preferred_el...  53.7 us
    unnamed x70, local copies, waits for them, and re-layouts  30 us
    pallas_call x1, Pallas kernels, ffn(): pl.pallas_call(ffn_kernel, grid=(total // rows,), out_shape=(jax.ShapeDty...  29.8 us
    all_to_all x1, blocking collectives, on_plane(): lax.all_to_all(gate_up, 'ctx', split_axis=0, concat_axis=0, tiled=True)  29.3 us
  transfers between devices with their start and end apart: 15, of which 5 were waited for; matrix products, arithmetic and copies ran while one was open for 20% of the time, Pallas kernels for 62%

profile of v2, /device:TPU:0, one launch (start us, length us, event | category | flops | bytes accessed | tf_op | source)
XLA Modules:
  0.0 681.4 jit_solution(11510644705512385918)
XLA Ops:
  13.0 15.0 %all_to_all.53 = bf16[4,136,640]{2,1,0:T(8,128)(2,1)} all-to-all(bf16[4,136,640]{2,1,0:T(8,128)(2,1)S(1)} %copy.97), channel_id=1, replica_groups=mesh['dp'=4,'ctx'=4,'tensor'=2] {'ctx'}, dimensions={0} | all-to-all | bytes 1392640 | tf_op jit(solution)/shard_map/all_to_all | solution.py:1116
  34.5 29.3 %all_to_all.54 = bf16[4,2,128,1024]{3,2,1,0:T(8,128)(2,1)S(1)} all-to-all(bf16[4,2,128,1024]{3,2,1,0:T(8,128)(2,1)} %copy.103), channel_id=1, replica_groups=mesh['dp'=4,'ctx'=4,'tensor'=2] {'ctx'}, dimensions={0} | all-to-all | bytes 4194304 | tf_op jit(solution)/shard_map/all_to_all | solution.py:1131
  68.1 40.1 %plane_gather.3 = bf16[2048,2048]{1,0:T(8,128)(2,1)} custom-call(bf16[256,2048]{1,0:T(8,128)(2,1)} %get-tuple-element.41.block_ref), custom_call_target="tpu_custom_call" | custom-call | bytes 67108864 | tf_op jit(solution)/shard_map/plane_gather/pallas_call | solution.py:374
  109.6 4.3 all-to-all-start.1
  117.3 11.0 %all-to-all-done.1 = bf16[128,4,1024]{2,0,1:T(8,128)(2,1)} async-done(((bf16[128,4,1024]{2,0,1:T(8,128)(2,1)}), bf16[128,4,1024]{2,0,1:T(8,128)(2,1)}, u32[]{:S(2)}, u32[]{:S(2)}) %all-to-all-start.1) | async-done | bytes 1048608 | tf_op jit(solution)/shard_map/all_to_all | solution.py:1068
  128.8 5.2 fusion
  136.9 9.8 %fusion.4.q_ref.kv_ref = f32[2048,384]{1,0:T(8,128)} fusion(bf16[2048,2048]{1,0:T(8,128)(2,1)} %plane_gather.3, f32[2048]{0:T(1024)S(1)} %bitcast.119, f32[2048]{0:T(1024)S(1)} %add_rsqrt_fusion, bf16[2048,640]{1,0:T(8,128)(2,1)S(1)} %bitcast.91), kind=kOutput, calls=%fused_computation.17 | convolution fusion | flops 3238002688 | bytes 13123584 | tf_op jit(solution)/shard_map/dot_general | solution.py:1142
  146.7 20.7 %attend.1 = (bf16[2048,256]{1,0:T(8,128)(2,1)S(1)}, bf16[2048,256]{1,0:T(8,128)(2,1)S(1)}, bf16[2048,128]{1,0:T(8,128)(2,1)S(1)}, f32[2048,256]{1,0:T(8,128)S(1)}) custom-call(f32[2048,384]{1,0:T(8,128)} %fusion.4.q_ref.kv_ref, f32[2048,384]{1,0:T(8,128)} %fusion.4.q_ref.kv_ref, f32[1024,128]{1,0:T(8,128)S(1)} %copy.99.cos_ref, f32[1024,128]{1,0:T(8,128)S(1)} %copy.100.sin_ref), custom_call_target="tpu_custom_call" | custom-call | flops 4294967296 | bytes 6291456 | tf_op jit(solution)/shard_map/attend/pallas_call | solution.py:797
  171.5 4.1 collective-permute-done.far_ref
  176.7 44.0 %product_scatter.2 = f32[256,2048]{1,0:T(8,128)} custom-call(bf16[2048,256]{1,0:T(8,128)(2,1)} %copy-done.9, bf16[1,2048,256]{2,1,0:T(8,128)(2,1)} %slice_bitcast_fusion.1.refs_1_), custom_call_target="tpu_custom_call" | custom-call | bytes 1024 | tf_op jit(solution)/shard_map/product_scatter/pallas_call | solution.py:593
  225.2 39.4 %plane_gather.4.in_ref = bf16[2048,2048]{1,0:T(8,128)(2,1)} custom-call(bf16[256,2048]{1,0:T(8,128)(2,1)} %multiply_convert_fusion.block_ref), custom_call_target="tpu_custom_call" | custom-call | bytes 67108864 | tf_op jit(solution)/shard_map/plane_gather/pallas_call | solution.py:374
  264.6 3.1 lay.1
  267.6 3.2 copy-done
  270.9 29.8 %ffn.1 = (bf16[2048,1024]{1,0:T(8,128)(2,1)S(1)}, bf16[2048,1024]{1,0:T(8,128)(2,1)S(1)}, bf16[2048,1024]{1,0:T(8,128)(2,1)S(1)}) custom-call(bf16[2048,2048]{1,0:T(8,128)(2,1)} %plane_gather.4.in_ref, bf16[2,2048,1024]{2,1,0:T(8,128)(2,1)} %all-gather.6.cloned.1.call-done.w_ref.right_ref), custom_call_target="tpu_custom_call" | custom-call | bytes 1024 | tf_op jit(solution)/shard_map/ffn/pallas_call | solution.py:712
  306.8 10.6 %convolution_convert_fusion.2 = bf16[2048,1024]{1,0:T(8,128)(2,1)} fusion(bf16[2048,2048]{1,0:T(8,128)(2,1)S(1)} %bitcast.89, bf16[2048,1024]{1,0:T(8,128)(2,1)S(1)} %get-tuple-element.50.left_ref), kind=kOutput, calls=%fused_computation.12 | convolution fusion | flops 8592031744 | bytes 16777216 | tf_op jit(solution)/shard_map/dot_general | solution.py:55
  317.5 64.0 %ffn_back.1 = (f32[256,2048]{1,0:T(8,128)}, bf16[2048,1024]{1,0:T(8,128)(2,1)}, bf16[2048,1024]{1,0:T(8,128)(2,1)}) custom-call(bf16[2048,2048]{1,0:T(8,128)(2,1)} %bitcast.88, bf16[2048,1024]{1,0:T(8,128)(2,1)} %copy-done.3, bf16[2048,1024]{1,0:T(8,128)(2,1)} %copy-done.4, bf16[2048,1024]{1,0:T(8,128)(2,1)} %all-gather.8.cloned.1.call-done.down_ref, ...), custom_call_target="tpu_custom_call" | custom-call | bytes 1024 | tf_op jit(solution)/shard_map/ffn_back/pallas_call | solution.py:665
  381.5 14.2 %convolution_convert_fusion.1 = bf16[2048,1024]{1,0:T(8,128)(2,1)} fusion(bf16[2048,2048]{1,0:T(8,128)(2,1)} %plane_gather.4.in_ref, bf16[2048,1024]{1,0:T(8,128)(2,1)} %get-tuple-element.55), kind=kOutput, calls=%fused_computation.11 | convolution fusion | flops 8592031744 | bytes 16777216 | tf_op jit(solution)/shard_map/dot_general | solution.py:55
  395.8 2.9 multiply_reduce_fusion
  401.6 39.2 %plane_gather.5 = bf16[2048,2048]{1,0:T(8,128)(2,1)} custom-call(bf16[256,2048]{1,0:T(8,128)(2,1)} %get-tuple-element.56.block_ref), custom_call_target="tpu_custom_call" | custom-call | bytes 67108864 | tf_op jit(solution)/shard_map/plane_gather/pallas_call | solution.py:374
  440.8 14.1 %convolution_convert_fusion = bf16[2048,1024]{1,0:T(8,128)(2,1)} fusion(bf16[2048,2048]{1,0:T(8,128)(2,1)} %plane_gather.4.in_ref, bf16[2048,1024]{1,0:T(8,128)(2,1)} %get-tuple-element.58), kind=kOutput, calls=%fused_computation.10 | convolution fusion | flops 8592031744 | bytes 16777216 | tf_op jit(solution)/shard_map/dot_general | solution.py:55
  456.1 6.8 %convolution_convert_fusion.4 = bf16[2048,256]{0,1:T(8,128)(2,1)} fusion(bf16[2048,2048]{1,0:T(8,128)(2,1)} %plane_gather.5, bf16[2048,256]{1,0:T(8,128)(2,1)S(1)} %copy-done.10), kind=kOutput, calls=%fused_computation.15 | convolution fusion | flops 2148007936 | bytes 10485760 | tf_op jit(solution)/shard_map/dot_general | solution.py:55
  462.9 7.0 %convolution_convert_fusion.5.up_ref = bf16[2048,256]{1,0:T(8,128)(2,1)} fusion(bf16[2048,2048]{1,0:T(8,128)(2,1)} %plane_gather.5, bf16[2048,640]{1,0:T(8,128)(2,1)} %bitcast.93), kind=kOutput, calls=%fused_computation.16 | convolution fusion | flops 2148007936 | bytes 10485760 | tf_op jit(solution)/shard_map/dot_general | solution.py:1165
  470.0 60.8 %attend_back.1 = (bf16[2048,256]{1,0:T(8,128)(2,1)}, bf16[2048,128]{1,0:T(8,128)(2,1)}, f32[256,2048]{1,0:T(8,128)}, bf16[4,128,1024]{2,1,0:T(8,128)(2,1)}) custom-call(bf16[2048,256]{1,0:T(8,128)(2,1)} %copy-done.11, bf16[2048,128]{1,0:T(8,128)(2,1)} %copy-done.12, bf16[2048,256]{1,0:T(8,128)(2,1)} %convolution_convert_fusion.5.up_ref, ...), custom_call_target="tpu_custom_call" | custom-call | bytes 1024 | tf_op jit(solution)/shard_map/attend_back/pallas_call | solution.py:935
  532.3 8.0 %convolution_convert_fusion.3 = bf16[2048,384]{0,1:T(8,128)(2,1)S(1)} fusion(bf16[2048,384]{1,0:T(8,128)(2,1)S(1)} %constant_dynamic-update-slice_fusion.refs_0_, bf16[2048,2048]{1,0:T(8,128)(2,1)} %plane_gather.3, f32[2048]{0:T(1024)S(1)} %bitcast.120, f32[2048]{0:T(1024)S(1)} %add_rsqrt_fusion), kind=kOutput, calls=%fused_computation.13 | convolution fusion | flops 3238789120 | bytes 11550720 | tf_op jit(solution)/shard_map/dot_general | solution.py:55
  544.7 56.3 %product_scatter.3 = (f32[256,2048]{1,0:T(8,128)}, bf16[4,128,1024]{2,1,0:T(8,128)(2,1)}) custom-call(bf16[2048,384]{1,0:T(8,128)(2,1)} %copy-done.21, bf16[1,2048,384]{2,1,0:T(8,128)(2,1)} %slice_bitcast_fusion.refs_1_, bf16[512,1024]{1,0:T(8,128)(2,1)} %reduce-scatter.7.cloned.1.call-done.refs_2_), custom_call_target="tpu_custom_call" | custom-call | bytes 1024 | tf_op jit(solution)/shard_map/product_scatter/pallas_call | solution.py:593
  605.8 24.1 %gain_sum.1 = f32[2,128]{1,0:T(2,128)} custom-call(f32[2,2048]{1,0:T(2,128)} %pad_maximum_fusion.4.terms_ref), custom_call_target="tpu_custom_call" | custom-call | tf_op jit(solution)/shard_map/gain_sum/pallas_call | solution.py:1004
  629.9 4.3 all-to-all-start.3
  634.2 2.9 add_convert_fusion
  653.6 3.5 all-to-all-start.4
  657.1 5.8 collective-permute-done.3
  662.9 3.9 maximum_select_fusion
  666.8 3.9 fusion.14
  (146 shorter events, 75.1 us)
Async XLA Ops:
  7.2 126.8 %all-gather.4.cloned.1.call-start = ((), (), s32[]{:S(2)}) async-start(), calls=%async_computation.9 | async-start | bytes 3481600 | tf_op jit(solution)/shard_map/all_gather | solution.py:1118
  13.0 15.1 %copy-start.24 = (bf16[128,4096]{1,0:T(8,128)(2,1)S(1)}, bf16[128,4096]{1,0:T(8,128)(2,1)}, u32[]{:S(2)}) copy-start(bf16[128,4096]{1,0:T(8,128)(2,1)} %param.18) | copy-start | bytes 3145732
  28.0 242.9 %all-gather.6.cloned.1.call-start = ((), (), s32[]{:S(2)}) async-start(), calls=%async_computation.10 | async-start | bytes 10485760 | tf_op jit(solution)/shard_map/all_gather | solution.py:1136
  68.1 40.1 %copy-start.26 = (bf16[4096,128]{1,0:T(8,128)(2,1)S(1)}, bf16[4096,128]{1,0:T(8,128)(2,1)}, u32[]{:S(2)}) copy-start(bf16[4096,128]{1,0:T(8,128)(2,1)} %param.20) | copy-start | bytes 3145732
  108.2 5.6 copy-start.2
  109.6 18.8 %all-to-all-start.1 = ((bf16[128,4,1024]{2,0,1:T(8,128)(2,1)}), bf16[128,4,1024]{2,0,1:T(8,128)(2,1)}, u32[]{:S(2)}, u32[]{:S(2)}) async-start(bf16[128,4,1024]{2,0,1:T(8,128)(2,1)} %copy.98), calls=%async_computation.1 | async-start | bytes 2097152 | tf_op jit(solution)/shard_map/all_to_all | solution.py:1068
  113.8 203.7 %all-gather.8.cloned.1.call-start = ((), (), s32[]{:S(2)}) async-start(), calls=%async_computation.11 | async-start | bytes 5242880 | tf_op jit(solution)/shard_map/all_gather | solution.py:1138
  113.9 150.7 %collective-permute-start.1 = (bf16[2,256,2048]{2,1,0:T(8,128)(2,1)S(1)}, bf16[2,256,2048]{2,1,0:T(8,128)(2,1)}, u32[]{:S(2)}, u32[]{:S(2)}) collective-permute-start(bf16[2,256,2048]{2,1,0:T(8,128)(2,1)S(1)} %copy-done.2), channel_id=1, source_target_pairs={{0,2},{2,0},{4,6},{6,4},{1,3},{3,1},{5,7},{7,5},{8,10},{10,8},{12,... | collective-permute-start | bytes 6291464 | tf_op jit(solution)/shard_map/ppermute | solution.py:1050
  115.2 31.5 %copy-start.7 = (f32[1024,128]{1,0:T(8,128)}, f32[1024,128]{1,0:T(8,128)S(1)}, u32[]{:S(2)}) copy-start(f32[1024,128]{1,0:T(8,128)S(1)} %copy.100.sin_ref) | copy-start | bytes 1572868
  117.3 29.4 %copy-start.8 = (f32[1024,128]{1,0:T(8,128)}, f32[1024,128]{1,0:T(8,128)S(1)}, u32[]{:S(2)}) copy-start(f32[1024,128]{1,0:T(8,128)S(1)} %copy.99.cos_ref) | copy-start | bytes 1572868
  128.3 47.3 %collective-permute-start = (bf16[2,256,2048]{2,1,0:T(8,128)(2,1)S(1)}, bf16[2,256,2048]{2,1,0:T(8,128)(2,1)}, u32[]{:S(2)}, u32[]{:S(2)}) collective-permute-start(bf16[2,256,2048]{2,1,0:T(8,128)(2,1)S(1)} %copy-done.2), channel_id=1, source_target_pairs={{0,4},{2,6},{4,0},{6,2},{1,5},{3,7},{5,1},{7,3},{8,12},{10,14},{12... | collective-permute-start | bytes 6291464 | tf_op jit(solution)/shard_map/ppermute | solution.py:1048
  128.7 341.2 %reduce-scatter.5.cloned.1.call-start = ((), (), s32[]{:S(2)}) async-start(), calls=%async_computation.12 | async-start | bytes 5242880 | tf_op jit(solution)/shard_map/reduce_scatter | solution.py:1154
  136.1 39.6 %copy-start.17 = (bf16[16,128,640]{2,1,0:T(8,128)(2,1)}, bf16[16,128,640]{2,1,0:T(8,128)(2,1)S(1)}, u32[]{:S(2)}) copy-start(bf16[16,128,640]{2,1,0:T(8,128)(2,1)S(1)} %slice.45) | copy-start | bytes 7864324
  175.6 88.9 %collective-permute-start.2 = (bf16[2,256,2048]{2,1,0:T(8,128)(2,1)}, bf16[2,256,2048]{2,1,0:T(8,128)(2,1)}, u32[]{:S(2)}, u32[]{:S(2)}) collective-permute-start(bf16[2,256,2048]{2,1,0:T(8,128)(2,1)} %collective-permute-done.far_ref), channel_id=1, source_target_pairs={{0,2},{2,0},{4,6},{6,4},{1,3},{3,1},{5,7},{7,5},{8,10},{10,8},{12,... | collective-permute-start | bytes 6291464 | tf_op jit(solution)/shard_map/ppermute | solution.py:1050
  176.7 44.0 %copy-start.16 = (bf16[256,2048]{1,0:T(8,128)(2,1)S(1)}, bf16[256,2048]{1,0:T(8,128)(2,1)}, u32[]{:S(2)}) copy-start(bf16[256,2048]{1,0:T(8,128)(2,1)} %get-tuple-element.41.block_ref) | copy-start | bytes 3145732
  267.6 3.2 copy-start
  270.9 35.9 %copy-start.1 = (bf16[2,1024,2048]{2,1,0:T(8,128)(2,1)S(1)}, bf16[2,1024,2048]{2,1,0:T(8,128)(2,1)}, u32[]{:S(2)}) copy-start(bf16[2,1024,2048]{2,1,0:T(8,128)(2,1)} %copy-done) | copy-start | bytes 25165828
  317.4 227.3 %reduce-scatter.7.cloned.1.call-start = ((), (), s32[]{:S(2)}) async-start(), calls=%async_computation.13 | async-start | bytes 5242880 | tf_op jit(solution)/shard_map/reduce_scatter | solution.py:1159
  395.8 234.1 %reduce-scatter.11.cloned.1.call-start = ((), (), s32[]{:S(2)}) async-start(), calls=%async_computation.15 | async-start | bytes 5242880 | tf_op jit(solution)/shard_map/reduce_scatter | solution.py:1164
  395.8 3.0 copy-start.14
  395.8 3.5 copy-start.20
  454.9 196.6 %reduce-scatter.9.cloned.1.call-start = ((), (), s32[]{:S(2)}) async-start(), calls=%async_computation.14 | async-start | bytes 3276800 | tf_op jit(solution)/shard_map/reduce_scatter | solution.py:1183
  532.2 8.0 %copy-start.21 = (bf16[2048,384]{1,0:T(8,128)(2,1)}, bf16[2048,384]{1,0:T(8,128)(2,1)S(1)}, u32[]{:S(2)}) copy-start(bf16[2048,384]{1,0:T(8,128)(2,1)S(1)} %constant_dynamic-update-slice_fusion.refs_0_) | copy-start | bytes 4718596
  532.3 8.0 %copy-start.23 = (bf16[2048,256]{0,1:T(8,128)(2,1)S(1)}, bf16[2048,256]{0,1:T(8,128)(2,1)}, u32[]{:S(2)}) copy-start(bf16[2048,256]{0,1:T(8,128)(2,1)} %convolution_convert_fusion.4) | copy-start | bytes 3145732
  544.7 58.7 %copy-start.19 = (f32[256,2048]{1,0:T(8,128)S(1)}, f32[256,2048]{1,0:T(8,128)}, u32[]{:S(2)}) copy-start(f32[256,2048]{1,0:T(8,128)} %get-tuple-element.122) | copy-start | bytes 6291460
  601.0 2.3 copy-start.18
  604.1 30.1 %copy-start.15 = (f32[256,2048]{1,0:T(8,128)S(1)}, f32[256,2048]{1,0:T(8,128)}, u32[]{:S(2)}) copy-start(f32[256,2048]{1,0:T(8,128)} %copy-done.13) | copy-start | bytes 6291460
  604.1 62.7 %collective-permute-start.4 = (bf16[256,2048]{1,0:T(8,128)(2,1)S(1)}, bf16[256,2048]{1,0:T(8,128)(2,1)}, u32[]{:S(2)}, u32[]{:S(2)}) collective-permute-start(bf16[256,2048]{1,0:T(8,128)(2,1)S(1)} %fusion.10), channel_id=1, source_target_pairs={{0,1},{1,0},{2,3},{3,2},{4,5},{5,4},{6,7},{7,6},{8,9},{9,8},{10,11... | collective-permute-start | bytes 3145736 | tf_op jit(solution)/shard_map/ppermute | solution.py:1193
  629.9 18.8 %all-to-all-start.3 = ((bf16[4,128,1024]{2,1,0:T(8,128)(2,1)}), bf16[4,128,1024]{2,1,0:T(8,128)(2,1)}, u32[]{:S(2)}, u32[]{:S(2)}) async-start(bf16[4,128,1024]{2,1,0:T(8,128)(2,1)} %bitcast.109), calls=%async_computation.7 | async-start | bytes 2097152 | tf_op jit(solution)/shard_map/all_to_all | solution.py:1072
  634.2 3.9 copy-start.22
  637.1 25.8 %collective-permute-start.3 = (bf16[256,2048]{1,0:T(8,128)(2,1)}, bf16[256,2048]{1,0:T(8,128)(2,1)}, u32[]{:S(2)}, u32[]{:S(2)}) collective-permute-start(bf16[256,2048]{1,0:T(8,128)(2,1)} %add_convert_fusion), channel_id=1, source_target_pairs={{0,1},{1,0},{2,3},{3,2},{4,5},{5,4},{6,7},{7,6},{8,9},{9,8},{10,11... | collective-permute-start | bytes 3145736 | tf_op jit(solution)/shard_map/ppermute | solution.py:1193
  653.6 17.2 %all-to-all-start.4 = ((bf16[4,128,640]{1,2,0:T(8,128)(2,1)}), bf16[4,128,640]{1,2,0:T(8,128)(2,1)S(1)}, u32[]{:S(2)}, u32[]{:S(2)}) async-start(bf16[4,128,640]{1,2,0:T(8,128)(2,1)} %copy_bitcast_fusion), calls=%async_computation.8 | async-start | bytes 1310720 | tf_op jit(solution)/shard_map/all_to_all | solution.py:1202
  (13 other events, 18.7 us)
Sparse Core Ops, SparseCore 0:
  28.1 58.2 all-gather.3
  88.6 148.3 all-gather.5
  238.5 78.9 all-gather.7
  319.7 75.2 reduce-scatter.4
  397.8 77.2 reduce-scatter.6
  477.3 77.2 reduce-scatter.10
  557.0 52.5 reduce-scatter.8

commit v3 on v2

--- a/solution.py
+++ b/solution.py
@@ -318,9 +318,27 @@
     )
 
 
-def gather_kernel(rows, block_ref, all_ref, send_sems, recv_sems, local_sem):
+def gather_kernel(rows, works, planes, block_ref, *refs):
+    if works:
+        left_ref, right_ref, all_ref, grad_ref, send_sems, recv_sems, local_sem = refs
+    elif planes:
+        gains_ref, all_ref, all_gains_ref, send_sems, recv_sems, local_sem, *gain_sems = refs
+    else:
+        all_ref, send_sems, recv_sems, local_sem = refs
     side, row, core, near_core, near_side, near_row = place()
     half = rows // 2
+
+    def work(first, last):
+        if not works:
+            return
+        size = left_ref.shape[1] // works
+
+        def step(index, carry):
+            at = pl.ds(pl.multiple_of(index * size, size), size)
+            grad_ref[at, :] = matmul_t(left_ref[:, at], right_ref[...]).astype(BF16)
+            return carry
+
+        lax.fori_loop(first * works // 8, last * works // 8, step, 0)
 
     def spot(a, b, c, part=None):
         start = (a * 4 + b * 2 + c) * rows
@@ -328,7 +346,17 @@
             return all_ref.at[pl.ds(pl.multiple_of(start, rows), rows)]
         return all_ref.at[pl.ds(pl.multiple_of(start + part * half, half), half)]
 
-    greet((near_core, near_side, near_row))
+    targets = []
+    if planes:
+        plane = lax.axis_index("dp")
+        here = row * 2 + core
+        targets = [
+            {"dp": (plane + step) % planes, "ctx": (here + turn) % 4}
+            for step in range(planes)
+            for turn in range(4)
+            if step or turn
+        ]
+    greet([near_side] + (targets if planes else [near_core, near_row]))
     copies = []
 
     def send(number, source, target, device):
@@ -337,6 +365,15 @@
         copies.append(copy)
         return copy
 
+    gain_copies = []
+    if planes:
+        mine = all_gains_ref.at[plane * 4 + here]
+        gain_copies = [
+            remote(gains_ref, mine, gain_sems[0].at[at], gain_sems[1].at[at], target)
+            for at, target in enumerate(targets)
+        ] + [pltpu.make_async_copy(gains_ref, mine, gain_sems[2])]
+        for copy in gain_copies:
+            copy.start()
     first = block_ref.at[pl.ds(0, half)]
     second = block_ref.at[pl.ds(half, half)]
     side_b = send(0, second, spot(side, row, core, 1), near_side)
@@ -346,10 +383,12 @@
     core_own = send(4, block_ref, spot(side, row, core), near_core)
     local = pltpu.make_async_copy(block_ref, spot(side, row, core), local_sem)
     local.start()
+    work(0, 6)
     side_b.wait_recv()
     away_b = send(5, spot(1 - side, row, core, 1), spot(1 - side, row, core, 1), near_row)
     row_a.wait_recv()
     away_a = send(6, spot(side, 1 - row, core, 0), spot(side, 1 - row, core, 0), near_side)
+    work(6, 8)
     side_a.wait_recv()
     core_side = send(7, spot(1 - side, row, core), spot(1 - side, row, core), near_core)
     row_b.wait_recv()
@@ -366,27 +405,46 @@
         copy.wait_recv()
     for copy in copies:
         copy.wait_send()
+    for copy in gain_copies:
+        copy.wait()
     local.wait()
 
 
-def plane_gather(block):
+def plane_gather(block, number=0, pair=None, gains=None):
     rows, width = block.shape
+    anywhere, vmem = pl.BlockSpec(memory_space=pl.ANY), pl.BlockSpec(memory_space=pltpu.VMEM)
+    shapes, ins, outs = [jax.ShapeDtypeStruct((8 * rows, width), block.dtype)], [anywhere], [anywhere]
+    operands = [block]
+    if pair is not None:
+        shapes.append(jax.ShapeDtypeStruct((pair[0].shape[1], pair[1].shape[1]), BF16))
+        ins += [vmem, vmem]
+        outs += [vmem]
+        operands += pair
+    planes, scratch = 0, []
+    if gains is not None:
+        planes = lax.axis_size("dp")
+        shapes.append(jax.ShapeDtypeStruct((4 * planes,) + gains.shape, gains.dtype))
+        ins += [vmem]
+        outs += [vmem]
+        operands += [gains]
+        scratch = [pltpu.SemaphoreType.DMA((4 * planes - 1,))] * 2 + [pltpu.SemaphoreType.DMA]
     return pl.pallas_call(
-        functools.partial(gather_kernel, rows),
-        out_shape=jax.ShapeDtypeStruct((8 * rows, width), block.dtype),
-        in_specs=[pl.BlockSpec(memory_space=pl.ANY)],
-        out_specs=pl.BlockSpec(memory_space=pl.ANY),
+        functools.partial(gather_kernel, rows, 8 if pair is not None else 0, planes),
+        out_shape=tuple(shapes),
+        in_specs=ins,
+        out_specs=tuple(outs),
         scratch_shapes=[
             pltpu.SemaphoreType.DMA((11,)),
             pltpu.SemaphoreType.DMA((11,)),
             pltpu.SemaphoreType.DMA,
-        ],
-        compiler_params=pltpu.CompilerParams(collective_id=0, has_side_effects=True),
-        cost_estimate=pl.CostEstimate(
-            flops=0, bytes_accessed=64 * rows * width * 2, transcendentals=0
+        ]
+        + scratch,
+        compiler_params=pltpu.CompilerParams(
+            collective_id=number, has_side_effects=True, vmem_limit_bytes=60 * 1024 * 1024
         ),
+        cost_estimate=pl.CostEstimate(flops=0, bytes_accessed=1024, transcendentals=0),
         name="plane_gather",
-    )(block)
+    )(*operands)
 
 
 def swap_scratch():
@@ -409,17 +467,19 @@
     return away, pltpu.make_async_copy(block(here), out_ref.at[here], local_sem)
 
 
-def scatter_steps(rows, lefts, right, out_ref, scratch, prepare=None, swap=None):
-    mine, theirs, other, to_side, to_row, from_side, from_row = scratch[:7]
-    on_side, on_row, got_side, got_row, send_sems, recv_sems = scratch[7:]
+def scatter_steps(rows, left_of, right_of, out_ref, scratch, swap=None, late=None):
+    made, other, to_side, to_row, from_side, from_row = scratch[:6]
+    on_side, on_row, got_side, got_row, send_sems, recv_sems = scratch[6:]
     side, row, core, near_core, near_side, near_row = place()
-    half = rows // 2
     tile = 32
-    width = out_ref.shape[1]
-    wide = 512
+    wide = out_ref.shape[1] // 2
 
     chips = ((side, row), (1 - side, row), (side, 1 - row), (1 - side, 1 - row))
-    routes = [(theirs.at[chip], other.at[chip], near_core) for chip in range(4)] + [
+    routes = [
+        (made.at[chip, part, 1 - core], other.at[chip, part], near_core)
+        for chip in range(4)
+        for part in range(2)
+    ] + [
         (to_side.at[0], from_side.at[0], near_side),
         (to_row.at[0], from_row.at[0], near_row),
         (to_side.at[1], from_side.at[1], near_side),
@@ -431,167 +491,155 @@
         remote(source, target, send_sems.at[at], recv_sems.at[at], device)
         for at, (source, target, device) in enumerate(routes)
     ]
-
-    order = [(chip, owner) for chip in (3, 1, 2, 0) for owner in (1 - core, core)]
-    starts = [
-        pl.multiple_of((chips[chip][0] * 4 + chips[chip][1] * 2 + owner) * rows, rows)
-        for chip, owner in order
-    ]
-
+    side_0, row_0, side_1, row_1, last_row, last_side = copies[8:]
     swapped = None if swap is None else swap_copies(*swap)
 
-    def product(target, number, twin):
-        turn = 2 * (3, 1, 2, 0).index(number) + twin
-        start = starts[turn]
-        if prepare is not None:
-            prepare(turn, starts)
-
-        def step(index, carry):
-            at = pl.multiple_of(index * wide, wide)
-            value = None
-            for which, left in enumerate(lefts):
-                term = matmul_nt(left[pl.ds(start, rows), :], right[which, pl.ds(at, wide), :])
-                value = term if value is None else value + term
-            target[number, :, pl.ds(at, wide)] = value.astype(BF16)
-            return carry
-
-        lax.fori_loop(0, width // wide, step, 0)
-
-    def give(number):
-        product(theirs, number, 0)
-        if number == 3:
+    def make(chip, part, first=False):
+        a, b = chips[chip]
+        start = pl.multiple_of((a * 4 + b * 2) * rows, 2 * rows)
+        value = matmul_nt(left_of(chip, start), right_of(pl.ds(part * wide, wide)))
+        made[chip, part, 0] = value[:rows].astype(BF16)
+        made[chip, part, 1] = value[rows:].astype(BF16)
+        if first:
             partners = (near_core, near_side, near_row)
             if swap is not None:
                 partners += ({"ctx": (1 - row) * 2 + 1 - core},)
             greet(partners)
-        copies[number].start()
-
-    def take(number):
-        product(mine, number, 1)
-        copies[number].wait_recv()
-
-    def both(number, part, at):
-        at = part * half + at
-        here = mine[number, pl.ds(at, tile), :].astype(F32)
-        return here + other[number, pl.ds(at, tile), :].astype(F32)
+        copies[2 * chip + part].start()
+
+    def both(chip, part, at):
+        here = made[chip, part, core, pl.ds(at, tile), :].astype(F32)
+        return here + other[chip, part, pl.ds(at, tile), :].astype(F32)
 
     def each(body):
         def step(index, carry):
             body(pl.multiple_of(index * tile, tile))
             return carry
 
-        lax.fori_loop(0, half // tile, step, 0)
-
-    def put(target, number, part, extra=None):
+        lax.fori_loop(0, rows // tile, step, 0)
+
+    def put(target, chip, part, copy, extra=None):
+        copies[2 * chip + part].wait_recv()
+
         def body(at):
-            value = both(number, part, at)
+            value = both(chip, part, at)
             if extra is not None:
                 value = value + extra[pl.ds(at, tile), :].astype(F32)
             target[pl.ds(at, tile), :] = value.astype(BF16)
 
         each(body)
+        copy.start()
 
     def across():
-        give(3)
-        take(3)
-        put(to_side.at[0], 3, 0)
-        copies[4].start()
-        put(to_row.at[0], 3, 1)
-        copies[5].start()
+        make(3, 0, True)
+        make(3, 1)
+        put(to_side.at[0], 3, 0, side_0)
+        put(to_row.at[0], 3, 1, row_0)
         if swap is not None:
             for copy in swapped[0] + [swapped[1]]:
                 copy.start()
 
     def along():
-        give(1)
-        take(1)
-        put(to_side.at[1], 1, 0)
-        copies[6].start()
-        give(2)
-        take(2)
-        put(to_row.at[1], 2, 1)
-        copies[7].start()
+        make(1, 0)
+        make(2, 1)
+        put(to_side.at[1], 1, 0, side_1)
+        put(to_row.at[1], 2, 1, row_1)
 
     def forward():
-        copies[4].wait_recv()
-        put(on_row, 2, 0, from_side.at[0])
-        copies[8].start()
-        copies[5].wait_recv()
-        put(on_side, 1, 1, from_row.at[0])
-        copies[9].start()
+        make(1, 1)
+        make(2, 0)
+        row_0.wait_recv()
+        put(on_side, 1, 1, last_side, from_row.at[0])
+        side_0.wait_recv()
+        put(on_row, 2, 0, last_row, from_side.at[0])
 
     def own():
-        give(0)
-        take(0)
+        make(0, 0)
+        make(0, 1)
 
     def finish():
-        copies[6].wait_recv()
-        copies[7].wait_recv()
+        copies[0].wait_recv()
+        copies[1].wait_recv()
+        side_1.wait_recv()
+        row_1.wait_recv()
 
         def first_sum(at):
-            out_ref[pl.ds(at, tile), :] = both(0, 0, at) + from_side[
-                1, pl.ds(at, tile), :
-            ].astype(F32)
-            out_ref[pl.ds(half + at, tile), :] = both(0, 1, at) + from_row[
-                1, pl.ds(at, tile), :
-            ].astype(F32)
+            here = pl.ds(at, tile)
+            out_ref[here, :wide] = both(0, 0, at) + from_side[1, here, :].astype(F32)
+            out_ref[here, wide:] = both(0, 1, at) + from_row[1, here, :].astype(F32)
 
         each(first_sum)
-        copies[8].wait_recv()
-        copies[9].wait_recv()
-
-        def last_sum(at):
-            out_ref[pl.ds(at, tile), :] += got_row[pl.ds(at, tile), :].astype(F32)
-            out_ref[pl.ds(half + at, tile), :] += got_side[pl.ds(at, tile), :].astype(F32)
-
-        each(last_sum)
-        for copy in copies:
-            copy.wait_send()
         if swap is not None:
             for copy in swapped[0]:
                 copy.wait()
             swapped[1].wait()
+            late()
+        last_side.wait_recv()
+        last_row.wait_recv()
+
+        def last_sum(at):
+            here = pl.ds(at, tile)
+            out_ref[here, :wide] += got_row[here, :].astype(F32)
+            out_ref[here, wide:] += got_side[here, :].astype(F32)
+
+        each(last_sum)
+        for copy in copies:
+            copy.wait_send()
 
     return across, along, forward, own, finish
 
 
 def scatter_scratch(rows, width):
-    half = rows // 2
+    half = width // 2
     return (
-        [pltpu.VMEM((4, rows, width), BF16)] * 3
-        + [pltpu.VMEM((2, half, width), BF16)] * 4
-        + [pltpu.VMEM((half, width), BF16)] * 4
-        + [pltpu.SemaphoreType.DMA((10,))] * 2
-    )
-
-
-def scatter_kernel(rows, terms, swaps, *refs):
-    lefts, right, refs = refs[:terms], refs[terms], refs[terms + 1 :]
-    swap = None
+        [pltpu.VMEM((4, 2, 2, rows, half), BF16), pltpu.VMEM((4, 2, rows, half), BF16)]
+        + [pltpu.VMEM((2, rows, half), BF16)] * 4
+        + [pltpu.VMEM((rows, half), BF16)] * 4
+        + [pltpu.SemaphoreType.DMA((14,))] * 2
+    )
+
+
+def scatter_kernel(rows, swaps, columns, left, right, *refs):
+    swap, late = None, None
     if swaps:
-        in_ref, out_ref, swapped_ref, *scratch = refs
-        swap = (in_ref, swapped_ref, *scratch[-3:])
-        scratch = scratch[:-3]
+        in_ref, out_ref, laid_ref, *scratch = refs
+        swapped = scratch[-4]
+        swap = (in_ref, swapped, *scratch[-3:])
+        scratch = scratch[:-4]
+
+        def late():
+            size = swapped.shape[2]
+            for part in range(4):
+                laid_ref[:, part * size : (part + 1) * size] = swapped[part]
+
     else:
         out_ref, *scratch = refs
-    for step in scatter_steps(rows, lefts, right, out_ref, scratch, swap=swap):
+
+    def left_of(chip, start):
+        return left[pl.ds(start, 2 * rows), :]
+
+    def right_of(at):
+        return right[at, columns]
+
+    for step in scatter_steps(rows, left_of, right_of, out_ref, scratch, swap=swap, late=late):
         step()
 
 
-def product_scatter(number, lefts, right, swap=None):
-    total = lefts[0].shape[0]
-    width = right.shape[1]
+def product_scatter(number, left, right, start, size, swap=None):
+    total = left.shape[0]
+    width = right.shape[0]
     rows = total // 8
     vmem = pl.BlockSpec(memory_space=pltpu.VMEM)
-    shapes, ins, scratch = [jax.ShapeDtypeStruct((rows, width), F32)], [vmem] * (len(lefts) + 1), []
-    operands = [*lefts, right]
+    shapes, ins, scratch = [jax.ShapeDtypeStruct((rows, width), F32)], [vmem, vmem], []
+    operands = [left, right]
     if swap is not None:
-        shapes.append(jax.ShapeDtypeStruct((4, swap.shape[0] // 4, swap.shape[1]), swap.dtype))
+        deep = swap.shape[0] // 4
+        shapes.append(jax.ShapeDtypeStruct((deep, 4 * swap.shape[1]), swap.dtype))
         ins.append(pl.BlockSpec(memory_space=pl.ANY))
         operands.append(swap)
-        scratch = swap_scratch()
+        scratch = [pltpu.VMEM((4, deep, swap.shape[1]), swap.dtype)] + swap_scratch()
     return pl.pallas_call(
-        functools.partial(scatter_kernel, rows, len(lefts), swap is not None),
+        functools.partial(scatter_kernel, rows, swap is not None, slice(start, start + size)),
         out_shape=tuple(shapes),
         in_specs=ins,
         out_specs=tuple([vmem] * len(shapes)),
@@ -606,7 +654,10 @@
 
 def ffn_back_kernel(
     rows,
-    cot_ref,
+    own_ref,
+    far_ref,
+    twin_ref,
+    twin_far_ref,
     gate_slope_ref,
     up_slope_ref,
     down_ref,
@@ -617,51 +668,94 @@
     cots,
     gate_slopes,
     up_slopes,
+    lefts,
     sems,
+    out_sems,
     *scratch,
 ):
-    wide = 512
-    sources = ((cot_ref, cots), (gate_slope_ref, gate_slopes), (up_slope_ref, up_slopes))
-
-    def fetch(turn, starts):
+    side, row, core, *_ = place()
+    units = down_ref.shape[1]
+    turns = (3, 1, 2, 0)
+    chips = ((side, row), (1 - side, row), (side, 1 - row), (1 - side, 1 - row))
+    starts = [pl.multiple_of((a * 4 + b * 2) * rows, 2 * rows) for a, b in chips]
+    stored = []
+
+    def fetch(turn):
+        chip = turns[turn]
+        near, away = (own_ref, twin_ref) if chip < 2 else (far_ref, twin_far_ref)
+        there = pl.ds(starts[chip], 2 * rows)
+        slot = turn % 2
+        return [
+            pltpu.make_async_copy(source, target, sems.at[which, slot])
+            for which, (source, target) in enumerate(
+                (
+                    (near.at[chips[chip][0]], cots.at[slot, core]),
+                    (away.at[chips[chip][0]], cots.at[slot, 1 - core]),
+                    (gate_slope_ref.at[there], gate_slopes.at[slot]),
+                    (up_slope_ref.at[there], up_slopes.at[slot]),
+                )
+            )
+        ]
+
+    def store(turn):
+        there = pl.ds(starts[turns[turn]], 2 * rows)
+        slot = turn % 2
         return [
             pltpu.make_async_copy(
-                source.at[pl.ds(starts[turn], rows)], target.at[turn % 2], sems.at[which, turn % 2]
+                lefts.at[slot, :, pl.ds(which * units, units)],
+                target.at[there],
+                out_sems.at[which, slot],
             )
-            for which, (source, target) in enumerate(sources)
+            for which, target in enumerate((gate_ref, up_ref))
         ]
 
-    def prepare(turn, starts):
+    def start(copies):
+        for copy in copies:
+            copy.start()
+
+    def wait(copies):
+        for copy in copies:
+            copy.wait()
+
+    def left_of(chip, _):
+        turn = turns.index(chip)
+        slot = turn % 2
+        if chip in stored:
+            return lefts[slot]
+        stored.append(chip)
         if turn == 0:
-            for copy in fetch(0, starts):
-                copy.start()
-        if turn < 7:
-            for copy in fetch(turn + 1, starts):
-                copy.start()
-        for copy in fetch(turn, starts):
-            copy.wait()
-        slot = turn % 2
-        here = pl.ds(starts[turn], rows)
-
-        def step(index, carry):
-            at = pl.ds(pl.multiple_of(index * wide, wide), wide)
-            grad = jnp.dot(cots[slot], down_ref[:, at], preferred_element_type=F32)
-            gate_ref[here, at] = (grad * gate_slopes[slot, :, at].astype(F32)).astype(BF16)
-            up_ref[here, at] = (grad * up_slopes[slot, :, at].astype(F32)).astype(BF16)
-            return carry
-
-        lax.fori_loop(0, down_ref.shape[1] // wide, step, 0)
-
-    for step in scatter_steps(rows, [gate_ref, up_ref], right_ref, out_ref, scratch, prepare):
+            start(fetch(0))
+        if turn == 1:
+            start(fetch(2))
+        if turn == 2:
+            start(fetch(3))
+        if turn == 0:
+            start(fetch(1))
+        wait(fetch(turn))
+        if turn > 1:
+            wait(store(turn - 2))
+        cot = cots[slot].reshape(2 * rows, cots.shape[3])
+        grad = jnp.dot(cot, down_ref[...], preferred_element_type=F32)
+        lefts[slot, :, :units] = (grad * gate_slopes[slot].astype(F32)).astype(BF16)
+        lefts[slot, :, units:] = (grad * up_slopes[slot].astype(F32)).astype(BF16)
+        start(store(turn))
+        return lefts[slot]
+
+    def right_of(at):
+        return right_ref[at, :]
+
+    for step in scatter_steps(rows, left_of, right_of, out_ref, scratch):
         step()
-
-
-def ffn_back(number, cot, gate_slope, up_slope, down_w, gate_up):
-    total, width = cot.shape
-    units = down_w.shape[1]
+    wait(store(2))
+    wait(store(3))
+
+
+def ffn_back(number, cots, gate_slope, up_slope, down_w, gate_up):
+    total, units = gate_slope.shape
+    width = down_w.shape[0]
     rows = total // 8
     vmem = pl.BlockSpec(memory_space=pltpu.VMEM)
-    left = pl.BlockSpec(memory_space=pl.ANY)
+    anywhere = pl.BlockSpec(memory_space=pl.ANY)
     return pl.pallas_call(
         functools.partial(ffn_back_kernel, rows),
         out_shape=(
@@ -669,45 +763,44 @@
             jax.ShapeDtypeStruct((total, units), BF16),
             jax.ShapeDtypeStruct((total, units), BF16),
         ),
-        in_specs=[left, left, left, vmem, vmem],
-        out_specs=(vmem, vmem, vmem),
+        in_specs=[anywhere] * 6 + [vmem, vmem],
+        out_specs=(vmem, anywhere, anywhere),
         scratch_shapes=[
-            pltpu.VMEM((2, rows, width), BF16),
-            pltpu.VMEM((2, rows, units), BF16),
-            pltpu.VMEM((2, rows, units), BF16),
-            pltpu.SemaphoreType.DMA((3, 2)),
+            pltpu.VMEM((2, 2, rows, width), BF16),
+            pltpu.VMEM((2, 2 * rows, units), BF16),
+            pltpu.VMEM((2, 2 * rows, units), BF16),
+            pltpu.VMEM((2, 2 * rows, 2 * units), BF16),
+            pltpu.SemaphoreType.DMA((4, 2)),
+            pltpu.SemaphoreType.DMA((2, 2)),
         ]
         + scatter_scratch(rows, width),
         compiler_params=pltpu.CompilerParams(
-            collective_id=number, has_side_effects=True, vmem_limit_bytes=56 * 1024 * 1024
+            collective_id=number, has_side_effects=True, vmem_limit_bytes=60 * 1024 * 1024
         ),
         cost_estimate=pl.CostEstimate(flops=0, bytes_accessed=1024, transcendentals=0),
         name="ffn_back",
-    )(cot, gate_slope, up_slope, down_w, gate_up)
+    )(*cots, gate_slope, up_slope, down_w, gate_up)
 
 
 def ffn_kernel(in_ref, w_ref, product_ref, gate_slope_ref, up_slope_ref):
-    wide = 256
+    units = product_ref.shape[1]
+    wide = 512
     rows_in = in_ref[...]
-
-    def step(index, carry):
-        at = pl.ds(pl.multiple_of(index * wide, wide), wide)
-        gate = jnp.dot(rows_in, w_ref[0, :, at], preferred_element_type=F32)
-        up = jnp.dot(rows_in, w_ref[1, :, at], preferred_element_type=F32)
+    for start in range(0, units, wide):
+        at = pl.ds(start, wide)
+        gate = jnp.dot(rows_in, w_ref[:, at], preferred_element_type=F32)
+        up = jnp.dot(rows_in, w_ref[:, pl.ds(units + start, wide)], preferred_element_type=F32)
         sigma = jax.nn.sigmoid(gate)
         active = gate * sigma
         product_ref[:, at] = (active * up).astype(BF16)
         gate_slope_ref[:, at] = (up * sigma * (1.0 + gate * (1.0 - sigma))).astype(BF16)
         up_slope_ref[:, at] = active.astype(BF16)
-        return carry
-
-    lax.fori_loop(0, w_ref.shape[2] // wide, step, 0)
 
 
 def ffn(rows_in, gate_up):
     total, width = rows_in.shape
-    units = gate_up.shape[2]
-    rows = 256
+    units = gate_up.shape[1] // 2
+    rows = 512
     out = pl.BlockSpec((rows, units), lambda i: (i, 0))
     return pl.pallas_call(
         ffn_kernel,
@@ -716,11 +809,11 @@
         in_specs=[
             pl.BlockSpec((rows, width), lambda i: (i, 0)),
             pl.BlockSpec(
-                (2, width, units), lambda i: (0, 0, 0), pipeline_mode=pl.Buffered(1)
+                (width, 2 * units), lambda i: (0, 0), pipeline_mode=pl.Buffered(1)
             ),
         ],
         out_specs=(out, out, out),
-        compiler_params=pltpu.CompilerParams(vmem_limit_bytes=40 * 1024 * 1024),
+        compiler_params=pltpu.CompilerParams(vmem_limit_bytes=60 * 1024 * 1024),
         cost_estimate=pl.CostEstimate(flops=0, bytes_accessed=1024, transcendentals=0),
         name="ffn",
     )(rows_in, gate_up)
@@ -836,21 +929,30 @@
     sin_ref,
     left_ref,
     right_ref,
+    hidden_ref,
     in_ref,
-    dq_ref,
-    dkv_ref,
+    back_ref,
     out_ref,
-    swapped_ref,
+    laid_ref,
     sum_ref,
+    ffn_ref,
+    swapped,
     *scratch,
 ):
+    def late():
+        size = swapped.shape[2]
+        for part in range(4):
+            turned = jnp.transpose(swapped[part].astype(F32))
+            laid_ref[part * size : (part + 1) * size, :] = turned.astype(BF16)
+
     across, along, forward, own, finish = scatter_steps(
         rows,
-        [left_ref],
-        right_ref,
-        out_ref,
+        lambda chip, start: left_ref[pl.ds(start, 2 * rows), :],
+        lambda at: right_ref[at, :],
+        ffn_ref,
         scratch[:-3],
-        swap=(in_ref, swapped_ref, *scratch[-3:]),
+        swap=(in_ref, swapped, *scratch[-3:]),
+        late=late,
     )
     scale = HEAD_DIM ** (-0.5)
     length = q_ref.shape[0] // seqs
@@ -910,7 +1012,7 @@
                 turned.append(out * scale)
             grad = jnp.concatenate(turned, axis=1)
             angle = pl.ds(block * QB, QB)
-            dq_ref[here, lanes_at] = (
+            back_ref[here, lanes_at] = (
                 grad * cos_ref[angle, :] - swap_halves(grad) * sin_ref[angle, :]
             ).astype(BF16)
 
@@ -919,50 +1021,82 @@
             grad = sum_ref[...]
             lane = lax.broadcasted_iota(jnp.int32, grad.shape, 1)
             back = grad * cos_ref[...] - swap_halves(grad) * sin_ref[...]
-            dkv_ref[pl.ds(base, length), :] = jnp.where(lane < HEAD_DIM, back, grad).astype(BF16)
+            back_ref[pl.ds(base, length), pairs * 128 :] = jnp.where(
+                lane < HEAD_DIM, back, grad
+            ).astype(BF16)
 
         return carry
 
     lax.fori_loop(0, seqs * pairs, one_pair, 0)
     finish()
 
-
-def attend_back(number, queries, keyvals, upstream, logs, cosine, signed, seqs, left, right, swap):
+    def add(index, carry):
+        at = pl.ds(pl.multiple_of(index * 32, 32), 32)
+        out_ref[at, :] = (hidden_ref[at, :] + ffn_ref[at, :]).astype(BF16)
+        return carry
+
+    lax.fori_loop(0, rows // 32, add, 0)
+
+
+def attend_back(
+    number, queries, keyvals, upstream, logs, cosine, signed, seqs, left, right, hidden, swap
+):
     total, width = queries.shape
     length = total // seqs
     rows = total // 8
+    deep = swap.shape[0] // 4
     vmem = pl.BlockSpec(memory_space=pltpu.VMEM)
     return pl.pallas_call(
         functools.partial(attend_back_kernel, seqs, rows),
         out_shape=(
-            jax.ShapeDtypeStruct((total, width), BF16),
-            jax.ShapeDtypeStruct((total, 128), BF16),
-            jax.ShapeDtypeStruct((rows, right.shape[1]), F32),
-            jax.ShapeDtypeStruct((4, swap.shape[0] // 4, swap.shape[1]), swap.dtype),
+            jax.ShapeDtypeStruct((total, width + 128), BF16),
+            jax.ShapeDtypeStruct(hidden.shape, BF16),
+            jax.ShapeDtypeStruct((4 * swap.shape[1], deep), BF16),
         ),
-        in_specs=[vmem] * 8 + [pl.BlockSpec(memory_space=pl.ANY)],
-        out_specs=(vmem, vmem, vmem, vmem),
-        scratch_shapes=[pltpu.VMEM((length, 128), F32)]
-        + scatter_scratch(rows, right.shape[1])
+        in_specs=[vmem] * 9 + [pl.BlockSpec(memory_space=pl.ANY)],
+        out_specs=(vmem, vmem, vmem),
+        scratch_shapes=[
+            pltpu.VMEM((length, 128), F32),
+            pltpu.VMEM(hidden.shape, F32),
+            pltpu.VMEM((4, deep, swap.shape[1]), BF16),
+        ]
+        + scatter_scratch(rows, right.shape[0])
         + swap_scratch(),
         compiler_params=pltpu.CompilerParams(
             collective_id=number, has_side_effects=True, vmem_limit_bytes=56 * 1024 * 1024
         ),
         cost_estimate=pl.CostEstimate(flops=0, bytes_accessed=1024, transcendentals=0),
         name="attend_back",
-    )(queries, keyvals, upstream, logs, cosine, signed, left, right, swap)
+    )(queries, keyvals, upstream, logs, cosine, signed, left, right, hidden, swap)
 
 
 def gain_kernel(
-    planes, parts, cols, terms_ref, out_ref, total, seen, far, mine, across, send_sems, recv_sems
+    planes,
+    parts,
+    cols,
+    terms_ref,
+    up_ref,
+    gain_ref,
+    laid_ref,
+    total,
+    seen,
+    far,
+    mine,
+    across,
+    swapped,
+    send_sems,
+    recv_sems,
+    *swap_sems,
 ):
     side, row, core, near_core, near_side, near_row = place()
     plane = lax.axis_index("dp")
     ctx = row * 2 + core
     others = [{"dp": (plane + step) % planes} for step in range(1, planes)]
-    greet((near_core, near_side, near_row) + tuple(others))
+    corner = {"ctx": (1 - row) * 2 + 1 - core}
+    greet((near_core, near_side, near_row, corner) + tuple(others))
     total[...] = terms_ref[...]
     copies = []
+    up_copies, up_local = swap_copies(up_ref, swapped, *swap_sems)
     for number, target in enumerate((near_core, near_row)):
         copy = remote(
             total, seen.at[number], send_sems.at[number], recv_sems.at[number], target
@@ -970,6 +1104,8 @@
         copy.start()
         copy.wait()
         total[...] += seen[number]
+    for copy in up_copies + [up_local]:
+        copy.start()
     for step, target in enumerate(others, 1):
         start = (((plane + step) % planes) * parts + ctx) * cols
         copy = remote(
@@ -990,34 +1126,92 @@
     last = remote(mine, across, send_sems.at[2], recv_sems.at[2], near_side)
     last.start()
     copies.append(last)
+    for copy in up_copies:
+        copy.wait()
+    up_local.wait()
+    size = swapped.shape[2]
+    for part in range(4):
+        laid_ref[:, part * size : (part + 1) * size] = swapped[part]
     last.wait_recv()
-    out_ref[...] = value + across[...]
+    gain_ref[...] = value + across[...]
     for copy in copies:
         copy.wait_send()
 
 
-def gain_sum(terms):
+def gain_sum(number, terms, up_sum):
     planes = lax.axis_size("dp")
     parts = lax.axis_size("ctx")
     rows, width = terms.shape
     cols = width // (planes * parts)
+    deep = up_sum.shape[0] // parts
+    vmem = pl.BlockSpec(memory_space=pltpu.VMEM)
+    anywhere = pl.BlockSpec(memory_space=pl.ANY)
     return pl.pallas_call(
         functools.partial(gain_kernel, planes, parts, cols),
-        out_shape=jax.ShapeDtypeStruct((rows, cols), F32),
-        in_specs=[pl.BlockSpec(memory_space=pltpu.VMEM)],
-        out_specs=pl.BlockSpec(memory_space=pltpu.VMEM),
+        out_shape=(
+            jax.ShapeDtypeStruct((rows, cols), F32),
+            jax.ShapeDtypeStruct((deep, parts * up_sum.shape[1]), BF16),
+        ),
+        in_specs=[vmem, anywhere],
+        out_specs=(vmem,) * 2,
         scratch_shapes=[
             pltpu.VMEM((rows, width), F32),
             pltpu.VMEM((2, rows, width), F32),
             pltpu.VMEM((planes - 1, rows, cols), F32),
             pltpu.VMEM((rows, cols), F32),
             pltpu.VMEM((rows, cols), F32),
+            pltpu.VMEM((parts, deep, up_sum.shape[1]), BF16),
             pltpu.SemaphoreType.DMA((planes + 2,)),
             pltpu.SemaphoreType.DMA((planes + 2,)),
-        ],
-        compiler_params=pltpu.CompilerParams(collective_id=2, has_side_effects=True),
+        ]
+        + swap_scratch(),
+        compiler_params=pltpu.CompilerParams(collective_id=number, has_side_effects=True),
+        cost_estimate=pl.CostEstimate(flops=0, bytes_accessed=1024, transcendentals=0),
         name="gain_sum",
-    )(terms)
+    )(terms, up_sum)
+
+
+def last_kernel(
+    q_cols, attn_ref, query_ref, key_ref, value_ref, wide_ref, swapped, *swap_sems
+):
+    _, row, core, near_core, _, near_row = place()
+    greet((near_core, near_row, {"ctx": (1 - row) * 2 + 1 - core}))
+    copies, local = swap_copies(attn_ref, swapped, *swap_sems)
+    for copy in copies + [local]:
+        copy.start()
+    for copy in copies:
+        copy.wait()
+    local.wait()
+    kv = key_ref.shape[1] // 4
+    for part in range(4):
+        query_ref[:, part * q_cols : (part + 1) * q_cols] = swapped[part, :, :q_cols]
+        turned = jnp.transpose(swapped[part, :, q_cols + 2 * kv :].astype(F32))
+        wide_ref[part * q_cols : (part + 1) * q_cols, :] = turned.astype(BF16)
+    for at, target in ((q_cols, key_ref), (q_cols + kv, value_ref)):
+        target[...] = jnp.concatenate(
+            [swapped[part, :, at : at + kv] for part in range(4)], axis=1
+        )
+
+
+def last_swap(number, attn_sum, q_cols, kv_cols):
+    parts = lax.axis_size("ctx")
+    deep = attn_sum.shape[0] // parts
+    vmem = pl.BlockSpec(memory_space=pltpu.VMEM)
+    return pl.pallas_call(
+        functools.partial(last_kernel, q_cols),
+        out_shape=(
+            jax.ShapeDtypeStruct((deep, parts * q_cols), BF16),
+            jax.ShapeDtypeStruct((deep, parts * kv_cols), BF16),
+            jax.ShapeDtypeStruct((deep, parts * kv_cols), BF16),
+            jax.ShapeDtypeStruct((parts * q_cols, deep), BF16),
+        ),
+        in_specs=[pl.BlockSpec(memory_space=pl.ANY)],
+        out_specs=(vmem,) * 4,
+        scratch_shapes=[pltpu.VMEM((parts, deep, attn_sum.shape[1]), BF16)] + swap_scratch(),
+        compiler_params=pltpu.CompilerParams(collective_id=number, has_side_effects=True),
+        cost_estimate=pl.CostEstimate(flops=0, bytes_accessed=1024, transcendentals=0),
+        name="last_swap",
+    )(attn_sum)
 
 
 def lay_kernel(own_ref, far_ref, twin_ref, twin_far_ref, all_ref, sems):
@@ -1057,7 +1251,105 @@
         compiler_params=pltpu.CompilerParams(vmem_limit_bytes=24 * 1024 * 1024),
         name="lay",
     )(block, far, twin, twin_far)
-    return whole.reshape(seqs * 4 * span, width)
+    return whole.reshape(seqs * 4 * span, width), (block, far, twin, twin_far)
+
+
+def deal_kernel(q_ref, kv_ref, out_ref, all_ref, send_sems, recv_sems, local_sems):
+    _, row, core, *_ = place()
+    here = row * 2 + core
+    peers = (row * 2 + 1 - core, (1 - row) * 2 + core, (1 - row) * 2 + 1 - core)
+    greet([{"ctx": peer} for peer in peers])
+    copies = []
+    start = 0
+    for which, source in enumerate((q_ref, kv_ref, out_ref)):
+        cols = source.shape[1] // 4
+        target = all_ref.at[here, :, pl.ds(start, cols)]
+        start += cols
+        for at, peer in enumerate(peers):
+            copies.append(
+                remote(
+                    source.at[:, pl.ds(pl.multiple_of(peer * cols, cols), cols)],
+                    target,
+                    send_sems.at[which, at],
+                    recv_sems.at[which, at],
+                    {"ctx": peer},
+                )
+            )
+        own = source.at[:, pl.ds(pl.multiple_of(here * cols, cols), cols)]
+        copies.append(pltpu.make_async_copy(own, target, local_sems.at[which]))
+    for copy in copies:
+        copy.start()
+    for copy in copies:
+        copy.wait()
+
+
+def deal(query, keyval, out):
+    rows = query.shape[0]
+    cols = (query.shape[1] + keyval.shape[1] + out.shape[1]) // 4
+    return pl.pallas_call(
+        deal_kernel,
+        out_shape=jax.ShapeDtypeStruct((4, rows, cols), BF16),
+        in_specs=[pl.BlockSpec(memory_space=pl.ANY)] * 3,
+        out_specs=pl.BlockSpec(memory_space=pltpu.VMEM),
+        scratch_shapes=[
+            pltpu.SemaphoreType.DMA((3, 3)),
+            pltpu.SemaphoreType.DMA((3, 3)),
+            pltpu.SemaphoreType.DMA((3,)),
+        ],
+        compiler_params=pltpu.CompilerParams(collective_id=6, has_side_effects=True),
+        cost_estimate=pl.CostEstimate(flops=0, bytes_accessed=1024, transcendentals=0),
+        name="deal",
+    )(query, keyval, out)
+
+
+def share_kernel(gate_ref, up_ref, all_ref, send_sems, recv_sems, local_sems):
+    _, row, core, *_ = place()
+    here = row * 2 + core
+    rows, units = gate_ref.shape[0], all_ref.shape[1] // 2
+    peers = (row * 2 + 1 - core, (1 - row) * 2 + core, (1 - row) * 2 + 1 - core)
+    greet([{"ctx": peer} for peer in peers])
+    copies = []
+    for which, source in enumerate((gate_ref, up_ref)):
+        target = all_ref.at[
+            pl.ds(pl.multiple_of(here * rows, rows), rows), pl.ds(which * units, units)
+        ]
+        for at, peer in enumerate(peers):
+            copies.append(
+                remote(
+                    source.at[:, pl.ds(pl.multiple_of(peer * units, units), units)],
+                    target,
+                    send_sems.at[which, at],
+                    recv_sems.at[which, at],
+                    {"ctx": peer},
+                )
+            )
+        own = source.at[:, pl.ds(pl.multiple_of(here * units, units), units)]
+        copies.append(pltpu.make_async_copy(own, target, local_sems.at[which]))
+    for copy in copies:
+        copy.start()
+    for copy in copies:
+        copy.wait()
+
+
+def share(gate, up):
+    parts = lax.axis_size("ctx")
+    anywhere = pl.BlockSpec(memory_space=pl.ANY)
+    return pl.pallas_call(
+        share_kernel,
+        out_shape=jax.ShapeDtypeStruct((parts * gate.shape[0], 2 * gate.shape[1] // parts), BF16),
+        in_specs=[anywhere, anywhere],
+        out_specs=anywhere,
+        scratch_shapes=[
+            pltpu.SemaphoreType.DMA((2, 3)),
+            pltpu.SemaphoreType.DMA((2, 3)),
+            pltpu.SemaphoreType.DMA((2,)),
+        ],
+        compiler_params=pltpu.CompilerParams(
+            collective_id=8, has_side_effects=True, vmem_limit_bytes=60 * 1024 * 1024
+        ),
+        cost_estimate=pl.CostEstimate(flops=0, bytes_accessed=1024, transcendentals=0),
+        name="share",
+    )(gate, up)
 
 
 def after(value, *earlier):
@@ -1068,8 +1360,8 @@
     return lax.all_to_all(weight, "ctx", split_axis=1, concat_axis=0, tiled=True)
 
 
-def from_units(grad):
-    return lax.all_to_all(grad, "ctx", split_axis=0, concat_axis=1, tiled=True)
+def swap_sides(block):
+    return lax.ppermute(block, "tensor", [(0, 1), (1, 0)])
 
 
 def on_plane(
@@ -1099,41 +1391,26 @@
     sine = jnp.sin(theta)
     signed = jnp.tile(jnp.concatenate([-sine, sine], axis=1), (1, 2))
 
-    gain_row = jnp.concatenate(
-        [attn_gain, ffn_gain, jnp.zeros((2 * q_cols + 2 * kv_cols - 2 * rows_w,), BF16)]
-    )
-    gain_rows = jnp.broadcast_to(gain_row[None, None, :], (parts, 8, gain_row.shape[0]))
-    mixed = jnp.concatenate(
-        [
-            w_query.reshape(rows_w, parts, q_cols),
-            w_key.reshape(rows_w, parts, kv_cols),
-            w_value.reshape(rows_w, parts, kv_cols),
-            w_out.T.reshape(rows_w, parts, q_cols),
-        ],
-        axis=2,
-    ).transpose(1, 0, 2)
-    mixed = jnp.concatenate([mixed, gain_rows], axis=1)
-    mixed = lax.all_to_all(mixed, "ctx", split_axis=0, concat_axis=0, tiled=True)
+    keyval = jnp.concatenate(
+        [w_key.reshape(rows_w, parts, kv_cols), w_value.reshape(rows_w, parts, kv_cols)], axis=2
+    ).reshape(rows_w, -1)
+    mixed = deal(w_query, keyval, w_out.T)
     ready_w = mixed
-    mixed = lax.all_gather(mixed, "dp", axis=0, tiled=True)
-    attn_w = mixed[:, :rows_w].reshape(width, -1)
-    gain_one = mixed[:, rows_w, :rows_w].reshape(width).astype(F32)
-    gain_two = mixed[:, rows_w, rows_w : 2 * rows_w].reshape(width).astype(F32)
+    attn_w = lax.all_gather(mixed.reshape(parts * rows_w, -1), "dp", axis=0, tiled=True)
     qkv_cols = q_cols + 2 * kv_cols
     w_qkv = attn_w[:, :qkv_cols]
     w_out_t = attn_w[:, qkv_cols:]
 
-    half_units = w_gate.shape[1] // parts
-    gate_up = jnp.stack(
-        [w_gate.reshape(rows_w, parts, half_units), w_up.reshape(rows_w, parts, half_units)]
-    )
-    gate_up = after(gate_up, ready_w).transpose(2, 0, 1, 3)
-    gate_up = lax.all_to_all(gate_up, "ctx", split_axis=0, concat_axis=0, tiled=True)
+    gate_up = share(after(w_gate, ready_w), w_up)
     own_in = lax.dynamic_index_in_dim(layer_input, side, 0, keepdims=False)
     own_cot = lax.dynamic_index_in_dim(cotangent, side, 0, keepdims=False)
-    all_in = plane_gather(after(own_in, ready_w))
-    gate_up = gate_up.transpose(1, 0, 2, 3).reshape(2, parts * rows_w, half_units)
-    gate_up = lax.all_gather(gate_up, "dp", axis=1, tiled=True)
+    gains = jnp.concatenate(
+        [attn_gain[None], ffn_gain[None], jnp.zeros((6, rows_w), BF16)]
+    ).astype(F32)
+    all_in, gains = plane_gather(after(own_in, ready_w), 10, gains=gains)
+    gain_one = gains[:, 0].reshape(width)
+    gain_two = gains[:, 1].reshape(width)
+    gate_up = lax.all_gather(gate_up, "dp", axis=0, tiled=True)
     down_own = to_units(after(w_down, all_in).T)
     down_w = lax.all_gather(down_own, "dp", axis=0, tiled=True)
 
@@ -1143,28 +1420,29 @@
     attended, queries, keyvals, logs = attend(pre, cosine, signed, seqs)
     inputs_f = own_in.astype(F32)
     factor_one = rms_factor(inputs_f)
-    hidden = inputs_f + product_scatter(1, [attended], w_out_t[None])[0]
+    hidden = inputs_f + product_scatter(1, attended, attn_w, qkv_cols, q_cols)[0]
     factor_two = rms_factor(hidden)
     normed_own = (hidden * factor_two * gain_two).astype(BF16)
-    normed_two = plane_gather(normed_own)
-    all_cot = along_ctx(cotangent, down_own, attended)
+    normed_two = plane_gather(normed_own)[0]
+    all_cot, cots = along_ctx(cotangent, down_own, attended)
 
     product, gate_slope, up_slope = ffn(normed_two, gate_up)
     down_grad = matmul_t(all_cot, product).astype(BF16)
     down_sum = lax.psum_scatter(down_grad, "dp", scatter_dimension=0, tiled=True)
     normed_two_grad, gate_grad, up_grad = ffn_back(
-        3, after(all_cot, down_grad), gate_slope, up_slope, down_w, gate_up
+        3, cots, after(gate_slope, down_grad), up_slope, down_w, gate_up
     )
     gate_w_grad = matmul_t(normed_two, gate_grad).astype(BF16)
     gate_sum = lax.psum_scatter(gate_w_grad, "dp", scatter_dimension=0, tiled=True)
     hidden_back, ffn_gain_term = rms_back(normed_two_grad, hidden, factor_two, gain_two)
     hidden_grad = own_cot.astype(F32) + hidden_back
-    hidden_low = plane_gather(after(hidden_grad.astype(BF16), gate_w_grad))
-    up_w_grad = matmul_t(normed_two, after(up_grad, hidden_low)).astype(BF16)
+    hidden_low, up_w_grad = plane_gather(
+        after(hidden_grad.astype(BF16), gate_w_grad), 7, [normed_two, up_grad]
+    )
     up_sum = lax.psum_scatter(up_w_grad, "dp", scatter_dimension=0, tiled=True)
     attended_grad = jnp.dot(after(hidden_low, up_w_grad), w_out_t, preferred_element_type=F32).astype(BF16)
     out_w_grad = matmul_t(hidden_low, attended).astype(BF16)
-    query_low, keyval_low, ffn_own, down_out = attend_back(
+    back, out_own, down_out = attend_back(
         5,
         queries,
         keyvals,
@@ -1174,50 +1452,43 @@
         signed,
         seqs,
         product,
-        down_w[None],
+        down_w,
+        hidden,
         down_sum,
     )
-    back = jnp.concatenate([query_low, keyval_low], axis=1)
+    out_other = swap_sides(out_own)
     qkv_grad = matmul_t(normed_one, back).astype(BF16)
     attn_grad = jnp.concatenate([qkv_grad, out_w_grad], axis=1)
     attn_sum = lax.psum_scatter(attn_grad, "dp", scatter_dimension=0, tiled=True)
     normed_one_grad, gate_out = product_scatter(
-        4, [after(back, attn_grad)], w_qkv[None], gate_sum
+        4, after(back, attn_grad), attn_w, 0, qkv_cols, gate_sum
     )
     input_back, attn_gain_term = rms_back(normed_one_grad, inputs_f, factor_one, gain_one)
     input_own = (hidden_grad + input_back).astype(BF16)
-    gain_own = gain_sum(after(jnp.stack([attn_gain_term, ffn_gain_term]), input_own))
-    out_own = (hidden + ffn_own).astype(BF16)
-
-    def both_sides(own):
-        other = lax.ppermute(own, "tensor", [(0, 1), (1, 0)])
+    input_other = swap_sides(input_own)
+    terms = jnp.stack([attn_gain_term, ffn_gain_term])
+    gain_own, up_out = gain_sum(2, after(terms, input_own, out_other), up_sum)
+    query_out, key_out, value_out, wide_out = last_swap(
+        9, after(attn_sum, gain_own), q_cols, kv_cols
+    )
+
+    def both_sides(own, other):
         return jnp.where(side == 0, jnp.stack([own, other]), jnp.stack([other, own]))
 
-    layer_output = both_sides(out_own)
-    input_grad = both_sides(input_own).astype(F32)
-    down_out, gate_out = (
-        swapped.transpose(1, 0, 2).reshape(rows_w, -1) for swapped in (down_out, gate_out)
-    )
-    up_out = from_units(after(up_sum, gain_own))
-    attn_out = lax.all_to_all(
-        after(attn_sum, up_out).reshape(parts, rows_w, -1), "ctx", split_axis=0, concat_axis=0, tiled=True
-    )
-
-    def columns(start, size):
-        return attn_out[:, :, start : start + size].transpose(1, 0, 2).reshape(rows_w, -1)
-
+    layer_output = both_sides(out_own, out_other)
+    input_grad = both_sides(input_own, after(input_other, gain_own)).astype(F32)
     return (
         layer_output,
         input_grad,
         gain_own[0],
-        columns(0, q_cols).astype(F32),
-        columns(q_cols, kv_cols).astype(F32),
-        columns(q_cols + kv_cols, kv_cols).astype(F32),
-        columns(qkv_cols, q_cols).T.astype(F32),
+        query_out.astype(F32),
+        key_out.astype(F32),
+        value_out.astype(F32),
+        wide_out.astype(F32),
         gain_own[1],
         gate_out.astype(F32),
         up_out.astype(F32),
-        down_out.T.astype(F32),
+        down_out.astype(F32),
     )
 
 

time: 691 us -> 649 us (0.939)
  Pallas kernels: 421 us -> 468 us
  blocking collectives: 44.3 us -> 0 us
  local copies, waits for them, and re-layouts: 52 us -> 23.9 us
  matrix products: 70.5 us -> 56.8 us
  starting transfers between devices: 15.4 us -> 6.96 us
    pallas_call x5 -> x8, Pallas kernels: 219 us -> 283 us  [the longest x3 131 us: plane_gather(): pl.pallas_call(functools.partial(gather_kernel, rows, 8 if pair is not No...]
    all_to_all x2 -> x0, blocking collectives: 44.3 us -> none  [the longest x1 29.3 us: on_plane(): lax.all_to_all(gate_up, 'ctx', split_axis=0, concat_axis=0, tiled=True)]
    dot_general x5 -> x4, matrix products: 53.7 us -> 39.5 us  [matmul_t(): lax.dot_general(left_op, right_op, (((0,), (0,)), ((), ())), preferred_el...]
    all_gather x1, waiting for transfers between devices: 0.11 us -> 13.3 us  [on_plane(): down_w = lax.all_gather(down_own, 'dp', axis=0, tiled=True)]
    unnamed x70 -> x53, local copies, waits for them, and re-layouts: 30 us -> 17.8 us
    pallas_call x1, Pallas kernels: 64 us -> 55 us  [ffn_back(): pl.pallas_call(functools.partial(ffn_back_kernel, rows), out_shape=(jax.S...]
    all_to_all x2 -> x0, starting transfers between devices: 7.73 us -> none  [the longest x1 4.25 us: from_units(): return lax.all_to_all(grad, 'ctx', split_axis=0, concat_axis=1, tiled=True)]
    convert_element_type x7 -> x8, other arithmetic: 12.3 us -> 15 us  [the longest x1 3.99 us: on_plane(): input_grad = both_sides(input_own, after(input_other, gain_own)).astype(F32)]
  transfers between devices with their start and end apart: 15 -> 13, of which waited for: 5 -> 3; matrix products, arithmetic and copies ran while one was open for 20% -> 15% of each run, Pallas kernels for 62% -> 69%
where the time goes in v3:
time: 649 us; the launch traced here: 642 us
  Pallas kernels  468 us (72%)
  matrix products  56.8 us (9%)
  other arithmetic  41.5 us (6%)
  waiting for transfers between devices  29.3 us (5%)
  local copies, waits for them, and re-layouts  23.9 us (4%)
  between operations  15.1 us (2%)
  starting transfers between devices  6.96 us (1%)
    pallas_call x3, Pallas kernels, plane_gather(): pl.pallas_call(functools.partial(gather_kernel, rows, 8 if pair is not No...  131 us
    pallas_call x2, Pallas kernels, product_scatter(): pl.pallas_call(functools.partial(scatter_kernel, rows, swap is not None,...  104 us
    pallas_call x1, Pallas kernels, attend_back(): pl.pallas_call(functools.partial(attend_back_kernel, seqs, rows), out_sha...  60.8 us
    pallas_call x1, Pallas kernels, ffn_back(): pl.pallas_call(functools.partial(ffn_back_kernel, rows), out_shape=(jax.S...  55 us
    dot_general x4, matrix products, matmul_t(): lax.dot_general(left_op, right_op, (((0,), (0,)), ((), ())), preferred_el...  39.5 us
    pallas_call x1, Pallas kernels, share(): pl.pallas_call(share_kernel, out_shape=jax.ShapeDtypeStruct((parts * gate...  25.5 us
    pallas_call x1, Pallas kernels, ffn(): pl.pallas_call(ffn_kernel, grid=(total // rows,), out_shape=(jax.ShapeDty...  25.1 us
    pallas_call x1, Pallas kernels, attend(): pl.pallas_call(functools.partial(attend_kernel, length), grid=(seqs, pair...  21 us
  transfers between devices with their start and end apart: 13, of which 3 were waited for; matrix products, arithmetic and copies ran while one was open for 15% of the time, Pallas kernels for 69%

profile of v3, /device:TPU:0, one launch (start us, length us, event | category | flops | bytes accessed | tf_op | source)
XLA Modules:
  0.0 641.5 jit_solution(16563566713456548421)
XLA Ops:
  11.7 12.4 %deal.1 = bf16[4,128,640]{2,1,0:T(8,128)(2,1)} custom-call(bf16[128,1024]{1,0:T(8,128)(2,1)} %q_ref.1, bf16[128,512]{1,0:T(8,128)(2,1)} %copy.39.kv_ref, bf16[128,1024]{1,0:T(8,128)(2,1)} %bitcast.50), custom_call_target="tpu_custom_call" | custom-call | bytes 1024 | tf_op jit(solution)/shard_map/deal/pallas_call | solution.py:1289
  24.2 25.5 %share.1 = bf16[512,2048]{1,0:T(8,128)(2,1)} custom-call(bf16[128,4096]{1,0:T(8,128)(2,1)} %gate_ref, bf16[128,4096]{1,0:T(8,128)(2,1)} %up_ref.1), custom_call_target="tpu_custom_call" | custom-call | bytes 1024 | tf_op jit(solution)/shard_map/share/pallas_call | solution.py:1337
  53.3 45.6 %plane_gather.3 = (bf16[2048,2048]{1,0:T(8,128)(2,1)}, f32[16,8,128]{2,1,0:T(8,128)}) custom-call(bf16[256,2048]{1,0:T(8,128)(2,1)} %get-tuple-element.49.block_ref, f32[8,128]{1,0:T(8,128)} %maximum_convert_fusion.refs_0_), custom_call_target="tpu_custom_call" | custom-call | bytes 1024 | tf_op jit(solution)/shard_map/plane_gather/pallas_call | solution.py:431
  100.2 3.5 all-to-all-start
  104.2 5.1 fusion
  109.4 8.8 %all-to-all-done = bf16[128,4,1024]{2,0,1:T(8,128)(2,1)S(1)} async-done(((bf16[128,4,1024]{2,0,1:T(8,128)(2,1)}), bf16[128,4,1024]{2,0,1:T(8,128)(2,1)S(1)}, u32[]{:S(2)}, u32[]{:S(2)}) %all-to-all-start) | async-done | bytes 1048608 | tf_op jit(solution)/shard_map/all_to_all | solution.py:1360
  123.3 10.1 %fusion.4.q_ref.kv_ref = f32[2048,384]{1,0:T(8,128)} fusion(bf16[2048,2048]{1,0:T(8,128)(2,1)} %get-tuple-element.50, f32[2048]{0:T(1024)S(1)} %bitcast.58, f32[2048]{0:T(1024)S(1)} %add_rsqrt_fusion, bf16[2048,640]{1,0:T(8,128)(2,1)} %all-gather.4.cloned.1.call-done.right), kind=kOutput, calls=%fused_computation.16 | convolution fusion | flops 3238002688 | bytes 13123584 | tf_op jit(solution)/shard_map/dot_general | solution.py:1419
  133.5 21.0 %attend.1 = (bf16[2048,256]{1,0:T(8,128)(2,1)S(1)}, bf16[2048,256]{1,0:T(8,128)(2,1)S(1)}, bf16[2048,128]{1,0:T(8,128)(2,1)S(1)}, f32[2048,256]{1,0:T(8,128)S(1)}) custom-call(f32[2048,384]{1,0:T(8,128)} %fusion.4.q_ref.kv_ref, f32[2048,384]{1,0:T(8,128)} %fusion.4.q_ref.kv_ref, f32[1024,128]{1,0:T(8,128)S(1)} %copy.31.cos_ref, f32[1024,128]{1,0:T(8,128)S(1)} %copy.32.sin_ref), custom_call_target="tpu_custom_call" | custom-call | flops 4294967296 | bytes 6291456 | tf_op jit(solution)/shard_map/attend/pallas_call | solution.py:890
  158.5 7.0 %collective-permute-done.far_ref = bf16[2,256,2048]{2,1,0:T(8,128)(2,1)} collective-permute-done((bf16[2,256,2048]{2,1,0:T(8,128)(2,1)S(1)}, bf16[2,256,2048]{2,1,0:T(8,128)(2,1)}, u32[]{:S(2)}, u32[]{:S(2)}) %collective-permute-start) | collective-permute-done | bytes 2097184 | tf_op jit(solution)/shard_map/ppermute | solution.py:1242
  165.5 43.8 %product_scatter.2 = f32[256,2048]{1,0:T(8,128)} custom-call(bf16[2048,256]{1,0:T(8,128)(2,1)} %copy-done.7, bf16[2048,640]{1,0:T(8,128)(2,1)} %all-gather.4.cloned.1.call-done.right), custom_call_target="tpu_custom_call" | custom-call | bytes 1024 | tf_op jit(solution)/shard_map/product_scatter/pallas_call | solution.py:641
  213.9 39.3 %plane_gather.4.in_ref.refs_0_ = bf16[2048,2048]{1,0:T(8,128)(2,1)} custom-call(bf16[256,2048]{1,0:T(8,128)(2,1)} %multiply_convert_fusion.block_ref), custom_call_target="tpu_custom_call" | custom-call | bytes 1024 | tf_op jit(solution)/shard_map/plane_gather/pallas_call | solution.py:431
  253.2 3.1 lay.1
  256.3 3.2 copy-done.2
  259.5 25.1 %ffn.1 = (bf16[2048,1024]{1,0:T(8,128)(2,1)}, bf16[2048,1024]{1,0:T(8,128)(2,1)}, bf16[2048,1024]{1,0:T(8,128)(2,1)}) custom-call(bf16[2048,2048]{1,0:T(8,128)(2,1)} %plane_gather.4.in_ref.refs_0_, bf16[2048,2048]{1,0:T(8,128)(2,1)} %all-gather.6.cloned.1.call-done.w_ref.right_ref), custom_call_target="tpu_custom_call" | custom-call | bytes 1024 | tf_op jit(solution)/shard_map/ffn/pallas_call | solution.py:805
  284.7 14.0 %convolution_convert_fusion.1 = bf16[2048,1024]{1,0:T(8,128)(2,1)} fusion(bf16[2048,2048]{1,0:T(8,128)(2,1)} %bitcast.43, bf16[2048,1024]{1,0:T(8,128)(2,1)} %get-tuple-element.61.left_ref), kind=kOutput, calls=%fused_computation.11 | convolution fusion | flops 8592031744 | bytes 16777216 | tf_op jit(solution)/shard_map/dot_general | solution.py:55
  298.8 13.3 %all-gather.8.cloned.1.call-done.down_ref.right_ref = bf16[2048,1024]{1,0:T(8,128)(2,1)} async-done(((bf16[512,1024]{1,0:T(8,128)(2,1)}), bf16[2048,1024]{1,0:T(8,128)(2,1)}) %all-gather.8.cloned.1.call-update) | async-done | bytes 4194320 | tf_op jit(solution)/shard_map/all_gather | solution.py:1415
  312.1 55.0 %ffn_back.1 = (f32[256,2048]{1,0:T(8,128)}, bf16[2048,1024]{1,0:T(8,128)(2,1)}, bf16[2048,1024]{1,0:T(8,128)(2,1)}) custom-call(bf16[2,256,2048]{2,1,0:T(8,128)(2,1)} %own_ref.3, bf16[2,256,2048]{2,1,0:T(8,128)(2,1)} %collective-permute-done.far_ref, bf16[2,256,2048]{2,1,0:T(8,128)(2,1)} %collective-permute-done.1.twin_ref, ...), custom_call_target="tpu_custom_call" | custom-call | bytes 1024 | tf_op jit(solution)/shard_map/ffn_back/pallas_call | solution.py:759
  367.1 14.0 %convolution_convert_fusion = bf16[2048,1024]{1,0:T(8,128)(2,1)} fusion(bf16[2048,2048]{1,0:T(8,128)(2,1)} %plane_gather.4.in_ref.refs_0_, bf16[2048,1024]{1,0:T(8,128)(2,1)} %get-tuple-element.65), kind=kOutput, calls=%fused_computation.10 | convolution fusion | flops 8592031744 | bytes 16777216 | tf_op jit(solution)/shard_map/dot_general | solution.py:55
  382.7 2.3 multiply_reduce_fusion
  385.6 2.4 fusion.18
  388.0 45.7 %plane_gather.5 = (bf16[2048,2048]{1,0:T(8,128)(2,1)}, bf16[2048,1024]{1,0:T(8,128)(2,1)}) custom-call(bf16[256,2048]{1,0:T(8,128)(2,1)} %get-tuple-element.66.block_ref, bf16[2048,2048]{1,0:T(8,128)(2,1)} %plane_gather.4.in_ref.refs_0_, bf16[2048,1024]{1,0:T(8,128)(2,1)} %get-tuple-element.67.refs_1_), custom_call_target="tpu_custom_call" | custom-call | bytes 1024 | tf_op jit(solution)/shard_map/plane_gather/pallas_call | solution.py:431
  433.8 7.1 %convolution_convert_fusion.4.up_ref = bf16[2048,256]{1,0:T(8,128)(2,1)} fusion(bf16[2048,2048]{1,0:T(8,128)(2,1)} %get-tuple-element.68, bf16[2048,640]{1,0:T(8,128)(2,1)} %all-gather.4.cloned.1.call-done.right), kind=kOutput, calls=%fused_computation.15 | convolution fusion | flops 2148007936 | bytes 10485760 | tf_op jit(solution)/shard_map/dot_general | solution.py:1443
  440.9 2.7 convolution_convert_fusion.3
  443.6 60.8 %attend_back.1 = (bf16[2048,384]{1,0:T(8,128)(2,1)}, bf16[256,2048]{1,0:T(8,128)(2,1)}, bf16[4096,128]{1,0:T(8,128)(2,1)}) custom-call(bf16[2048,256]{1,0:T(8,128)(2,1)} %copy-done.6, bf16[2048,128]{1,0:T(8,128)(2,1)} %copy-done.9, bf16[2048,256]{1,0:T(8,128)(2,1)} %convolution_convert_fusion.4.up_ref, f32[2048,256]{1,0:T(8,128)} %copy-done.3, ...), custom_call_target="tpu_custom_call" | custom-call | bytes 1024 | tf_op jit(solution)/shard_map/attend_back/pallas_call | solution.py:1049
  504.5 8.9 %convolution_convert_fusion.2 = bf16[2048,384]{1,0:T(8,128)(2,1)S(1)} fusion(bf16[2048,384]{1,0:T(8,128)(2,1)} %get-tuple-element.72.left, bf16[2048,2048]{1,0:T(8,128)(2,1)} %get-tuple-element.50, f32[2048]{0:T(1024)S(1)} %bitcast.59, f32[2048]{0:T(1024)S(1)} %add_rsqrt_fusion), kind=kOutput, calls=%fused_computation.12 | convolution fusion | flops 3238789120 | bytes 11550720 | tf_op jit(solution)/shard_map/dot_general | solution.py:55
  517.6 60.1 %product_scatter.3 = (f32[256,2048]{1,0:T(8,128)}, bf16[128,4096]{1,0:T(8,128)(2,1)}) custom-call(bf16[2048,384]{1,0:T(8,128)(2,1)} %get-tuple-element.72.left, bf16[2048,640]{1,0:T(8,128)(2,1)} %all-gather.4.cloned.1.call-done.right, bf16[512,1024]{1,0:T(8,128)(2,1)} %reduce-scatter.7.cloned.1.call-done.refs_0_), custom_call_target="tpu_custom_call" | custom-call | bytes 1024 | tf_op jit(solution)/shard_map/product_scatter/pallas_call | solution.py:641
  581.9 2.8 convert_element_type.113
  586.7 19.6 %gain_sum.1 = (f32[2,128]{1,0:T(2,128)}, bf16[128,4096]{1,0:T(8,128)(2,1)}) custom-call(f32[2,2048]{1,0:T(2,128)} %pad_maximum_fusion.3.terms_ref, bf16[512,1024]{1,0:T(8,128)(2,1)} %reduce-scatter.9.cloned.1.call-done.up_ref), custom_call_target="tpu_custom_call" | custom-call | bytes 1024 | tf_op jit(solution)/shard_map/gain_sum/pallas_call | solution.py:1149
  606.3 2.8 convert_element_type.114
  609.6 3.2 maximum_select_fusion
  612.8 4.0 fusion.14
  616.8 10.8 %last_swap.1 = (bf16[128,1024]{1,0:T(8,128)(2,1)}, bf16[128,256]{1,0:T(8,128)(2,1)}, bf16[128,256]{1,0:T(8,128)(2,1)}, bf16[1024,128]{1,0:T(8,128)(2,1)}) custom-call(bf16[512,640]{1,0:T(8,128)(2,1)} %reduce-scatter.11.cloned.1.call-done.attn_ref), custom_call_target="tpu_custom_call" | custom-call | bytes 1024 | tf_op jit(solution)/shard_map/last_swap/pallas_call | solution.py:1200
  (114 shorter events, 43.4 us)
Async XLA Ops:
  7.2 116.1 %all-gather.4.cloned.1.call-start = ((), (), s32[]{:S(2)}) async-start(), calls=%async_computation.5 | async-start | bytes 3276800 | tf_op jit(solution)/shard_map/all_gather | solution.py:1399
  24.2 235.4 %all-gather.6.cloned.1.call-start = ((), (), s32[]{:S(2)}) async-start(), calls=%async_computation.6 | async-start | bytes 10485760 | tf_op jit(solution)/shard_map/all_gather | solution.py:1413
  49.7 1.6 copy-start.20
  49.7 2.9 copy-start.22
  49.8 2.8 copy-start.23
  49.8 49.1 %copy-start.19 = (bf16[4096,128]{1,0:T(8,128)(2,1)S(1)}, bf16[4096,128]{1,0:T(8,128)(2,1)}, u32[]{:S(2)}) copy-start(bf16[4096,128]{1,0:T(8,128)(2,1)} %param.20) | copy-start | bytes 3145732
  98.9 4.9 copy-start
  100.2 18.0 %all-to-all-start = ((bf16[128,4,1024]{2,0,1:T(8,128)(2,1)}), bf16[128,4,1024]{2,0,1:T(8,128)(2,1)S(1)}, u32[]{:S(2)}, u32[]{:S(2)}) async-start(bf16[128,4,1024]{2,0,1:T(8,128)(2,1)} %copy.30), calls=%async_computation | async-start | bytes 2097152 | tf_op jit(solution)/shard_map/all_to_all | solution.py:1360
  103.7 208.4 %all-gather.8.cloned.1.call-start = ((), (), s32[]{:S(2)}) async-start(), calls=%async_computation.7 | async-start | bytes 5242880 | tf_op jit(solution)/shard_map/all_gather | solution.py:1415
  103.8 149.4 %collective-permute-start.1 = (bf16[2,256,2048]{2,1,0:T(8,128)(2,1)S(1)}, bf16[2,256,2048]{2,1,0:T(8,128)(2,1)}, u32[]{:S(2)}, u32[]{:S(2)}) collective-permute-start(bf16[2,256,2048]{2,1,0:T(8,128)(2,1)S(1)} %copy-done), channel_id=1, source_target_pairs={{0,2},{2,0},{4,6},{6,4},{1,3},{3,1},{5,7},{7,5},{8,10},{10,8},{12,... | collective-permute-start | bytes 6291464 | tf_op jit(solution)/shard_map/ppermute | solution.py:1244
  118.1 47.4 %collective-permute-start = (bf16[2,256,2048]{2,1,0:T(8,128)(2,1)S(1)}, bf16[2,256,2048]{2,1,0:T(8,128)(2,1)}, u32[]{:S(2)}, u32[]{:S(2)}) collective-permute-start(bf16[2,256,2048]{2,1,0:T(8,128)(2,1)S(1)} %copy-done), channel_id=1, source_target_pairs={{0,4},{2,6},{4,0},{6,2},{1,5},{3,7},{5,1},{7,3},{8,12},{10,14},{12... | collective-permute-start | bytes 6291464 | tf_op jit(solution)/shard_map/ppermute | solution.py:1242
  119.2 324.5 %reduce-scatter.5.cloned.1.call-start = ((), (), s32[]{:S(2)}) async-start(), calls=%async_computation.8 | async-start | bytes 5242880 | tf_op jit(solution)/shard_map/reduce_scatter | solution.py:1431
  120.0 13.4 %copy-start.4 = (f32[1024,128]{1,0:T(8,128)}, f32[1024,128]{1,0:T(8,128)S(1)}, u32[]{:S(2)}) copy-start(f32[1024,128]{1,0:T(8,128)S(1)} %copy.32.sin_ref) | copy-start | bytes 1572868
  122.2 11.2 %copy-start.5 = (f32[1024,128]{1,0:T(8,128)}, f32[1024,128]{1,0:T(8,128)S(1)}, u32[]{:S(2)}) copy-start(f32[1024,128]{1,0:T(8,128)S(1)} %copy.31.cos_ref) | copy-start | bytes 1572868
  154.5 1.3 copy-start.3
  165.5 43.8 %copy-start.12 = (bf16[256,2048]{1,0:T(8,128)(2,1)S(1)}, bf16[256,2048]{1,0:T(8,128)(2,1)}, u32[]{:S(2)}) copy-start(bf16[256,2048]{1,0:T(8,128)(2,1)} %get-tuple-element.49.block_ref) | copy-start | bytes 3145732
  165.5 87.7 %collective-permute-start.2 = (bf16[2,256,2048]{2,1,0:T(8,128)(2,1)}, bf16[2,256,2048]{2,1,0:T(8,128)(2,1)}, u32[]{:S(2)}, u32[]{:S(2)}) collective-permute-start(bf16[2,256,2048]{2,1,0:T(8,128)(2,1)} %collective-permute-done.far_ref), channel_id=1, source_target_pairs={{0,2},{2,0},{4,6},{6,4},{1,3},{3,1},{5,7},{7,5},{8,10},{10,8},{12,... | collective-permute-start | bytes 6291464 | tf_op jit(solution)/shard_map/ppermute | solution.py:1244
  256.3 3.2 copy-start.2
  298.7 218.8 %reduce-scatter.7.cloned.1.call-start = ((), (), s32[]{:S(2)}) async-start(), calls=%async_computation.9 | async-start | bytes 5242880 | tf_op jit(solution)/shard_map/reduce_scatter | solution.py:1436
  381.1 1.6 copy-start.11
  381.1 205.6 %reduce-scatter.9.cloned.1.call-start = ((), (), s32[]{:S(2)}) async-start(), calls=%async_computation.10 | async-start | bytes 5242880 | tf_op jit(solution)/shard_map/reduce_scatter | solution.py:1442
  382.7 2.3 copy-start.1
  382.7 2.9 copy-start.15
  433.7 183.0 %reduce-scatter.11.cloned.1.call-start = ((), (), s32[]{:S(2)}) async-start(), calls=%async_computation.11 | async-start | bytes 3276800 | tf_op jit(solution)/shard_map/reduce_scatter | solution.py:1462
  433.8 7.1 %copy-start.8 = (bf16[2048,256]{1,0:T(8,128)(2,1)S(1)}, bf16[2048,256]{1,0:T(8,128)(2,1)}, u32[]{:S(2)}) copy-start(bf16[2048,256]{1,0:T(8,128)(2,1)} %copy-done.7) | copy-start | bytes 3145732
  433.8 7.1 %copy-start.24 = (bf16[2048,2048]{1,0:T(8,128)(2,1)S(1)}, bf16[2048,2048]{1,0:T(8,128)(2,1)}, u32[]{:S(2)}) copy-start(bf16[2048,2048]{1,0:T(8,128)(2,1)} %get-tuple-element.68) | copy-start | bytes 25165828
  516.4 70.3 %collective-permute-start.3 = (bf16[256,2048]{1,0:T(8,128)(2,1)S(1)}, bf16[256,2048]{1,0:T(8,128)(2,1)}, u32[]{:S(2)}, u32[]{:S(2)}) collective-permute-start(bf16[256,2048]{1,0:T(8,128)(2,1)S(1)} %copy-done.17), channel_id=1, source_target_pairs={{0,1},{1,0},{2,3},{3,2},{4,5},{5,4},{6,7},{7,6},{8,9},{9,8},{10,11... | collective-permute-start | bytes 3145736 | tf_op jit(solution)/shard_map/ppermute | solution.py:1364
  517.6 62.4 %copy-start.14 = (f32[256,2048]{1,0:T(8,128)S(1)}, f32[256,2048]{1,0:T(8,128)}, u32[]{:S(2)}) copy-start(f32[256,2048]{1,0:T(8,128)} %get-tuple-element.93) | copy-start | bytes 6291460
  577.7 2.3 copy-start.13
  580.7 4.0 copy-start.18
  580.7 25.6 %collective-permute-start.4 = (bf16[256,2048]{1,0:T(8,128)(2,1)S(1)}, bf16[256,2048]{1,0:T(8,128)(2,1)}, u32[]{:S(2)}, u32[]{:S(2)}) collective-permute-start(bf16[256,2048]{1,0:T(8,128)(2,1)S(1)} %fusion.10), channel_id=1, source_target_pairs={{0,1},{1,0},{2,3},{3,2},{4,5},{5,4},{6,7},{7,6},{8,9},{9,8},{10,11... | collective-permute-start | bytes 3145736 | tf_op jit(solution)/shard_map/ppermute | solution.py:1364
  606.3 2.8 copy-start.21
  (6 other events, 6.3 us)
Sparse Core Ops, SparseCore 0:
  24.3 57.2 all-gather.3
  83.2 148.2 all-gather.5
  233.1 78.9 all-gather.7
  314.2 75.2 reduce-scatter.4
  391.8 77.2 reduce-scatter.6
  471.3 77.2 reduce-scatter.8
  551.0 52.6 reduce-scatter.10

commit v4 on v3

--- a/solution.py
+++ b/solution.py
@@ -467,6 +467,26 @@
     return away, pltpu.make_async_copy(block(here), out_ref.at[here], local_sem)
 
 
+def norm_back(rows, grad_ref, value_ref, factor_ref, gain_ref, base_ref, out_ref, low_ref, term_ref):
+    tile = 32
+    gain = gain_ref[...]
+
+    def step(index, total):
+        here = pl.ds(pl.multiple_of(index * tile, tile), tile)
+        grad, value, factor = grad_ref[here, :], value_ref[here, :], factor_ref[here, :]
+        scaled = grad * gain
+        inner = jnp.mean(scaled * value, axis=1, keepdims=True)
+        back = factor * scaled - value * (factor * factor * factor) * inner
+        result = base_ref[here, :].astype(F32) + back
+        if out_ref is not None:
+            out_ref[here, :] = result
+        low_ref[here, :] = result.astype(BF16)
+        return total + jnp.sum(grad * value * factor, axis=0, keepdims=True)
+
+    total = lax.fori_loop(0, rows // tile, step, jnp.zeros((1, gain.shape[1]), F32))
+    term_ref[...] = jnp.broadcast_to(total, term_ref.shape)
+
+
 def scatter_steps(rows, left_of, right_of, out_ref, scratch, swap=None, late=None):
     made, other, to_side, to_row, from_side, from_row = scratch[:6]
     on_side, on_row, got_side, got_row, send_sems, recv_sems = scratch[6:]
@@ -602,7 +622,8 @@
 def scatter_kernel(rows, swaps, columns, left, right, *refs):
     swap, late = None, None
     if swaps:
-        in_ref, out_ref, laid_ref, *scratch = refs
+        in_ref, value_ref, factor_ref, gain_ref, base_ref, low_ref, term_ref, laid_ref = refs[:8]
+        out_ref, *scratch = refs[8:]
         swapped = scratch[-4]
         swap = (in_ref, swapped, *scratch[-3:])
         scratch = scratch[:-4]
@@ -623,27 +644,38 @@
 
     for step in scatter_steps(rows, left_of, right_of, out_ref, scratch, swap=swap, late=late):
         step()
-
-
-def product_scatter(number, left, right, start, size, swap=None):
+    if swaps:
+        norm_back(
+            rows, out_ref, value_ref, factor_ref, gain_ref, base_ref, None, low_ref, term_ref
+        )
+
+
+def product_scatter(number, left, right, start, size, swap=None, norm=()):
     total = left.shape[0]
     width = right.shape[0]
     rows = total // 8
     vmem = pl.BlockSpec(memory_space=pltpu.VMEM)
-    shapes, ins, scratch = [jax.ShapeDtypeStruct((rows, width), F32)], [vmem, vmem], []
-    operands = [left, right]
-    if swap is not None:
+    if swap is None:
+        shapes, ins, scratch = [jax.ShapeDtypeStruct((rows, width), F32)], [vmem, vmem], []
+        operands = [left, right]
+    else:
         deep = swap.shape[0] // 4
-        shapes.append(jax.ShapeDtypeStruct((deep, 4 * swap.shape[1]), swap.dtype))
-        ins.append(pl.BlockSpec(memory_space=pl.ANY))
-        operands.append(swap)
+        shapes = [
+            jax.ShapeDtypeStruct((rows, width), BF16),
+            jax.ShapeDtypeStruct((8, width), F32),
+            jax.ShapeDtypeStruct((deep, 4 * swap.shape[1]), swap.dtype),
+        ]
+        ins = [vmem, vmem, pl.BlockSpec(memory_space=pl.ANY)] + [vmem] * 4
+        operands = [left, right, swap, *norm]
         scratch = [pltpu.VMEM((4, deep, swap.shape[1]), swap.dtype)] + swap_scratch()
     return pl.pallas_call(
         functools.partial(scatter_kernel, rows, swap is not None, slice(start, start + size)),
         out_shape=tuple(shapes),
         in_specs=ins,
         out_specs=tuple([vmem] * len(shapes)),
-        scratch_shapes=scatter_scratch(rows, width) + scratch,
+        scratch_shapes=([pltpu.VMEM((rows, width), F32)] if swap is not None else [])
+        + scatter_scratch(rows, width)
+        + scratch,
         compiler_params=pltpu.CompilerParams(
             collective_id=number, has_side_effects=True, vmem_limit_bytes=56 * 1024 * 1024
         ),
@@ -662,9 +694,16 @@
     up_slope_ref,
     down_ref,
     right_ref,
-    out_ref,
+    value_ref,
+    factor_ref,
+    gain_ref,
+    base_ref,
+    result_ref,
+    low_ref,
+    term_ref,
     gate_ref,
     up_ref,
+    out_ref,
     cots,
     gate_slopes,
     up_slopes,
@@ -746,11 +785,14 @@
 
     for step in scatter_steps(rows, left_of, right_of, out_ref, scratch):
         step()
+    norm_back(
+        rows, out_ref, value_ref, factor_ref, gain_ref, base_ref, result_ref, low_ref, term_ref
+    )
     wait(store(2))
     wait(store(3))
 
 
-def ffn_back(number, cots, gate_slope, up_slope, down_w, gate_up):
+def ffn_back(number, cots, gate_slope, up_slope, down_w, gate_up, norm):
     total, units = gate_slope.shape
     width = down_w.shape[0]
     rows = total // 8
@@ -760,12 +802,15 @@
         functools.partial(ffn_back_kernel, rows),
         out_shape=(
             jax.ShapeDtypeStruct((rows, width), F32),
+            jax.ShapeDtypeStruct((rows, width), BF16),
+            jax.ShapeDtypeStruct((8, width), F32),
             jax.ShapeDtypeStruct((total, units), BF16),
             jax.ShapeDtypeStruct((total, units), BF16),
         ),
-        in_specs=[anywhere] * 6 + [vmem, vmem],
-        out_specs=(vmem, anywhere, anywhere),
+        in_specs=[anywhere] * 6 + [vmem] * 6,
+        out_specs=(vmem, vmem, vmem, anywhere, anywhere),
         scratch_shapes=[
+            pltpu.VMEM((rows, width), F32),
             pltpu.VMEM((2, 2, rows, width), BF16),
             pltpu.VMEM((2, 2 * rows, units), BF16),
             pltpu.VMEM((2, 2 * rows, units), BF16),
@@ -779,7 +824,7 @@
         ),
         cost_estimate=pl.CostEstimate(flops=0, bytes_accessed=1024, transcendentals=0),
         name="ffn_back",
-    )(*cots, gate_slope, up_slope, down_w, gate_up)
+    )(*cots, gate_slope, up_slope, down_w, gate_up, *norm)
 
 
 def ffn_kernel(in_ref, w_ref, product_ref, gate_slope_ref, up_slope_ref):
@@ -1214,6 +1259,46 @@
     )(attn_sum)
 
 
+def final_kernel(own_ref, other_ref, in_ref, in_other_ref, *refs):
+    first = lax.axis_index("tensor") == 0
+    sources, (out_ref, in_out_ref, *targets) = refs[:7], refs[7:]
+    own, other = own_ref[...], other_ref[...]
+    out_ref[0], out_ref[1] = jnp.where(first, own, other), jnp.where(first, other, own)
+    own, other = in_ref[...].astype(F32), in_other_ref[...].astype(F32)
+    in_out_ref[0], in_out_ref[1] = jnp.where(first, own, other), jnp.where(first, other, own)
+    for source, target in zip(sources, targets):
+        target[...] = source[...].astype(F32)
+
+
+def final_forms(out_own, out_other, in_own, in_other, *grads):
+    steps = 8
+    rows, width = out_own.shape
+    halves = pl.BlockSpec((rows // steps, width), lambda i: (i, 0))
+    whole = pl.BlockSpec((2, rows // steps, width), lambda i: (0, i, 0))
+
+    def block_of(grad):
+        deep, wide = grad.shape
+        if wide // steps % 128 == 0:
+            return pl.BlockSpec((deep, wide // steps), lambda i: (0, i))
+        return pl.BlockSpec((deep // steps, wide), lambda i: (i, 0))
+
+    blocks = [block_of(grad) for grad in grads]
+    return pl.pallas_call(
+        final_kernel,
+        grid=(steps,),
+        out_shape=(
+            jax.ShapeDtypeStruct((2, rows, width), BF16),
+            jax.ShapeDtypeStruct((2, rows, width), F32),
+        )
+        + tuple(jax.ShapeDtypeStruct(grad.shape, F32) for grad in grads),
+        in_specs=[halves] * 4 + blocks,
+        out_specs=(whole, whole, *blocks),
+        compiler_params=pltpu.CompilerParams(vmem_limit_bytes=60 * 1024 * 1024),
+        cost_estimate=pl.CostEstimate(flops=0, bytes_accessed=1024, transcendentals=0),
+        name="final_forms",
+    )(out_own, out_other, in_own, in_other, *grads)
+
+
 def lay_kernel(own_ref, far_ref, twin_ref, twin_far_ref, all_ref, sems):
     ctx = lax.axis_index("ctx")
     row, core = ctx // 2, ctx % 2
@@ -1254,102 +1339,178 @@
     return whole.reshape(seqs * 4 * span, width), (block, far, twin, twin_far)
 
 
-def deal_kernel(q_ref, kv_ref, out_ref, all_ref, send_sems, recv_sems, local_sems):
+def open_kernel(
+    planes,
+    q_ref,
+    kv_ref,
+    wide_ref,
+    gate_ref,
+    up_ref,
+    down_ref,
+    attn_ref,
+    gate_up_ref,
+    down_own_ref,
+    send_sems,
+    recv_sems,
+    local_sems,
+    line_send,
+    line_recv,
+):
     _, row, core, *_ = place()
+    plane = lax.axis_index("dp")
     here = row * 2 + core
+    rows, units = q_ref.shape[0], gate_ref.shape[1] // 4
     peers = (row * 2 + 1 - core, (1 - row) * 2 + core, (1 - row) * 2 + 1 - core)
-    greet([{"ctx": peer} for peer in peers])
-    copies = []
+    ahead, behind = {"dp": (plane + 1) % planes}, {"dp": (plane + planes - 1) % planes}
+    barrier = pltpu.get_barrier_semaphore()
+    more, fewer = plane + 1 < planes, plane > 0
+    for peer in peers:
+        pl.semaphore_signal(barrier, inc=1, device_id={"ctx": peer}, device_id_type=MESH_ID)
+
+    @pl.when(more)
+    def _():
+        pl.semaphore_signal(barrier, inc=1, device_id=ahead, device_id_type=MESH_ID)
+
+    @pl.when(fewer)
+    def _():
+        pl.semaphore_signal(barrier, inc=1, device_id=behind, device_id_type=MESH_ID)
+
+    pl.semaphore_wait(barrier, 3 + more.astype(jnp.int32) + fewer.astype(jnp.int32))
+
+    mine = pl.multiple_of(here * rows, rows)
+    base = pl.multiple_of(plane * 4 * rows, 4 * rows)
+    moves = []
     start = 0
-    for which, source in enumerate((q_ref, kv_ref, out_ref)):
+    for source in (q_ref, kv_ref, wide_ref):
         cols = source.shape[1] // 4
-        target = all_ref.at[here, :, pl.ds(start, cols)]
+        moves.append((source, cols, attn_ref.at[pl.ds(base + mine, rows), pl.ds(start, cols)]))
         start += cols
-        for at, peer in enumerate(peers):
-            copies.append(
+    for which, source in enumerate((gate_ref, up_ref)):
+        lanes = pl.ds(which * units, units)
+        moves.append((source, units, gate_up_ref.at[pl.ds(mine, rows), lanes]))
+    moves.append((down_ref, units, down_own_ref.at[pl.ds(mine, rows)]))
+    away, local = [], []
+    for which, (source, cols, target) in enumerate(moves):
+
+        def columns(index, source=source, cols=cols):
+            return source.at[:, pl.ds(pl.multiple_of(index * cols, cols), cols)]
+
+        away.append(
+            [
                 remote(
-                    source.at[:, pl.ds(pl.multiple_of(peer * cols, cols), cols)],
+                    columns(peer),
                     target,
                     send_sems.at[which, at],
                     recv_sems.at[which, at],
                     {"ctx": peer},
                 )
-            )
-        own = source.at[:, pl.ds(pl.multiple_of(here * cols, cols), cols)]
-        copies.append(pltpu.make_async_copy(own, target, local_sems.at[which]))
-    for copy in copies:
-        copy.start()
-    for copy in copies:
-        copy.wait()
-
-
-def deal(query, keyval, out):
+                for at, peer in enumerate(peers)
+            ]
+        )
+        local.append(pltpu.make_async_copy(columns(here), target, local_sems.at[which]))
+    for which in range(3):
+        away[which][0].start()
+        local[which].start()
+    for at in (1, 2):
+        for which in range(3):
+            away[which][at].start()
+    for which in range(3, 6):
+        for copy in away[which]:
+            copy.start()
+        local[which].start()
+
+    def hop(way, far, part):
+        whose = plane - far if way == 0 else plane + far
+        half = row if part == 0 else 1 - row
+        spot = attn_ref.at[
+            pl.ds(pl.multiple_of((whose * 4 + half * 2) * rows, 2 * rows), 2 * rows)
+        ]
+        return remote(
+            spot,
+            spot,
+            line_send.at[way, far, part],
+            line_recv.at[way, far, part],
+            ahead if way == 0 else behind,
+        )
+
+    def sends(way, far):
+        if way == 0:
+            return (plane - far >= 0) & more
+        return (plane + far < planes) & fewer
+
+    def gets(way, far):
+        return plane - 1 - far >= 0 if way == 0 else plane + 1 + far < planes
+
+    def hop_start(way, far, part):
+        @pl.when(sends(way, far))
+        def _():
+            hop(way, far, part).start()
+
+    for which in range(3):
+        local[which].wait()
+        away[which][0].wait_recv()
+    for way in range(2):
+        hop_start(way, 0, 0)
+    for which in range(3):
+        away[which][1].wait_recv()
+        away[which][2].wait_recv()
+    for way in range(2):
+        hop_start(way, 0, 1)
+    for far in range(planes - 1):
+        for part in range(2):
+            for way in range(2):
+
+                @pl.when(gets(way, far))
+                def _(way=way, far=far, part=part):
+                    hop(way, far, part).wait_recv()
+
+                if far + 1 < planes - 1:
+                    hop_start(way, far + 1, part)
+    for far in range(planes - 1):
+        for part in range(2):
+            for way in range(2):
+
+                @pl.when(sends(way, far))
+                def _(way=way, far=far, part=part):
+                    hop(way, far, part).wait_send()
+
+    for which in range(6):
+        if which > 2:
+            local[which].wait()
+            for copy in away[which]:
+                copy.wait_recv()
+        for copy in away[which]:
+            copy.wait_send()
+
+
+def open_weights(query, keyval, wide, gate, up, down):
+    planes = lax.axis_size("dp")
     rows = query.shape[0]
-    cols = (query.shape[1] + keyval.shape[1] + out.shape[1]) // 4
+    cols = (query.shape[1] + keyval.shape[1] + wide.shape[1]) // 4
+    units = gate.shape[1] // 4
+    anywhere, vmem = pl.BlockSpec(memory_space=pl.ANY), pl.BlockSpec(memory_space=pltpu.VMEM)
     return pl.pallas_call(
-        deal_kernel,
-        out_shape=jax.ShapeDtypeStruct((4, rows, cols), BF16),
-        in_specs=[pl.BlockSpec(memory_space=pl.ANY)] * 3,
-        out_specs=pl.BlockSpec(memory_space=pltpu.VMEM),
+        functools.partial(open_kernel, planes),
+        out_shape=(
+            jax.ShapeDtypeStruct((planes * 4 * rows, cols), BF16),
+            jax.ShapeDtypeStruct((4 * rows, 2 * units), BF16),
+            jax.ShapeDtypeStruct((4 * rows, units), BF16),
+        ),
+        in_specs=[anywhere] * 6,
+        out_specs=(vmem, anywhere, anywhere),
         scratch_shapes=[
-            pltpu.SemaphoreType.DMA((3, 3)),
-            pltpu.SemaphoreType.DMA((3, 3)),
-            pltpu.SemaphoreType.DMA((3,)),
-        ],
-        compiler_params=pltpu.CompilerParams(collective_id=6, has_side_effects=True),
-        cost_estimate=pl.CostEstimate(flops=0, bytes_accessed=1024, transcendentals=0),
-        name="deal",
-    )(query, keyval, out)
-
-
-def share_kernel(gate_ref, up_ref, all_ref, send_sems, recv_sems, local_sems):
-    _, row, core, *_ = place()
-    here = row * 2 + core
-    rows, units = gate_ref.shape[0], all_ref.shape[1] // 2
-    peers = (row * 2 + 1 - core, (1 - row) * 2 + core, (1 - row) * 2 + 1 - core)
-    greet([{"ctx": peer} for peer in peers])
-    copies = []
-    for which, source in enumerate((gate_ref, up_ref)):
-        target = all_ref.at[
-            pl.ds(pl.multiple_of(here * rows, rows), rows), pl.ds(which * units, units)
-        ]
-        for at, peer in enumerate(peers):
-            copies.append(
-                remote(
-                    source.at[:, pl.ds(pl.multiple_of(peer * units, units), units)],
-                    target,
-                    send_sems.at[which, at],
-                    recv_sems.at[which, at],
-                    {"ctx": peer},
-                )
-            )
-        own = source.at[:, pl.ds(pl.multiple_of(here * units, units), units)]
-        copies.append(pltpu.make_async_copy(own, target, local_sems.at[which]))
-    for copy in copies:
-        copy.start()
-    for copy in copies:
-        copy.wait()
-
-
-def share(gate, up):
-    parts = lax.axis_size("ctx")
-    anywhere = pl.BlockSpec(memory_space=pl.ANY)
-    return pl.pallas_call(
-        share_kernel,
-        out_shape=jax.ShapeDtypeStruct((parts * gate.shape[0], 2 * gate.shape[1] // parts), BF16),
-        in_specs=[anywhere, anywhere],
-        out_specs=anywhere,
-        scratch_shapes=[
-            pltpu.SemaphoreType.DMA((2, 3)),
-            pltpu.SemaphoreType.DMA((2, 3)),
-            pltpu.SemaphoreType.DMA((2,)),
+            pltpu.SemaphoreType.DMA((6, 3)),
+            pltpu.SemaphoreType.DMA((6, 3)),
+            pltpu.SemaphoreType.DMA((6,)),
+            pltpu.SemaphoreType.DMA((2, planes - 1, 2)),
+            pltpu.SemaphoreType.DMA((2, planes - 1, 2)),
         ],
         compiler_params=pltpu.CompilerParams(
-            collective_id=8, has_side_effects=True, vmem_limit_bytes=60 * 1024 * 1024
+            collective_id=6, has_side_effects=True, vmem_limit_bytes=60 * 1024 * 1024
         ),
         cost_estimate=pl.CostEstimate(flops=0, bytes_accessed=1024, transcendentals=0),
-        name="share",
-    )(gate, up)
+        name="open_weights",
+    )(query, keyval, wide, gate, up, down)
 
 
 def after(value, *earlier):
@@ -1394,29 +1555,26 @@
     keyval = jnp.concatenate(
         [w_key.reshape(rows_w, parts, kv_cols), w_value.reshape(rows_w, parts, kv_cols)], axis=2
     ).reshape(rows_w, -1)
-    mixed = deal(w_query, keyval, w_out.T)
-    ready_w = mixed
-    attn_w = lax.all_gather(mixed.reshape(parts * rows_w, -1), "dp", axis=0, tiled=True)
+    attn_w, gate_up, down_own = open_weights(
+        w_query, keyval, w_out.T, w_gate, w_up, w_down.T
+    )
     qkv_cols = q_cols + 2 * kv_cols
     w_qkv = attn_w[:, :qkv_cols]
     w_out_t = attn_w[:, qkv_cols:]
-
-    gate_up = share(after(w_gate, ready_w), w_up)
     own_in = lax.dynamic_index_in_dim(layer_input, side, 0, keepdims=False)
     own_cot = lax.dynamic_index_in_dim(cotangent, side, 0, keepdims=False)
     gains = jnp.concatenate(
         [attn_gain[None], ffn_gain[None], jnp.zeros((6, rows_w), BF16)]
     ).astype(F32)
-    all_in, gains = plane_gather(after(own_in, ready_w), 10, gains=gains)
+    all_in, gains = plane_gather(after(own_in, gate_up), 10, gains=gains)
     gain_one = gains[:, 0].reshape(width)
     gain_two = gains[:, 1].reshape(width)
     gate_up = lax.all_gather(gate_up, "dp", axis=0, tiled=True)
-    down_own = to_units(after(w_down, all_in).T)
     down_w = lax.all_gather(down_own, "dp", axis=0, tiled=True)
 
     all_f = all_in.astype(F32)
     normed_one = (all_f * rms_factor(all_f) * gain_one).astype(BF16)
-    pre = after(jnp.dot(normed_one, w_qkv, preferred_element_type=F32), down_own)
+    pre = jnp.dot(normed_one, w_qkv, preferred_element_type=F32)
     attended, queries, keyvals, logs = attend(pre, cosine, signed, seqs)
     inputs_f = own_in.astype(F32)
     factor_one = rms_factor(inputs_f)
@@ -1424,21 +1582,23 @@
     factor_two = rms_factor(hidden)
     normed_own = (hidden * factor_two * gain_two).astype(BF16)
     normed_two = plane_gather(normed_own)[0]
-    all_cot, cots = along_ctx(cotangent, down_own, attended)
+    all_cot, cots = along_ctx(cotangent, all_in, hidden)
 
     product, gate_slope, up_slope = ffn(normed_two, gate_up)
     down_grad = matmul_t(all_cot, product).astype(BF16)
     down_sum = lax.psum_scatter(down_grad, "dp", scatter_dimension=0, tiled=True)
-    normed_two_grad, gate_grad, up_grad = ffn_back(
-        3, cots, after(gate_slope, down_grad), up_slope, down_w, gate_up
+    hidden_grad, hidden_own, ffn_term, gate_grad, up_grad = ffn_back(
+        3,
+        cots,
+        after(gate_slope, down_grad),
+        up_slope,
+        down_w,
+        gate_up,
+        (hidden, factor_two, gain_two[None], own_cot),
     )
     gate_w_grad = matmul_t(normed_two, gate_grad).astype(BF16)
     gate_sum = lax.psum_scatter(gate_w_grad, "dp", scatter_dimension=0, tiled=True)
-    hidden_back, ffn_gain_term = rms_back(normed_two_grad, hidden, factor_two, gain_two)
-    hidden_grad = own_cot.astype(F32) + hidden_back
-    hidden_low, up_w_grad = plane_gather(
-        after(hidden_grad.astype(BF16), gate_w_grad), 7, [normed_two, up_grad]
-    )
+    hidden_low, up_w_grad = plane_gather(after(hidden_own, gate_w_grad), 7, [normed_two, up_grad])
     up_sum = lax.psum_scatter(up_w_grad, "dp", scatter_dimension=0, tiled=True)
     attended_grad = jnp.dot(after(hidden_low, up_w_grad), w_out_t, preferred_element_type=F32).astype(BF16)
     out_w_grad = matmul_t(hidden_low, attended).astype(BF16)
@@ -1460,35 +1620,49 @@
     qkv_grad = matmul_t(normed_one, back).astype(BF16)
     attn_grad = jnp.concatenate([qkv_grad, out_w_grad], axis=1)
     attn_sum = lax.psum_scatter(attn_grad, "dp", scatter_dimension=0, tiled=True)
-    normed_one_grad, gate_out = product_scatter(
-        4, after(back, attn_grad), attn_w, 0, qkv_cols, gate_sum
-    )
-    input_back, attn_gain_term = rms_back(normed_one_grad, inputs_f, factor_one, gain_one)
-    input_own = (hidden_grad + input_back).astype(BF16)
+    input_own, attn_term, gate_out = product_scatter(
+        4,
+        after(back, attn_grad),
+        attn_w,
+        0,
+        qkv_cols,
+        gate_sum,
+        (inputs_f, factor_one, gain_one[None], hidden_grad),
+    )
     input_other = swap_sides(input_own)
-    terms = jnp.stack([attn_gain_term, ffn_gain_term])
+    terms = jnp.concatenate([attn_term[:1], ffn_term[:1]])
     gain_own, up_out = gain_sum(2, after(terms, input_own, out_other), up_sum)
     query_out, key_out, value_out, wide_out = last_swap(
         9, after(attn_sum, gain_own), q_cols, kv_cols
     )
 
-    def both_sides(own, other):
-        return jnp.where(side == 0, jnp.stack([own, other]), jnp.stack([other, own]))
-
-    layer_output = both_sides(out_own, out_other)
-    input_grad = both_sides(input_own, after(input_other, gain_own)).astype(F32)
+    layer_output, input_grad, query_out, key_out, value_out, wide_out, gate_out, up_out, down_out = (
+        final_forms(
+            out_own,
+            out_other,
+            input_own,
+            after(input_other, gain_own),
+            query_out,
+            key_out,
+            value_out,
+            wide_out,
+            gate_out,
+            up_out,
+            down_out,
+        )
+    )
     return (
         layer_output,
         input_grad,
         gain_own[0],
-        query_out.astype(F32),
-        key_out.astype(F32),
-        value_out.astype(F32),
-        wide_out.astype(F32),
+        query_out,
+        key_out,
+        value_out,
+        wide_out,
         gain_own[1],
-        gate_out.astype(F32),
-        up_out.astype(F32),
-        down_out.astype(F32),
+        gate_out,
+        up_out,
+        down_out,
     )
 
 

time: 649 us -> 624 us (0.961)
  Pallas kernels: 468 us -> 496 us
  waiting for transfers between devices: 29.3 us -> 1.4 us
  other arithmetic: 41.5 us -> 15.9 us
    pallas_call x2, Pallas kernels: 37.9 us -> 60 us  [the longest x1 49.8 us: open_weights(): pl.pallas_call(functools.partial(open_kernel, planes), out_shape=(jax.Sha...]
    convert_element_type x10 -> x1, other arithmetic: 20.5 us -> 1.56 us  [on_plane(): inputs_f = own_in.astype(F32)]
    all_gather x1, waiting for transfers between devices: 13.3 us -> 1.28 us  [on_plane(): down_w = lax.all_gather(down_own, 'dp', axis=0, tiled=True)]
    all_to_all x1 -> x0, waiting for transfers between devices: 8.78 us -> none  [to_units(): lax.all_to_all(weight, 'ctx', split_axis=1, concat_axis=0, tiled=True)]
    ppermute x1, waiting for transfers between devices: 7.01 us -> 0.01 us  [along_ctx(): lax.ppermute(after(block, earlier), 'ctx', [(0, 2), (1, 3), (2, 0), (3, 1)])]
    unnamed x53 -> x40, local copies, waits for them, and re-layouts: 17.8 us -> 14.6 us
  transfers between devices with their start and end apart: 13 -> 11, of which waited for: 3 -> 1; matrix products, arithmetic and copies ran while one was open for 15% -> 14% of each run, Pallas kernels for 69% -> 69%
where the time goes in v4:
time: 624 us; the launch traced here: 617 us
  Pallas kernels  496 us (79%)
  matrix products  58.1 us (9%)
  local copies, waits for them, and re-layouts  25 us (4%)
  other arithmetic  15.9 us (3%)
  between operations  14.9 us (2%)
    pallas_call x3, Pallas kernels, plane_gather(): pl.pallas_call(functools.partial(gather_kernel, rows, 8 if pair is not No...  130 us
    pallas_call x2, Pallas kernels, product_scatter(): pl.pallas_call(functools.partial(scatter_kernel, rows, swap is not None,...  105 us
    pallas_call x1, Pallas kernels, attend_back(): pl.pallas_call(functools.partial(attend_back_kernel, seqs, rows), out_sha...  60.9 us
    pallas_call x1, Pallas kernels, ffn_back(): pl.pallas_call(functools.partial(ffn_back_kernel, rows), out_shape=(jax.S...  58.2 us
    pallas_call x1, Pallas kernels, open_weights(): pl.pallas_call(functools.partial(open_kernel, planes), out_shape=(jax.Sha...  49.8 us
    dot_general x4, matrix products, matmul_t(): lax.dot_general(left_op, right_op, (((0,), (0,)), ((), ())), preferred_el...  40.6 us
    pallas_call x1, Pallas kernels, ffn(): pl.pallas_call(ffn_kernel, grid=(total // rows,), out_shape=(jax.ShapeDty...  25.1 us
    pallas_call x1, Pallas kernels, gain_sum(): pl.pallas_call(functools.partial(gain_kernel, planes, parts, cols), out_s...  22.1 us
  transfers between devices with their start and end apart: 11, of which 1 were waited for; matrix products, arithmetic and copies ran while one was open for 14% of the time, Pallas kernels for 69%

profile of v4, /device:TPU:0, one launch (start us, length us, event | category | flops | bytes accessed | tf_op | source)
XLA Modules:
  0.0 616.6 jit_solution(18324653727996749452)
XLA Ops:
  7.2 2.4 copy.30
  12.4 1.8 copy.29
  14.2 49.8 %open_weights.1 = (bf16[2048,640]{1,0:T(8,128)(2,1)}, bf16[512,2048]{1,0:T(8,128)(2,1)}, bf16[512,1024]{1,0:T(8,128)(2,1)}) custom-call(bf16[128,1024]{1,0:T(8,128)(2,1)} %q_ref.1, bf16[128,512]{1,0:T(8,128)(2,1)} %copy.41.kv_ref, bf16[128,1024]{1,0:T(8,128)(2,1)} %bitcast.39, bf16[128,4096]{1,0:T(8,128)(2,1)} %gate_ref.1, bf16[128,4096]{1,0:T(8,128)(2,1)} %up_ref.1, ...), custom_call_target="tpu_custom_call" | custom-call | bytes 1024 | tf_op jit(solution)/shard_map/open_weights/pallas_call | solution.py:1492
  64.0 1.6 collective-permute-start.1
  65.6 2.4 multiply_reduce_fusion
  68.7 44.5 %plane_gather.3 = (bf16[2048,2048]{1,0:T(8,128)(2,1)}, f32[16,8,128]{2,1,0:T(8,128)}) custom-call(bf16[256,2048]{1,0:T(8,128)(2,1)} %get-tuple-element.62.block_ref, f32[8,128]{1,0:T(8,128)} %maximum_convert_fusion.refs_0_), custom_call_target="tpu_custom_call" | custom-call | bytes 1024 | tf_op jit(solution)/shard_map/plane_gather/pallas_call | solution.py:431
  113.9 5.2 fusion
  119.1 1.5 slice_bitcast_fusion.3
  123.7 10.3 %fusion.4.q_ref.kv_ref = f32[2048,384]{1,0:T(8,128)} fusion(bf16[2048,2048]{1,0:T(8,128)(2,1)} %get-tuple-element.63, f32[2048]{0:T(1024)S(1)} %bitcast.45, f32[2048]{0:T(1024)S(1)} %add_rsqrt_fusion, bf16[2048,640]{1,0:T(8,128)(2,1)} %get-tuple-element.65.right), kind=kOutput, calls=%fused_computation.11 | convolution fusion | flops 3238002688 | bytes 13123584 | tf_op jit(solution)/shard_map/dot_general | solution.py:1577
  133.9 20.9 %attend.1 = (bf16[2048,256]{1,0:T(8,128)(2,1)S(1)}, bf16[2048,256]{1,0:T(8,128)(2,1)S(1)}, bf16[2048,128]{1,0:T(8,128)(2,1)S(1)}, f32[2048,256]{1,0:T(8,128)S(1)}) custom-call(f32[2048,384]{1,0:T(8,128)} %fusion.4.q_ref.kv_ref, f32[2048,384]{1,0:T(8,128)} %fusion.4.q_ref.kv_ref, f32[1024,128]{1,0:T(8,128)S(1)} %copy.31.cos_ref, f32[1024,128]{1,0:T(8,128)S(1)} %copy.32.sin_ref), custom_call_target="tpu_custom_call" | custom-call | flops 4294967296 | bytes 6291456 | tf_op jit(solution)/shard_map/attend/pallas_call | solution.py:935
  154.9 1.3 copy-done.2
  158.9 43.9 %product_scatter.2 = f32[256,2048]{1,0:T(8,128)} custom-call(bf16[2048,256]{1,0:T(8,128)(2,1)} %copy-done.6, bf16[2048,640]{1,0:T(8,128)(2,1)} %get-tuple-element.65.right), custom_call_target="tpu_custom_call" | custom-call | bytes 1024 | tf_op jit(solution)/shard_map/product_scatter/pallas_call | solution.py:671
  202.9 1.9 multiply_reduce_fusion.1
  207.3 39.7 %plane_gather.4.in_ref.refs_0_ = bf16[2048,2048]{1,0:T(8,128)(2,1)} custom-call(bf16[256,2048]{1,0:T(8,128)(2,1)} %multiply_convert_fusion.block_ref), custom_call_target="tpu_custom_call" | custom-call | bytes 1024 | tf_op jit(solution)/shard_map/plane_gather/pallas_call | solution.py:431
  247.0 3.1 lay.1
  250.1 3.2 copy-done.1
  253.3 25.1 %ffn.1 = (bf16[2048,1024]{1,0:T(8,128)(2,1)}, bf16[2048,1024]{1,0:T(8,128)(2,1)}, bf16[2048,1024]{1,0:T(8,128)(2,1)}) custom-call(bf16[2048,2048]{1,0:T(8,128)(2,1)} %plane_gather.4.in_ref.refs_0_, bf16[2048,2048]{1,0:T(8,128)(2,1)} %all-gather.3.cloned.1.call-done.w_ref.right_ref), custom_call_target="tpu_custom_call" | custom-call | bytes 1024 | tf_op jit(solution)/shard_map/ffn/pallas_call | solution.py:850
  278.5 14.0 %convolution_convert_fusion.1 = bf16[2048,1024]{1,0:T(8,128)(2,1)} fusion(bf16[2048,2048]{1,0:T(8,128)(2,1)} %bitcast.35, bf16[2048,1024]{1,0:T(8,128)(2,1)} %get-tuple-element.72.left_ref), kind=kOutput, calls=%fused_computation.6 | convolution fusion | flops 8592031744 | bytes 16777216 | tf_op jit(solution)/shard_map/dot_general | solution.py:55
  295.8 58.2 %ffn_back.1 = (f32[256,2048]{1,0:T(8,128)}, bf16[256,2048]{1,0:T(8,128)(2,1)}, f32[8,2048]{1,0:T(8,128)}, bf16[2048,1024]{1,0:T(8,128)(2,1)}, bf16[2048,1024]{1,0:T(8,128)(2,1)}) custom-call(bf16[2,256,2048]{2,1,0:T(8,128)(2,1)} %own_ref.3, bf16[2,256,2048]{2,1,0:T(8,128)(2,1)} %collective-permute-done.far_ref, ...), custom_call_target="tpu_custom_call" | custom-call | bytes 1024 | tf_op jit(solution)/shard_map/ffn_back/pallas_call | solution.py:801
  353.9 14.1 %convolution_convert_fusion = bf16[2048,1024]{1,0:T(8,128)(2,1)} fusion(bf16[2048,2048]{1,0:T(8,128)(2,1)} %plane_gather.4.in_ref.refs_0_, bf16[2048,1024]{1,0:T(8,128)(2,1)} %get-tuple-element.77), kind=kOutput, calls=%fused_computation.5 | convolution fusion | flops 8592031744 | bytes 16777216 | tf_op jit(solution)/shard_map/dot_general | solution.py:55
  368.1 46.0 %plane_gather.5 = (bf16[2048,2048]{1,0:T(8,128)(2,1)}, bf16[2048,1024]{1,0:T(8,128)(2,1)}) custom-call(bf16[256,2048]{1,0:T(8,128)(2,1)} %get-tuple-element.78.block_ref, bf16[2048,2048]{1,0:T(8,128)(2,1)} %plane_gather.4.in_ref.refs_0_, bf16[2048,1024]{1,0:T(8,128)(2,1)} %get-tuple-element.79.refs_1_), custom_call_target="tpu_custom_call" | custom-call | bytes 1024 | tf_op jit(solution)/shard_map/plane_gather/pallas_call | solution.py:431
  414.4 7.2 %convolution_convert_fusion.4.up_ref = bf16[2048,256]{1,0:T(8,128)(2,1)} fusion(bf16[2048,2048]{1,0:T(8,128)(2,1)} %get-tuple-element.80, bf16[2048,640]{1,0:T(8,128)(2,1)} %get-tuple-element.65.right), kind=kOutput, calls=%fused_computation.10 | convolution fusion | flops 2148007936 | bytes 10485760 | tf_op jit(solution)/shard_map/dot_general | solution.py:1603
  421.6 3.6 convolution_convert_fusion.3
  425.2 60.9 %attend_back.1 = (bf16[2048,384]{1,0:T(8,128)(2,1)}, bf16[256,2048]{1,0:T(8,128)(2,1)}, bf16[4096,128]{1,0:T(8,128)(2,1)}) custom-call(bf16[2048,256]{1,0:T(8,128)(2,1)} %copy-done.5, bf16[2048,128]{1,0:T(8,128)(2,1)} %copy-done.8, bf16[2048,256]{1,0:T(8,128)(2,1)} %convolution_convert_fusion.4.up_ref, f32[2048,256]{1,0:T(8,128)} %copy-done.2, ...), custom_call_target="tpu_custom_call" | custom-call | bytes 1024 | tf_op jit(solution)/shard_map/attend_back/pallas_call | solution.py:1094
  486.1 8.9 %convolution_convert_fusion.2 = bf16[2048,384]{1,0:T(8,128)(2,1)S(1)} fusion(bf16[2048,384]{1,0:T(8,128)(2,1)} %get-tuple-element.84.left, bf16[2048,2048]{1,0:T(8,128)(2,1)} %get-tuple-element.63, f32[2048]{0:T(1024)S(1)} %bitcast.46, f32[2048]{0:T(1024)S(1)} %add_rsqrt_fusion), kind=kOutput, calls=%fused_computation.7 | convolution fusion | flops 3238789120 | bytes 11550720 | tf_op jit(solution)/shard_map/dot_general | solution.py:55
  495.0 1.8 pad_maximum_fusion
  496.8 1.6 convert_element_type.61.refs_1_
  500.4 60.9 %product_scatter.3 = (bf16[256,2048]{1,0:T(8,128)(2,1)}, f32[8,2048]{1,0:T(8,128)}, bf16[128,4096]{1,0:T(8,128)(2,1)}) custom-call(bf16[2048,384]{1,0:T(8,128)(2,1)} %get-tuple-element.84.left, bf16[2048,640]{1,0:T(8,128)(2,1)} %get-tuple-element.65.right, bf16[512,1024]{1,0:T(8,128)(2,1)} %reduce-scatter.7.cloned.1.call-done.refs_0_, ...), custom_call_target="tpu_custom_call" | custom-call | bytes 1024 | tf_op jit(solution)/shard_map/product_scatter/pallas_call | solution.py:671
  561.3 1.3 collective-permute-start.4
  564.9 22.1 %gain_sum.1 = (f32[2,128]{1,0:T(2,128)}, bf16[128,4096]{1,0:T(8,128)(2,1)}) custom-call(f32[2,2048]{1,0:T(2,128)} %pad_maximum_fusion.3.terms_ref, bf16[512,1024]{1,0:T(8,128)(2,1)} %reduce-scatter.9.cloned.1.call-done.up_ref), custom_call_target="tpu_custom_call" | custom-call | bytes 1024 | tf_op jit(solution)/shard_map/gain_sum/pallas_call | solution.py:1194
  588.3 10.8 %last_swap.1 = (bf16[128,1024]{1,0:T(8,128)(2,1)}, bf16[128,256]{1,0:T(8,128)(2,1)}, bf16[128,256]{1,0:T(8,128)(2,1)}, bf16[1024,128]{1,0:T(8,128)(2,1)}) custom-call(bf16[512,640]{1,0:T(8,128)(2,1)} %reduce-scatter.11.cloned.1.call-done.attn_ref), custom_call_target="tpu_custom_call" | custom-call | bytes 1024 | tf_op jit(solution)/shard_map/last_swap/pallas_call | solution.py:1245
  599.1 10.2 %final_forms.1 = (bf16[2,256,2048]{2,1,0:T(8,128)(2,1)}, f32[2,256,2048]{2,1,0:T(8,128)}, f32[128,1024]{1,0:T(8,128)}, f32[128,256]{1,0:T(8,128)}, f32[128,256]{...) custom-call(bf16[256,2048]{1,0:T(8,128)(2,1)} %get-tuple-element.82.own_ref, ...), custom_call_target="tpu_custom_call" | custom-call | bytes 1024 | tf_op jit(solution)/shard_map/final_forms/pallas_call | solution.py:1286
  (86 shorter events, 21.7 us)
Async XLA Ops:
  7.2 56.9 %copy-start = (bf16[2,256,2048]{2,1,0:T(8,128)(2,1)S(1)}, bf16[2,256,2048]{2,1,0:T(8,128)(2,1)}, u32[]{:S(2)}) copy-start(bf16[2,256,2048]{2,1,0:T(8,128)(2,1)} %own_ref.3) | copy-start | bytes 6291460
  7.2 246.1 %all-gather.3.cloned.1.call-start = ((), (), s32[]{:S(2)}) async-start(), calls=%async_computation.4 | async-start | bytes 10485760 | tf_op jit(solution)/shard_map/all_gather | solution.py:1572
  12.3 55.7 %copy-start.15 = (bf16[128]{0:T(256)(128)(2,1)S(1)}, bf16[128]{0:T(256)(128)(2,1)}, u32[]{:S(2)}) copy-start(bf16[128]{0:T(256)(128)(2,1)} %param.17) | copy-start | bytes 772
  12.3 55.7 %copy-start.16 = (bf16[128]{0:T(256)(128)(2,1)S(1)}, bf16[128]{0:T(256)(128)(2,1)}, u32[]{:S(2)}) copy-start(bf16[128]{0:T(256)(128)(2,1)} %param.12) | copy-start | bytes 772
  64.0 231.8 %all-gather.5.cloned.1.call-start = ((), (), s32[]{:S(2)}) async-start(), calls=%async_computation.5 | async-start | bytes 5242880 | tf_op jit(solution)/shard_map/all_gather | solution.py:1573
  64.0 183.0 %collective-permute-start.1 = (bf16[2,256,2048]{2,1,0:T(8,128)(2,1)S(1)}, bf16[2,256,2048]{2,1,0:T(8,128)(2,1)}, u32[]{:S(2)}, u32[]{:S(2)}) collective-permute-start(bf16[2,256,2048]{2,1,0:T(8,128)(2,1)S(1)} %copy-done), channel_id=1, source_target_pairs={{0,2},{2,0},{4,6},{6,4},{1,3},{3,1},{5,7},{7,5},{8,10},{10,8},{12,... | collective-permute-start | bytes 6291464 | tf_op jit(solution)/shard_map/ppermute | solution.py:1329
  113.2 91.6 %collective-permute-start = (bf16[2,256,2048]{2,1,0:T(8,128)(2,1)S(1)}, bf16[2,256,2048]{2,1,0:T(8,128)(2,1)}, u32[]{:S(2)}, u32[]{:S(2)}) collective-permute-start(bf16[2,256,2048]{2,1,0:T(8,128)(2,1)S(1)} %copy-done), channel_id=1, source_target_pairs={{0,4},{2,6},{4,0},{6,2},{1,5},{3,7},{5,1},{7,3},{8,12},{10,14},{12... | collective-permute-start | bytes 6291464 | tf_op jit(solution)/shard_map/ppermute | solution.py:1327
  113.9 311.3 %reduce-scatter.5.cloned.1.call-start = ((), (), s32[]{:S(2)}) async-start(), calls=%async_computation.6 | async-start | bytes 5242880 | tf_op jit(solution)/shard_map/reduce_scatter | solution.py:1589
  121.5 12.5 %copy-start.3 = (f32[1024,128]{1,0:T(8,128)}, f32[1024,128]{1,0:T(8,128)S(1)}, u32[]{:S(2)}) copy-start(f32[1024,128]{1,0:T(8,128)S(1)} %copy.32.sin_ref) | copy-start | bytes 1572868
  123.6 10.3 %copy-start.4 = (f32[1024,128]{1,0:T(8,128)}, f32[1024,128]{1,0:T(8,128)S(1)}, u32[]{:S(2)}) copy-start(f32[1024,128]{1,0:T(8,128)S(1)} %copy.31.cos_ref) | copy-start | bytes 1572868
  154.9 1.3 copy-start.2
  156.2 1.0 copy-start.5
  157.2 1.0 copy-start.6
  158.1 0.8 copy-start.8
  158.9 43.9 %copy-start.10 = (bf16[256,2048]{1,0:T(8,128)(2,1)S(1)}, bf16[256,2048]{1,0:T(8,128)(2,1)}, u32[]{:S(2)}) copy-start(bf16[256,2048]{1,0:T(8,128)(2,1)} %get-tuple-element.62.block_ref) | copy-start | bytes 3145732
  204.8 1.3 copy-start.9
  204.8 42.2 %collective-permute-start.2 = (bf16[2,256,2048]{2,1,0:T(8,128)(2,1)}, bf16[2,256,2048]{2,1,0:T(8,128)(2,1)}, u32[]{:S(2)}, u32[]{:S(2)}) collective-permute-start(bf16[2,256,2048]{2,1,0:T(8,128)(2,1)} %collective-permute-done.far_ref), channel_id=1, source_target_pairs={{0,2},{2,0},{4,6},{6,4},{1,3},{3,1},{5,7},{7,5},{8,10},{10,8},{12,... | collective-permute-start | bytes 6291464 | tf_op jit(solution)/shard_map/ppermute | solution.py:1329
  250.1 3.2 copy-start.1
  292.5 207.8 %reduce-scatter.7.cloned.1.call-start = ((), (), s32[]{:S(2)}) async-start(), calls=%async_computation.7 | async-start | bytes 5242880 | tf_op jit(solution)/shard_map/reduce_scatter | solution.py:1600
  368.0 196.9 %reduce-scatter.9.cloned.1.call-start = ((), (), s32[]{:S(2)}) async-start(), calls=%async_computation.8 | async-start | bytes 5242880 | tf_op jit(solution)/shard_map/reduce_scatter | solution.py:1602
  414.1 174.1 %reduce-scatter.11.cloned.1.call-start = ((), (), s32[]{:S(2)}) async-start(), calls=%async_computation.9 | async-start | bytes 3276800 | tf_op jit(solution)/shard_map/reduce_scatter | solution.py:1622
  414.4 7.2 %copy-start.7 = (bf16[2048,256]{1,0:T(8,128)(2,1)S(1)}, bf16[2048,256]{1,0:T(8,128)(2,1)}, u32[]{:S(2)}) copy-start(bf16[2048,256]{1,0:T(8,128)(2,1)} %copy-done.6) | copy-start | bytes 3145732
  414.4 7.2 %copy-start.17 = (bf16[2048,2048]{1,0:T(8,128)(2,1)S(1)}, bf16[2048,2048]{1,0:T(8,128)(2,1)}, u32[]{:S(2)}) copy-start(bf16[2048,2048]{1,0:T(8,128)(2,1)} %get-tuple-element.80) | copy-start | bytes 25165828
  486.1 8.9 %copy-start.14 = (bf16[2048,256]{1,0:T(8,128)(2,1)S(1)}, bf16[2048,256]{1,0:T(8,128)(2,1)}, u32[]{:S(2)}) copy-start(bf16[2048,256]{1,0:T(8,128)(2,1)} %convolution_convert_fusion.3) | copy-start | bytes 3145732
  496.8 2.4 copy-start.11
  499.2 65.7 %collective-permute-start.3 = (bf16[256,2048]{1,0:T(8,128)(2,1)S(1)}, bf16[256,2048]{1,0:T(8,128)(2,1)S(1)}, u32[]{:S(2)}, u32[]{:S(2)}) collective-permute-start(bf16[256,2048]{1,0:T(8,128)(2,1)S(1)} %copy-done.11), channel_id=1, source_target_pairs={{0,1},{1,0},{2,3},{3,2},{4,5},{5,4},{6,7},{7,6},{8,9},{9,8},{10,11... | collective-permute-start | bytes 3145736 | tf_op jit(solution)/shard_map/ppermute | solution.py:1525
  561.3 25.7 %collective-permute-start.4 = (bf16[256,2048]{1,0:T(8,128)(2,1)}, bf16[256,2048]{1,0:T(8,128)(2,1)S(1)}, u32[]{:S(2)}, u32[]{:S(2)}) collective-permute-start(bf16[256,2048]{1,0:T(8,128)(2,1)} %get-tuple-element.86.in_ref), channel_id=1, source_target_pairs={{0,1},{1,0},{2,3},{3,2},{4,5},{5,4},{6,7},{7,6},{8,9},{9,8},{10,11... | collective-permute-start | bytes 3145736 | tf_op jit(solution)/shard_map/ppermute | solution.py:1525
  564.9 34.2 %copy-start.12 = (bf16[256,2048]{1,0:T(8,128)(2,1)}, bf16[256,2048]{1,0:T(8,128)(2,1)S(1)}, u32[]{:S(2)}) copy-start(bf16[256,2048]{1,0:T(8,128)(2,1)S(1)} %collective-permute-done.3.other_ref) | copy-start | bytes 3145732
  587.0 12.1 %copy-start.13 = (bf16[256,2048]{1,0:T(8,128)(2,1)}, bf16[256,2048]{1,0:T(8,128)(2,1)S(1)}, u32[]{:S(2)}) copy-start(bf16[256,2048]{1,0:T(8,128)(2,1)S(1)} %collective-permute-done.4.in_other_ref) | copy-start | bytes 3145732
Sparse Core Ops, SparseCore 0:
  64.1 151.0 all-gather.2
  216.7 78.9 all-gather.4
  298.1 75.2 reduce-scatter.4
  375.6 77.2 reduce-scatter.6
  455.1 77.2 reduce-scatter.8
  535.2 52.6 reduce-scatter.10

commit v5 on v4

--- a/solution.py
+++ b/solution.py
@@ -1119,7 +1119,8 @@
     planes,
     parts,
     cols,
-    terms_ref,
+    attn_term_ref,
+    ffn_term_ref,
     up_ref,
     gain_ref,
     laid_ref,
@@ -1139,7 +1140,8 @@
     others = [{"dp": (plane + step) % planes} for step in range(1, planes)]
     corner = {"ctx": (1 - row) * 2 + 1 - core}
     greet((near_core, near_side, near_row, corner) + tuple(others))
-    total[...] = terms_ref[...]
+    first = lax.broadcasted_iota(jnp.int32, total.shape, 0) == 0
+    total[...] = jnp.where(first, attn_term_ref[...], ffn_term_ref[...])
     copies = []
     up_copies, up_local = swap_copies(up_ref, swapped, *swap_sems)
     for number, target in enumerate((near_core, near_row)):
@@ -1183,10 +1185,10 @@
         copy.wait_send()
 
 
-def gain_sum(number, terms, up_sum):
+def gain_sum(number, attn_term, ffn_term, up_sum):
     planes = lax.axis_size("dp")
     parts = lax.axis_size("ctx")
-    rows, width = terms.shape
+    rows, width = attn_term.shape
     cols = width // (planes * parts)
     deep = up_sum.shape[0] // parts
     vmem = pl.BlockSpec(memory_space=pltpu.VMEM)
@@ -1197,7 +1199,7 @@
             jax.ShapeDtypeStruct((rows, cols), F32),
             jax.ShapeDtypeStruct((deep, parts * up_sum.shape[1]), BF16),
         ),
-        in_specs=[vmem, anywhere],
+        in_specs=[vmem, vmem, anywhere],
         out_specs=(vmem,) * 2,
         scratch_shapes=[
             pltpu.VMEM((rows, width), F32),
@@ -1213,7 +1215,7 @@
         compiler_params=pltpu.CompilerParams(collective_id=number, has_side_effects=True),
         cost_estimate=pl.CostEstimate(flops=0, bytes_accessed=1024, transcendentals=0),
         name="gain_sum",
-    )(terms, up_sum)
+    )(attn_term, ffn_term, up_sum)
 
 
 def last_kernel(
@@ -1259,20 +1261,19 @@
     )(attn_sum)
 
 
-def final_kernel(own_ref, other_ref, in_ref, in_other_ref, *refs):
+def final_kernel(own_ref, other_ref, *refs):
     first = lax.axis_index("tensor") == 0
-    sources, (out_ref, in_out_ref, *targets) = refs[:7], refs[7:]
-    own, other = own_ref[...], other_ref[...]
+    half = len(refs) // 2
+    sources, (out_ref, *targets) = refs[:half], refs[half:]
+    own, other = own_ref[...].astype(out_ref.dtype), other_ref[...].astype(out_ref.dtype)
     out_ref[0], out_ref[1] = jnp.where(first, own, other), jnp.where(first, other, own)
-    own, other = in_ref[...].astype(F32), in_other_ref[...].astype(F32)
-    in_out_ref[0], in_out_ref[1] = jnp.where(first, own, other), jnp.where(first, other, own)
     for source, target in zip(sources, targets):
         target[...] = source[...].astype(F32)
 
 
-def final_forms(out_own, out_other, in_own, in_other, *grads):
-    steps = 8
-    rows, width = out_own.shape
+def final_forms(own, other, dtype, *grads):
+    steps = 4
+    rows, width = own.shape
     halves = pl.BlockSpec((rows // steps, width), lambda i: (i, 0))
     whole = pl.BlockSpec((2, rows // steps, width), lambda i: (0, i, 0))
 
@@ -1286,17 +1287,14 @@
     return pl.pallas_call(
         final_kernel,
         grid=(steps,),
-        out_shape=(
-            jax.ShapeDtypeStruct((2, rows, width), BF16),
-            jax.ShapeDtypeStruct((2, rows, width), F32),
-        )
+        out_shape=(jax.ShapeDtypeStruct((2, rows, width), dtype),)
         + tuple(jax.ShapeDtypeStruct(grad.shape, F32) for grad in grads),
-        in_specs=[halves] * 4 + blocks,
-        out_specs=(whole, whole, *blocks),
+        in_specs=[halves] * 2 + blocks,
+        out_specs=(whole, *blocks),
         compiler_params=pltpu.CompilerParams(vmem_limit_bytes=60 * 1024 * 1024),
         cost_estimate=pl.CostEstimate(flops=0, bytes_accessed=1024, transcendentals=0),
         name="final_forms",
-    )(out_own, out_other, in_own, in_other, *grads)
+    )(own, other, *grads)
 
 
 def lay_kernel(own_ref, far_ref, twin_ref, twin_far_ref, all_ref, sems):
@@ -1342,14 +1340,23 @@
 def open_kernel(
     planes,
     q_ref,
-    kv_ref,
-    wide_ref,
+    key_ref,
+    value_ref,
+    out_ref,
     gate_ref,
     up_ref,
-    down_ref,
+    down_in_ref,
     attn_ref,
     gate_up_ref,
     down_own_ref,
+    key_in,
+    value_in,
+    out_in,
+    down_in,
+    kv_ref,
+    wide_ref,
+    down_ref,
+    load_sems,
     send_sems,
     recv_sems,
     local_sems,
@@ -1375,6 +1382,23 @@
     def _():
         pl.semaphore_signal(barrier, inc=1, device_id=behind, device_id_type=MESH_ID)
 
+    loads = [
+        pltpu.make_async_copy(source, target, load_sems.at[at])
+        for at, (source, target) in enumerate(
+            ((key_ref, key_in), (value_ref, value_in), (out_ref, out_in), (down_in_ref, down_in))
+        )
+    ]
+    for load in loads:
+        load.start()
+    for load in loads[:3]:
+        load.wait()
+    size = key_in.shape[1] // 4
+    for part in range(4):
+        lanes = slice(part * size, (part + 1) * size)
+        kv_ref[:, part * 2 * size : (part + 1) * 2 * size] = jnp.concatenate(
+            [key_in[:, lanes], value_in[:, lanes]], axis=1
+        )
+    wide_ref[...] = jnp.transpose(out_in[...].astype(F32)).astype(BF16)
     pl.semaphore_wait(barrier, 3 + more.astype(jnp.int32) + fewer.astype(jnp.int32))
 
     mine = pl.multiple_of(here * rows, rows)
@@ -1414,7 +1438,7 @@
     for at in (1, 2):
         for which in range(3):
             away[which][at].start()
-    for which in range(3, 6):
+    for which in range(3, 5):
         for copy in away[which]:
             copy.start()
         local[which].start()
@@ -1456,6 +1480,12 @@
         away[which][2].wait_recv()
     for way in range(2):
         hop_start(way, 0, 1)
+    loads[3].wait()
+    for part in range(4):
+        there = slice(part * units, (part + 1) * units)
+        down_ref[:, there] = jnp.transpose(down_in[there, :].astype(F32)).astype(BF16)
+    for copy in away[5] + [local[5]]:
+        copy.start()
     for far in range(planes - 1):
         for part in range(2):
             for way in range(2):
@@ -1483,10 +1513,10 @@
             copy.wait_send()
 
 
-def open_weights(query, keyval, wide, gate, up, down):
+def open_weights(query, key, value, out, gate, up, down):
     planes = lax.axis_size("dp")
     rows = query.shape[0]
-    cols = (query.shape[1] + keyval.shape[1] + wide.shape[1]) // 4
+    cols = (query.shape[1] + 2 * key.shape[1] + out.shape[0]) // 4
     units = gate.shape[1] // 4
     anywhere, vmem = pl.BlockSpec(memory_space=pl.ANY), pl.BlockSpec(memory_space=pltpu.VMEM)
     return pl.pallas_call(
@@ -1496,9 +1526,17 @@
             jax.ShapeDtypeStruct((4 * rows, 2 * units), BF16),
             jax.ShapeDtypeStruct((4 * rows, units), BF16),
         ),
-        in_specs=[anywhere] * 6,
+        in_specs=[anywhere] * 7,
         out_specs=(vmem, anywhere, anywhere),
         scratch_shapes=[
+            pltpu.VMEM(key.shape, BF16),
+            pltpu.VMEM(value.shape, BF16),
+            pltpu.VMEM(out.shape, BF16),
+            pltpu.VMEM(down.shape, BF16),
+            pltpu.VMEM((rows, 2 * key.shape[1]), BF16),
+            pltpu.VMEM((rows, out.shape[0]), BF16),
+            pltpu.VMEM((rows, down.shape[0]), BF16),
+            pltpu.SemaphoreType.DMA((4,)),
             pltpu.SemaphoreType.DMA((6, 3)),
             pltpu.SemaphoreType.DMA((6, 3)),
             pltpu.SemaphoreType.DMA((6,)),
@@ -1510,7 +1548,7 @@
         ),
         cost_estimate=pl.CostEstimate(flops=0, bytes_accessed=1024, transcendentals=0),
         name="open_weights",
-    )(query, keyval, wide, gate, up, down)
+    )(query, key, value, out, gate, up, down)
 
 
 def after(value, *earlier):
@@ -1552,12 +1590,7 @@
     sine = jnp.sin(theta)
     signed = jnp.tile(jnp.concatenate([-sine, sine], axis=1), (1, 2))
 
-    keyval = jnp.concatenate(
-        [w_key.reshape(rows_w, parts, kv_cols), w_value.reshape(rows_w, parts, kv_cols)], axis=2
-    ).reshape(rows_w, -1)
-    attn_w, gate_up, down_own = open_weights(
-        w_query, keyval, w_out.T, w_gate, w_up, w_down.T
-    )
+    attn_w, gate_up, down_own = open_weights(w_query, w_key, w_value, w_out, w_gate, w_up, w_down)
     qkv_cols = q_cols + 2 * kv_cols
     w_qkv = attn_w[:, :qkv_cols]
     w_out_t = attn_w[:, qkv_cols:]
@@ -1630,26 +1663,22 @@
         (inputs_f, factor_one, gain_one[None], hidden_grad),
     )
     input_other = swap_sides(input_own)
-    terms = jnp.concatenate([attn_term[:1], ffn_term[:1]])
-    gain_own, up_out = gain_sum(2, after(terms, input_own, out_other), up_sum)
+    layer_output, gate_out, down_out = final_forms(
+        out_own, after(out_other, input_own), BF16, gate_out, down_out
+    )
+    gain_own, up_out = gain_sum(2, after(attn_term, layer_output), ffn_term, up_sum)
     query_out, key_out, value_out, wide_out = last_swap(
         9, after(attn_sum, gain_own), q_cols, kv_cols
     )
-
-    layer_output, input_grad, query_out, key_out, value_out, wide_out, gate_out, up_out, down_out = (
-        final_forms(
-            out_own,
-            out_other,
-            input_own,
-            after(input_other, gain_own),
-            query_out,
-            key_out,
-            value_out,
-            wide_out,
-            gate_out,
-            up_out,
-            down_out,
-        )
+    input_grad, query_out, key_out, value_out, wide_out, up_out = final_forms(
+        input_own,
+        after(input_other, gain_own),
+        F32,
+        query_out,
+        key_out,
+        value_out,
+        wide_out,
+        up_out,
     )
     return (
         layer_output,

time: 624 us -> 613 us (0.982)
  local copies, waits for them, and re-layouts: 25 us -> 17.4 us
    unnamed x40 -> x34, local copies, waits for them, and re-layouts: 14.6 us -> 9.4 us
  transfers between devices with their start and end apart: 11 -> 11, of which waited for: 1 -> 2; matrix products, arithmetic and copies ran while one was open for 14% -> 13% of each run, Pallas kernels for 69% -> 70%
where the time goes in v5:
time: 613 us; the launch traced here: 605 us
  Pallas kernels  493 us (80%)
  matrix products  58.1 us (9%)
  local copies, waits for them, and re-layouts  17.4 us (3%)
  other arithmetic  15.3 us (2%)
  between operations  14.9 us (2%)
    pallas_call x3, Pallas kernels, plane_gather(): pl.pallas_call(functools.partial(gather_kernel, rows, 8 if pair is not No...  130 us
    pallas_call x2, Pallas kernels, product_scatter(): pl.pallas_call(functools.partial(scatter_kernel, rows, swap is not None,...  103 us
    pallas_call x1, Pallas kernels, attend_back(): pl.pallas_call(functools.partial(attend_back_kernel, seqs, rows), out_sha...  60.9 us
    pallas_call x1, Pallas kernels, ffn_back(): pl.pallas_call(functools.partial(ffn_back_kernel, rows), out_shape=(jax.S...  58.1 us
    pallas_call x1, Pallas kernels, open_weights(): pl.pallas_call(functools.partial(open_kernel, planes), out_shape=(jax.Sha...  49.9 us
    dot_general x4, matrix products, matmul_t(): lax.dot_general(left_op, right_op, (((0,), (0,)), ((), ())), preferred_el...  40.6 us
    pallas_call x1, Pallas kernels, ffn(): pl.pallas_call(ffn_kernel, grid=(total // rows,), out_shape=(jax.ShapeDty...  25.1 us
    pallas_call x1, Pallas kernels, attend(): pl.pallas_call(functools.partial(attend_kernel, length), grid=(seqs, pair...  20.9 us
  transfers between devices with their start and end apart: 11, of which 2 were waited for; matrix products, arithmetic and copies ran while one was open for 13% of the time, Pallas kernels for 70%

profile of v5, /device:TPU:0, one launch (start us, length us, event | category | flops | bytes accessed | tf_op | source)
XLA Modules:
  0.0 605.3 jit_solution(9553273901569741843)
XLA Ops:
  7.3 49.9 %open_weights.1 = (bf16[2048,640]{1,0:T(8,128)(2,1)}, bf16[512,2048]{1,0:T(8,128)(2,1)}, bf16[512,1024]{1,0:T(8,128)(2,1)}) custom-call(bf16[128,1024]{1,0:T(8,128)(2,1)} %q_ref.1, bf16[128,256]{1,0:T(8,128)(2,1)} %key_ref.1, bf16[128,256]{1,0:T(8,128)(2,1)} %value_ref.1, bf16[1024,128]{1,0:T(8,128)(2,1)} %out_ref.1, bf16[128,4096]{1,0:T(8,128)(2,1)} %gate_ref.1, ...), custom_call_target="tpu_custom_call" | custom-call | bytes 1024 | tf_op jit(solution)/shard_map/open_weights/pallas_call | solution.py:1522
  57.3 1.6 collective-permute-start.1
  58.8 2.4 multiply_reduce_fusion
  62.0 44.4 %plane_gather.3 = (bf16[2048,2048]{1,0:T(8,128)(2,1)}, f32[16,8,128]{2,1,0:T(8,128)}) custom-call(bf16[256,2048]{1,0:T(8,128)(2,1)} %get-tuple-element.63.block_ref, f32[8,128]{1,0:T(8,128)} %maximum_convert_fusion.refs_0_), custom_call_target="tpu_custom_call" | custom-call | bytes 1024 | tf_op jit(solution)/shard_map/plane_gather/pallas_call | solution.py:431
  107.1 5.2 fusion
  112.3 1.5 slice_bitcast_fusion.3
  116.9 10.3 %fusion.4.q_ref.kv_ref = f32[2048,384]{1,0:T(8,128)} fusion(bf16[2048,2048]{1,0:T(8,128)(2,1)} %get-tuple-element.64, f32[2048]{0:T(1024)S(1)} %bitcast.35, f32[2048]{0:T(1024)S(1)} %add_rsqrt_fusion, bf16[2048,640]{1,0:T(8,128)(2,1)} %get-tuple-element.66.right), kind=kOutput, calls=%fused_computation.11 | convolution fusion | flops 3238002688 | bytes 13123584 | tf_op jit(solution)/shard_map/dot_general | solution.py:1610
  127.1 20.9 %attend.1 = (bf16[2048,256]{1,0:T(8,128)(2,1)S(1)}, bf16[2048,256]{1,0:T(8,128)(2,1)S(1)}, bf16[2048,128]{1,0:T(8,128)(2,1)S(1)}, f32[2048,256]{1,0:T(8,128)S(1)}) custom-call(f32[2048,384]{1,0:T(8,128)} %fusion.4.q_ref.kv_ref, f32[2048,384]{1,0:T(8,128)} %fusion.4.q_ref.kv_ref, f32[1024,128]{1,0:T(8,128)S(1)} %copy.24.cos_ref, f32[1024,128]{1,0:T(8,128)S(1)} %copy.25.sin_ref), custom_call_target="tpu_custom_call" | custom-call | flops 4294967296 | bytes 6291456 | tf_op jit(solution)/shard_map/attend/pallas_call | solution.py:935
  148.1 1.3 copy-done.2
  152.1 43.9 %product_scatter.2 = f32[256,2048]{1,0:T(8,128)} custom-call(bf16[2048,256]{1,0:T(8,128)(2,1)} %copy-done.6, bf16[2048,640]{1,0:T(8,128)(2,1)} %get-tuple-element.66.right), custom_call_target="tpu_custom_call" | custom-call | bytes 1024 | tf_op jit(solution)/shard_map/product_scatter/pallas_call | solution.py:671
  196.0 1.9 multiply_reduce_fusion.1
  200.5 39.6 %plane_gather.4.in_ref.refs_0_ = bf16[2048,2048]{1,0:T(8,128)(2,1)} custom-call(bf16[256,2048]{1,0:T(8,128)(2,1)} %multiply_convert_fusion.block_ref), custom_call_target="tpu_custom_call" | custom-call | bytes 1024 | tf_op jit(solution)/shard_map/plane_gather/pallas_call | solution.py:431
  240.2 3.1 lay.1
  243.3 3.2 copy-done.1
  246.5 25.1 %ffn.1 = (bf16[2048,1024]{1,0:T(8,128)(2,1)}, bf16[2048,1024]{1,0:T(8,128)(2,1)}, bf16[2048,1024]{1,0:T(8,128)(2,1)}) custom-call(bf16[2048,2048]{1,0:T(8,128)(2,1)} %plane_gather.4.in_ref.refs_0_, bf16[2048,2048]{1,0:T(8,128)(2,1)} %all-gather.3.cloned.1.call-done.w_ref.right_ref), custom_call_target="tpu_custom_call" | custom-call | bytes 1024 | tf_op jit(solution)/shard_map/ffn/pallas_call | solution.py:850
  271.6 14.0 %convolution_convert_fusion.1 = bf16[2048,1024]{1,0:T(8,128)(2,1)} fusion(bf16[2048,2048]{1,0:T(8,128)(2,1)} %bitcast.30, bf16[2048,1024]{1,0:T(8,128)(2,1)} %get-tuple-element.73.left_ref), kind=kOutput, calls=%fused_computation.6 | convolution fusion | flops 8592031744 | bytes 16777216 | tf_op jit(solution)/shard_map/dot_general | solution.py:55
  288.9 58.1 %ffn_back.1 = (f32[256,2048]{1,0:T(8,128)}, bf16[256,2048]{1,0:T(8,128)(2,1)}, f32[8,2048]{1,0:T(8,128)}, bf16[2048,1024]{1,0:T(8,128)(2,1)}, bf16[2048,1024]{1,0:T(8,128)(2,1)}) custom-call(bf16[2,256,2048]{2,1,0:T(8,128)(2,1)} %own_ref.3, bf16[2,256,2048]{2,1,0:T(8,128)(2,1)} %collective-permute-done.far_ref, ...), custom_call_target="tpu_custom_call" | custom-call | bytes 1024 | tf_op jit(solution)/shard_map/ffn_back/pallas_call | solution.py:801
  347.0 14.1 %convolution_convert_fusion = bf16[2048,1024]{1,0:T(8,128)(2,1)} fusion(bf16[2048,2048]{1,0:T(8,128)(2,1)} %plane_gather.4.in_ref.refs_0_, bf16[2048,1024]{1,0:T(8,128)(2,1)} %get-tuple-element.78), kind=kOutput, calls=%fused_computation.5 | convolution fusion | flops 8592031744 | bytes 16777216 | tf_op jit(solution)/shard_map/dot_general | solution.py:55
  361.1 46.0 %plane_gather.5 = (bf16[2048,2048]{1,0:T(8,128)(2,1)}, bf16[2048,1024]{1,0:T(8,128)(2,1)}) custom-call(bf16[256,2048]{1,0:T(8,128)(2,1)} %get-tuple-element.79.block_ref, bf16[2048,2048]{1,0:T(8,128)(2,1)} %plane_gather.4.in_ref.refs_0_, bf16[2048,1024]{1,0:T(8,128)(2,1)} %get-tuple-element.80.refs_1_), custom_call_target="tpu_custom_call" | custom-call | bytes 1024 | tf_op jit(solution)/shard_map/plane_gather/pallas_call | solution.py:431
  407.4 7.2 %convolution_convert_fusion.4.up_ref = bf16[2048,256]{1,0:T(8,128)(2,1)} fusion(bf16[2048,2048]{1,0:T(8,128)(2,1)} %get-tuple-element.81, bf16[2048,640]{1,0:T(8,128)(2,1)} %get-tuple-element.66.right), kind=kOutput, calls=%fused_computation.10 | convolution fusion | flops 2148007936 | bytes 10485760 | tf_op jit(solution)/shard_map/dot_general | solution.py:1636
  414.7 3.6 convolution_convert_fusion.3
  418.3 60.9 %attend_back.1 = (bf16[2048,384]{1,0:T(8,128)(2,1)}, bf16[256,2048]{1,0:T(8,128)(2,1)}, bf16[4096,128]{1,0:T(8,128)(2,1)}) custom-call(bf16[2048,256]{1,0:T(8,128)(2,1)} %copy-done.5, bf16[2048,128]{1,0:T(8,128)(2,1)} %copy-done.8, bf16[2048,256]{1,0:T(8,128)(2,1)} %convolution_convert_fusion.4.up_ref, f32[2048,256]{1,0:T(8,128)} %copy-done.2, ...), custom_call_target="tpu_custom_call" | custom-call | bytes 1024 | tf_op jit(solution)/shard_map/attend_back/pallas_call | solution.py:1094
  479.2 8.9 %convolution_convert_fusion.2 = bf16[2048,384]{1,0:T(8,128)(2,1)S(1)} fusion(bf16[2048,384]{1,0:T(8,128)(2,1)} %get-tuple-element.85.left, bf16[2048,2048]{1,0:T(8,128)(2,1)} %get-tuple-element.64, f32[2048]{0:T(1024)S(1)} %bitcast.36, f32[2048]{0:T(1024)S(1)} %add_rsqrt_fusion), kind=kOutput, calls=%fused_computation.7 | convolution fusion | flops 3238789120 | bytes 11550720 | tf_op jit(solution)/shard_map/dot_general | solution.py:55
  488.1 1.8 pad_maximum_fusion
  491.1 1.6 convert_element_type.61.refs_1_
  493.5 58.8 %product_scatter.3 = (bf16[256,2048]{1,0:T(8,128)(2,1)}, f32[8,2048]{1,0:T(8,128)}, bf16[128,4096]{1,0:T(8,128)(2,1)}) custom-call(bf16[2048,384]{1,0:T(8,128)(2,1)} %get-tuple-element.85.left, bf16[2048,640]{1,0:T(8,128)(2,1)} %get-tuple-element.66.right, bf16[512,1024]{1,0:T(8,128)(2,1)} %reduce-scatter.7.cloned.1.call-done.refs_0_, ...), custom_call_target="tpu_custom_call" | custom-call | bytes 1024 | tf_op jit(solution)/shard_map/product_scatter/pallas_call | solution.py:671
  552.2 1.3 collective-permute-start.4
  554.5 5.3 final_forms.2
  559.8 19.9 %gain_sum.1 = (f32[8,128]{1,0:T(8,128)}, bf16[128,4096]{1,0:T(8,128)(2,1)}) custom-call(f32[8,2048]{1,0:T(8,128)} %get-tuple-element.93.attn_term_ref, f32[8,2048]{1,0:T(8,128)} %get-tuple-element.94.ffn_term_ref, bf16[512,1024]{1,0:T(8,128)(2,1)} %reduce-scatter.9.cloned.1.call-done.up_ref), custom_call_target="tpu_custom_call" | custom-call | bytes 1024 | tf_op jit(solution)/shard_map/gain_sum/pallas_call | solution.py:1196
  579.7 1.3 slice_bitcast_fusion
  581.2 11.0 %last_swap.1 = (bf16[128,1024]{1,0:T(8,128)(2,1)}, bf16[128,256]{1,0:T(8,128)(2,1)}, bf16[128,256]{1,0:T(8,128)(2,1)}, bf16[1024,128]{1,0:T(8,128)(2,1)}) custom-call(bf16[512,640]{1,0:T(8,128)(2,1)} %reduce-scatter.11.cloned.1.call-done.attn_ref), custom_call_target="tpu_custom_call" | custom-call | bytes 1024 | tf_op jit(solution)/shard_map/last_swap/pallas_call | solution.py:1247
  592.3 5.7 final_forms.3
  (76 shorter events, 16.6 us)
Async XLA Ops:
  7.2 50.1 %copy-start = (bf16[2,256,2048]{2,1,0:T(8,128)(2,1)S(1)}, bf16[2,256,2048]{2,1,0:T(8,128)(2,1)}, u32[]{:S(2)}) copy-start(bf16[2,256,2048]{2,1,0:T(8,128)(2,1)} %own_ref.3) | copy-start | bytes 6291460
  7.2 54.1 %copy-start.15 = (bf16[128]{0:T(256)(128)(2,1)S(1)}, bf16[128]{0:T(256)(128)(2,1)}, u32[]{:S(2)}) copy-start(bf16[128]{0:T(256)(128)(2,1)} %param.12) | copy-start | bytes 772
  7.2 54.1 %copy-start.14 = (bf16[128]{0:T(256)(128)(2,1)S(1)}, bf16[128]{0:T(256)(128)(2,1)}, u32[]{:S(2)}) copy-start(bf16[128]{0:T(256)(128)(2,1)} %param.17) | copy-start | bytes 772
  7.2 239.3 %all-gather.3.cloned.1.call-start = ((), (), s32[]{:S(2)}) async-start(), calls=%async_computation.4 | async-start | bytes 10485760 | tf_op jit(solution)/shard_map/all_gather | solution.py:1605
  57.2 231.7 %all-gather.5.cloned.1.call-start = ((), (), s32[]{:S(2)}) async-start(), calls=%async_computation.5 | async-start | bytes 5242880 | tf_op jit(solution)/shard_map/all_gather | solution.py:1606
  57.3 182.9 %collective-permute-start.1 = (bf16[2,256,2048]{2,1,0:T(8,128)(2,1)S(1)}, bf16[2,256,2048]{2,1,0:T(8,128)(2,1)}, u32[]{:S(2)}, u32[]{:S(2)}) collective-permute-start(bf16[2,256,2048]{2,1,0:T(8,128)(2,1)S(1)} %copy-done), channel_id=1, source_target_pairs={{0,2},{2,0},{4,6},{6,4},{1,3},{3,1},{5,7},{7,5},{8,10},{10,8},{12,... | collective-permute-start | bytes 6291464 | tf_op jit(solution)/shard_map/ppermute | solution.py:1327
  106.4 91.6 %collective-permute-start = (bf16[2,256,2048]{2,1,0:T(8,128)(2,1)S(1)}, bf16[2,256,2048]{2,1,0:T(8,128)(2,1)}, u32[]{:S(2)}, u32[]{:S(2)}) collective-permute-start(bf16[2,256,2048]{2,1,0:T(8,128)(2,1)S(1)} %copy-done), channel_id=1, source_target_pairs={{0,4},{2,6},{4,0},{6,2},{1,5},{3,7},{5,1},{7,3},{8,12},{10,14},{12... | collective-permute-start | bytes 6291464 | tf_op jit(solution)/shard_map/ppermute | solution.py:1325
  107.1 311.2 %reduce-scatter.5.cloned.1.call-start = ((), (), s32[]{:S(2)}) async-start(), calls=%async_computation.6 | async-start | bytes 5242880 | tf_op jit(solution)/shard_map/reduce_scatter | solution.py:1622
  114.7 12.5 %copy-start.3 = (f32[1024,128]{1,0:T(8,128)}, f32[1024,128]{1,0:T(8,128)S(1)}, u32[]{:S(2)}) copy-start(f32[1024,128]{1,0:T(8,128)S(1)} %copy.25.sin_ref) | copy-start | bytes 1572868
  116.8 10.3 %copy-start.4 = (f32[1024,128]{1,0:T(8,128)}, f32[1024,128]{1,0:T(8,128)S(1)}, u32[]{:S(2)}) copy-start(f32[1024,128]{1,0:T(8,128)S(1)} %copy.24.cos_ref) | copy-start | bytes 1572868
  148.1 1.3 copy-start.2
  149.4 1.0 copy-start.5
  150.4 1.0 copy-start.6
  151.3 0.8 copy-start.8
  152.1 43.9 %copy-start.10 = (bf16[256,2048]{1,0:T(8,128)(2,1)S(1)}, bf16[256,2048]{1,0:T(8,128)(2,1)}, u32[]{:S(2)}) copy-start(bf16[256,2048]{1,0:T(8,128)(2,1)} %get-tuple-element.63.block_ref) | copy-start | bytes 3145732
  198.0 1.3 copy-start.9
  198.0 42.2 %collective-permute-start.2 = (bf16[2,256,2048]{2,1,0:T(8,128)(2,1)}, bf16[2,256,2048]{2,1,0:T(8,128)(2,1)}, u32[]{:S(2)}, u32[]{:S(2)}) collective-permute-start(bf16[2,256,2048]{2,1,0:T(8,128)(2,1)} %collective-permute-done.far_ref), channel_id=1, source_target_pairs={{0,2},{2,0},{4,6},{6,4},{1,3},{3,1},{5,7},{7,5},{8,10},{10,8},{12,... | collective-permute-start | bytes 6291464 | tf_op jit(solution)/shard_map/ppermute | solution.py:1327
  243.3 3.2 copy-start.1
  285.7 207.8 %reduce-scatter.7.cloned.1.call-start = ((), (), s32[]{:S(2)}) async-start(), calls=%async_computation.7 | async-start | bytes 5242880 | tf_op jit(solution)/shard_map/reduce_scatter | solution.py:1633
  361.1 198.7 %reduce-scatter.9.cloned.1.call-start = ((), (), s32[]{:S(2)}) async-start(), calls=%async_computation.8 | async-start | bytes 5242880 | tf_op jit(solution)/shard_map/reduce_scatter | solution.py:1635
  407.2 174.0 %reduce-scatter.11.cloned.1.call-start = ((), (), s32[]{:S(2)}) async-start(), calls=%async_computation.9 | async-start | bytes 3276800 | tf_op jit(solution)/shard_map/reduce_scatter | solution.py:1655
  407.4 7.2 %copy-start.7 = (bf16[2048,256]{1,0:T(8,128)(2,1)S(1)}, bf16[2048,256]{1,0:T(8,128)(2,1)}, u32[]{:S(2)}) copy-start(bf16[2048,256]{1,0:T(8,128)(2,1)} %copy-done.6) | copy-start | bytes 3145732
  407.4 7.2 %copy-start.16 = (bf16[2048,2048]{1,0:T(8,128)(2,1)S(1)}, bf16[2048,2048]{1,0:T(8,128)(2,1)}, u32[]{:S(2)}) copy-start(bf16[2048,2048]{1,0:T(8,128)(2,1)} %get-tuple-element.81) | copy-start | bytes 25165828
  479.2 8.9 %copy-start.11 = (bf16[2048,256]{1,0:T(8,128)(2,1)S(1)}, bf16[2048,256]{1,0:T(8,128)(2,1)}, u32[]{:S(2)}) copy-start(bf16[2048,256]{1,0:T(8,128)(2,1)} %convolution_convert_fusion.3) | copy-start | bytes 3145732
  489.9 63.6 %collective-permute-start.3 = (bf16[256,2048]{1,0:T(8,128)(2,1)}, bf16[256,2048]{1,0:T(8,128)(2,1)S(1)}, u32[]{:S(2)}, u32[]{:S(2)}) collective-permute-start(bf16[256,2048]{1,0:T(8,128)(2,1)} %get-tuple-element.83.own_ref), channel_id=1, source_target_pairs={{0,1},{1,0},{2,3},{3,2},{4,5},{5,4},{6,7},{7,6},{8,9},{9,8},{10,11... | collective-permute-start | bytes 3145736 | tf_op jit(solution)/shard_map/ppermute | solution.py:1563
  552.2 27.4 %collective-permute-start.4 = (bf16[256,2048]{1,0:T(8,128)(2,1)}, bf16[256,2048]{1,0:T(8,128)(2,1)S(1)}, u32[]{:S(2)}, u32[]{:S(2)}) collective-permute-start(bf16[256,2048]{1,0:T(8,128)(2,1)} %get-tuple-element.87.own_ref), channel_id=1, source_target_pairs={{0,1},{1,0},{2,3},{3,2},{4,5},{5,4},{6,7},{7,6},{8,9},{9,8},{10,11... | collective-permute-start | bytes 3145736 | tf_op jit(solution)/shard_map/ppermute | solution.py:1563
  553.5 1.0 copy-start.13
  579.7 12.6 %copy-start.12 = (bf16[256,2048]{1,0:T(8,128)(2,1)}, bf16[256,2048]{1,0:T(8,128)(2,1)S(1)}, u32[]{:S(2)}) copy-start(bf16[256,2048]{1,0:T(8,128)(2,1)S(1)} %collective-permute-done.4.other_ref) | copy-start | bytes 3145732
Sparse Core Ops, SparseCore 0:
  57.3 150.9 all-gather.2
  209.9 78.9 all-gather.4
  291.2 75.2 reduce-scatter.4
  368.8 77.2 reduce-scatter.6
  448.2 77.2 reduce-scatter.8
  528.3 52.8 reduce-scatter.10

commit v6 on v5

--- a/solution.py
+++ b/solution.py
@@ -318,11 +318,86 @@
     )
 
 
-def gather_kernel(rows, works, planes, block_ref, *refs):
+class Line:
+    def __init__(self, planes, all_ref, send_sems, recv_sems):
+        self.planes, self.all_ref = planes, all_ref
+        self.send_sems, self.recv_sems = send_sems, recv_sems
+        self.plane = lax.axis_index("dp")
+        self.rows = all_ref.shape[0] // planes
+        self.more, self.fewer = self.plane + 1 < planes, self.plane > 0
+        self.ahead = {"dp": (self.plane + 1) % planes}
+        self.behind = {"dp": (self.plane + planes - 1) % planes}
+
+    def shard(self, whose):
+        return self.all_ref.at[pl.ds(pl.multiple_of(whose * self.rows, self.rows), self.rows)]
+
+    def greet(self, neighbours):
+        barrier = pltpu.get_barrier_semaphore()
+        for target in neighbours:
+            pl.semaphore_signal(barrier, inc=1, device_id=target, device_id_type=MESH_ID)
+        for there, target in ((self.more, self.ahead), (self.fewer, self.behind)):
+
+            @pl.when(there)
+            def _(target=target):
+                pl.semaphore_signal(barrier, inc=1, device_id=target, device_id_type=MESH_ID)
+
+        count = len(neighbours) + self.more.astype(jnp.int32) + self.fewer.astype(jnp.int32)
+        pl.semaphore_wait(barrier, count)
+
+    def hop(self, way, far):
+        spot = self.shard(self.plane - far if way == 0 else self.plane + far)
+        return remote(
+            spot,
+            spot,
+            self.send_sems.at[way, far],
+            self.recv_sems.at[way, far],
+            self.ahead if way == 0 else self.behind,
+        )
+
+    def sends(self, way, far):
+        if way == 0:
+            return (self.plane - far >= 0) & self.more
+        return (self.plane + far < self.planes) & self.fewer
+
+    def gets(self, way, far):
+        if way == 0:
+            return self.plane - 1 - far >= 0
+        return self.plane + 1 + far < self.planes
+
+    def send(self, far):
+        for way in range(2):
+
+            @pl.when(self.sends(way, far))
+            def _(way=way):
+                self.hop(way, far).start()
+
+    def take(self, far):
+        for way in range(2):
+
+            @pl.when(self.gets(way, far))
+            def _(way=way):
+                self.hop(way, far).wait_recv()
+
+        if far + 1 < self.planes - 1:
+            self.send(far + 1)
+
+    def settle(self):
+        for far in range(self.planes - 1):
+            for way in range(2):
+
+                @pl.when(self.sends(way, far))
+                def _(way=way, far=far):
+                    self.hop(way, far).wait_send()
+
+
+def gather_kernel(rows, works, planes, lines, block_ref, *refs):
     if works:
         left_ref, right_ref, all_ref, grad_ref, send_sems, recv_sems, local_sem = refs
     elif planes:
         gains_ref, all_ref, all_gains_ref, send_sems, recv_sems, local_sem, *gain_sems = refs
+    elif lines:
+        shard_ref, all_ref, line_ref, send_sems, recv_sems, local_sem, *line_sems = refs
+        line = Line(lines, line_ref, *line_sems[:2])
     else:
         all_ref, send_sems, recv_sems, local_sem = refs
     side, row, core, near_core, near_side, near_row = place()
@@ -356,7 +431,10 @@
             for turn in range(4)
             if step or turn
         ]
-    greet([near_side] + (targets if planes else [near_core, near_row]))
+    if lines:
+        line.greet([near_side, near_core, near_row])
+    else:
+        greet([near_side] + (targets if planes else [near_core, near_row]))
     copies = []
 
     def send(number, source, target, device):
@@ -383,16 +461,25 @@
     core_own = send(4, block_ref, spot(side, row, core), near_core)
     local = pltpu.make_async_copy(block_ref, spot(side, row, core), local_sem)
     local.start()
+    if lines:
+        own = pltpu.make_async_copy(shard_ref, line.shard(line.plane), line_sems[2])
+        own.start()
+        own.wait()
+        line.send(0)
     work(0, 6)
     side_b.wait_recv()
     away_b = send(5, spot(1 - side, row, core, 1), spot(1 - side, row, core, 1), near_row)
     row_a.wait_recv()
     away_a = send(6, spot(side, 1 - row, core, 0), spot(side, 1 - row, core, 0), near_side)
     work(6, 8)
+    if lines:
+        line.take(0)
     side_a.wait_recv()
     core_side = send(7, spot(1 - side, row, core), spot(1 - side, row, core), near_core)
     row_b.wait_recv()
     core_row = send(8, spot(side, 1 - row, core), spot(side, 1 - row, core), near_core)
+    for far in range(1, lines - 1):
+        line.take(far)
     away_a.wait_recv()
     core_away_a = send(
         9, spot(1 - side, 1 - row, core, 0), spot(1 - side, 1 - row, core, 0), near_core
@@ -407,10 +494,12 @@
         copy.wait_send()
     for copy in gain_copies:
         copy.wait()
+    if lines:
+        line.settle()
     local.wait()
 
 
-def plane_gather(block, number=0, pair=None, gains=None):
+def plane_gather(block, number=0, pair=None, gains=None, shard=None):
     rows, width = block.shape
     anywhere, vmem = pl.BlockSpec(memory_space=pl.ANY), pl.BlockSpec(memory_space=pltpu.VMEM)
     shapes, ins, outs = [jax.ShapeDtypeStruct((8 * rows, width), block.dtype)], [anywhere], [anywhere]
@@ -420,7 +509,14 @@
         ins += [vmem, vmem]
         outs += [vmem]
         operands += pair
-    planes, scratch = 0, []
+    planes, lines, scratch = 0, 0, []
+    if shard is not None:
+        lines = lax.axis_size("dp")
+        shapes.append(jax.ShapeDtypeStruct((lines * shard.shape[0], shard.shape[1]), shard.dtype))
+        ins += [anywhere]
+        outs += [vmem]
+        operands += [shard]
+        scratch = [pltpu.SemaphoreType.DMA((2, lines - 1))] * 2 + [pltpu.SemaphoreType.DMA]
     if gains is not None:
         planes = lax.axis_size("dp")
         shapes.append(jax.ShapeDtypeStruct((4 * planes,) + gains.shape, gains.dtype))
@@ -429,7 +525,7 @@
         operands += [gains]
         scratch = [pltpu.SemaphoreType.DMA((4 * planes - 1,))] * 2 + [pltpu.SemaphoreType.DMA]
     return pl.pallas_call(
-        functools.partial(gather_kernel, rows, 8 if pair is not None else 0, planes),
+        functools.partial(gather_kernel, rows, 8 if pair is not None else 0, planes, lines),
         out_shape=tuple(shapes),
         in_specs=ins,
         out_specs=tuple(outs),
@@ -517,7 +613,12 @@
     def make(chip, part, first=False):
         a, b = chips[chip]
         start = pl.multiple_of((a * 4 + b * 2) * rows, 2 * rows)
-        value = matmul_nt(left_of(chip, start), right_of(pl.ds(part * wide, wide)))
+        left, value, first_col = left_of(chip, start), None, 0
+        for right in right_of(pl.ds(part * wide, wide)):
+            last_col = first_col + right.shape[1]
+            term = matmul_nt(left[:, first_col:last_col], right)
+            value = term if value is None else value + term
+            first_col = last_col
         made[chip, part, 0] = value[:rows].astype(BF16)
         made[chip, part, 1] = value[rows:].astype(BF16)
         if first:
@@ -640,7 +741,7 @@
         return left[pl.ds(start, 2 * rows), :]
 
     def right_of(at):
-        return right[at, columns]
+        return [right[at, columns]]
 
     for step in scatter_steps(rows, left_of, right_of, out_ref, scratch, swap=swap, late=late):
         step()
@@ -692,6 +793,7 @@
     twin_far_ref,
     gate_slope_ref,
     up_slope_ref,
+    down_lead_ref,
     down_ref,
     right_ref,
     value_ref,
@@ -704,6 +806,8 @@
     gate_ref,
     up_ref,
     out_ref,
+    weight,
+    weight_sems,
     cots,
     gate_slopes,
     up_slopes,
@@ -713,7 +817,8 @@
     *scratch,
 ):
     side, row, core, *_ = place()
-    units = down_ref.shape[1]
+    lead = down_lead_ref.shape[1]
+    units = lead + down_ref.shape[1]
     turns = (3, 1, 2, 0)
     chips = ((side, row), (1 - side, row), (side, 1 - row), (1 - side, 1 - row))
     starts = [pl.multiple_of((a * 4 + b * 2) * rows, 2 * rows) for a, b in chips]
@@ -748,6 +853,11 @@
             for which, target in enumerate((gate_ref, up_ref))
         ]
 
+    joins = [
+        pltpu.make_async_copy(source, weight.at[:, pl.ds(first, source.shape[1])], weight_sems.at[at])
+        for at, (source, first) in enumerate(((down_lead_ref, 0), (down_ref, lead)))
+    ]
+
     def start(copies):
         for copy in copies:
             copy.start()
@@ -763,6 +873,7 @@
             return lefts[slot]
         stored.append(chip)
         if turn == 0:
+            start(joins)
             start(fetch(0))
         if turn == 1:
             start(fetch(2))
@@ -770,18 +881,20 @@
             start(fetch(3))
         if turn == 0:
             start(fetch(1))
+        if turn == 0:
+            wait(joins)
         wait(fetch(turn))
         if turn > 1:
             wait(store(turn - 2))
         cot = cots[slot].reshape(2 * rows, cots.shape[3])
-        grad = jnp.dot(cot, down_ref[...], preferred_element_type=F32)
+        grad = jnp.dot(cot, weight[...], preferred_element_type=F32)
         lefts[slot, :, :units] = (grad * gate_slopes[slot].astype(F32)).astype(BF16)
         lefts[slot, :, units:] = (grad * up_slopes[slot].astype(F32)).astype(BF16)
         start(store(turn))
         return lefts[slot]
 
     def right_of(at):
-        return right_ref[at, :]
+        return [right_ref[at, :]]
 
     for step in scatter_steps(rows, left_of, right_of, out_ref, scratch):
         step()
@@ -792,7 +905,7 @@
     wait(store(3))
 
 
-def ffn_back(number, cots, gate_slope, up_slope, down_w, gate_up, norm):
+def ffn_back(number, cots, gate_slope, up_slope, down_lead, down_w, gate_up, norm):
     total, units = gate_slope.shape
     width = down_w.shape[0]
     rows = total // 8
@@ -807,10 +920,12 @@
             jax.ShapeDtypeStruct((total, units), BF16),
             jax.ShapeDtypeStruct((total, units), BF16),
         ),
-        in_specs=[anywhere] * 6 + [vmem] * 6,
+        in_specs=[anywhere] * 8 + [vmem] * 5,
         out_specs=(vmem, vmem, vmem, anywhere, anywhere),
         scratch_shapes=[
             pltpu.VMEM((rows, width), F32),
+            pltpu.VMEM((width, units), BF16),
+            pltpu.SemaphoreType.DMA((2,)),
             pltpu.VMEM((2, 2, rows, width), BF16),
             pltpu.VMEM((2, 2 * rows, units), BF16),
             pltpu.VMEM((2, 2 * rows, units), BF16),
@@ -824,7 +939,7 @@
         ),
         cost_estimate=pl.CostEstimate(flops=0, bytes_accessed=1024, transcendentals=0),
         name="ffn_back",
-    )(*cots, gate_slope, up_slope, down_w, gate_up, *norm)
+    )(*cots, gate_slope, up_slope, down_lead, down_w, gate_up, *norm)
 
 
 def ffn_kernel(in_ref, w_ref, product_ref, gate_slope_ref, up_slope_ref):
@@ -953,7 +1068,7 @@
             pl.BlockSpec(block, lambda s, h: (s, 0)),
             pl.BlockSpec(block, lambda s, h: (s, h)),
         ),
-        compiler_params=pltpu.CompilerParams(vmem_limit_bytes=48 * 1024 * 1024),
+        compiler_params=pltpu.CompilerParams(vmem_limit_bytes=60 * 1024 * 1024),
         cost_estimate=pl.CostEstimate(
             flops=8 * rows * length * 128 * pairs,
             bytes_accessed=rows * pairs * 128 * 12,
@@ -973,6 +1088,7 @@
     cos_ref,
     sin_ref,
     left_ref,
+    right_lead_ref,
     right_ref,
     hidden_ref,
     in_ref,
@@ -993,7 +1109,7 @@
     across, along, forward, own, finish = scatter_steps(
         rows,
         lambda chip, start: left_ref[pl.ds(start, 2 * rows), :],
-        lambda at: right_ref[at, :],
+        lambda at: [right_lead_ref[at, :], right_ref[at, :]],
         ffn_ref,
         scratch[:-3],
         swap=(in_ref, swapped, *scratch[-3:]),
@@ -1084,7 +1200,7 @@
 
 
 def attend_back(
-    number, queries, keyvals, upstream, logs, cosine, signed, seqs, left, right, hidden, swap
+    number, queries, keyvals, upstream, logs, cosine, signed, seqs, left, lead, right, hidden, swap
 ):
     total, width = queries.shape
     length = total // seqs
@@ -1098,7 +1214,7 @@
             jax.ShapeDtypeStruct(hidden.shape, BF16),
             jax.ShapeDtypeStruct((4 * swap.shape[1], deep), BF16),
         ),
-        in_specs=[vmem] * 9 + [pl.BlockSpec(memory_space=pl.ANY)],
+        in_specs=[vmem] * 10 + [pl.BlockSpec(memory_space=pl.ANY)],
         out_specs=(vmem, vmem, vmem),
         scratch_shapes=[
             pltpu.VMEM((length, 128), F32),
@@ -1112,7 +1228,7 @@
         ),
         cost_estimate=pl.CostEstimate(flops=0, bytes_accessed=1024, transcendentals=0),
         name="attend_back",
-    )(queries, keyvals, upstream, logs, cosine, signed, left, right, hidden, swap)
+    )(queries, keyvals, upstream, logs, cosine, signed, left, lead, right, hidden, swap)
 
 
 def gain_kernel(
@@ -1325,16 +1441,21 @@
     far = lax.ppermute(after(block, earlier), "ctx", [(0, 2), (1, 3), (2, 0), (3, 1)])
     far = after(far, later)
     twin, twin_far = lax.ppermute(block, "ctx", cores), lax.ppermute(far, "ctx", cores)
+    return block, far, twin, twin_far
+
+
+def lay_along(parts):
+    seqs, span, width = parts[0].shape
     whole = pl.pallas_call(
         lay_kernel,
-        out_shape=jax.ShapeDtypeStruct((seqs, 4 * span, width), block.dtype),
+        out_shape=jax.ShapeDtypeStruct((seqs, 4 * span, width), parts[0].dtype),
         in_specs=[pl.BlockSpec(memory_space=pl.ANY)] * 4,
         out_specs=pl.BlockSpec(memory_space=pltpu.VMEM),
         scratch_shapes=[pltpu.SemaphoreType.DMA((4,))],
         compiler_params=pltpu.CompilerParams(vmem_limit_bytes=24 * 1024 * 1024),
         name="lay",
-    )(block, far, twin, twin_far)
-    return whole.reshape(seqs * 4 * span, width), (block, far, twin, twin_far)
+    )(*parts)
+    return whole.reshape(seqs * 4 * span, width)
 
 
 def open_kernel(
@@ -1348,6 +1469,7 @@
     down_in_ref,
     attn_ref,
     gate_up_ref,
+    down_lead_ref,
     down_own_ref,
     key_in,
     value_in,
@@ -1407,17 +1529,20 @@
     start = 0
     for source in (q_ref, kv_ref, wide_ref):
         cols = source.shape[1] // 4
-        moves.append((source, cols, attn_ref.at[pl.ds(base + mine, rows), pl.ds(start, cols)]))
+        target = attn_ref.at[pl.ds(base + mine, rows), pl.ds(start, cols)]
+        moves.append((source, cols, 0, cols, target))
         start += cols
     for which, source in enumerate((gate_ref, up_ref)):
-        lanes = pl.ds(which * units, units)
-        moves.append((source, units, gate_up_ref.at[pl.ds(mine, rows), lanes]))
-    moves.append((down_ref, units, down_own_ref.at[pl.ds(mine, rows)]))
+        target = gate_up_ref.at[pl.ds(mine, rows), pl.ds(which * units, units)]
+        moves.append((source, units, 0, units, target))
+    lead = down_lead_ref.shape[1]
+    moves.append((down_ref, units, 0, lead, down_lead_ref.at[pl.ds(mine, rows)]))
+    moves.append((down_ref, units, lead, units - lead, down_own_ref.at[pl.ds(mine, rows)]))
     away, local = [], []
-    for which, (source, cols, target) in enumerate(moves):
-
-        def columns(index, source=source, cols=cols):
-            return source.at[:, pl.ds(pl.multiple_of(index * cols, cols), cols)]
+    for which, (source, stride, shift, cols, target) in enumerate(moves):
+
+        def columns(index, source=source, stride=stride, shift=shift, cols=cols):
+            return source.at[:, pl.ds(pl.multiple_of(index * stride + shift, 128), cols)]
 
         away.append(
             [
@@ -1484,7 +1609,7 @@
     for part in range(4):
         there = slice(part * units, (part + 1) * units)
         down_ref[:, there] = jnp.transpose(down_in[there, :].astype(F32)).astype(BF16)
-    for copy in away[5] + [local[5]]:
+    for copy in away[5] + away[6] + [local[5], local[6]]:
         copy.start()
     for far in range(planes - 1):
         for part in range(2):
@@ -1504,7 +1629,7 @@
                 def _(way=way, far=far, part=part):
                     hop(way, far, part).wait_send()
 
-    for which in range(6):
+    for which in range(7):
         if which > 2:
             local[which].wait()
             for copy in away[which]:
@@ -1513,7 +1638,7 @@
             copy.wait_send()
 
 
-def open_weights(query, key, value, out, gate, up, down):
+def open_weights(query, key, value, out, gate, up, down, lead):
     planes = lax.axis_size("dp")
     rows = query.shape[0]
     cols = (query.shape[1] + 2 * key.shape[1] + out.shape[0]) // 4
@@ -1524,10 +1649,11 @@
         out_shape=(
             jax.ShapeDtypeStruct((planes * 4 * rows, cols), BF16),
             jax.ShapeDtypeStruct((4 * rows, 2 * units), BF16),
-            jax.ShapeDtypeStruct((4 * rows, units), BF16),
+            jax.ShapeDtypeStruct((4 * rows, lead), BF16),
+            jax.ShapeDtypeStruct((4 * rows, units - lead), BF16),
         ),
         in_specs=[anywhere] * 7,
-        out_specs=(vmem, anywhere, anywhere),
+        out_specs=(vmem, anywhere, anywhere, anywhere),
         scratch_shapes=[
             pltpu.VMEM(key.shape, BF16),
             pltpu.VMEM(value.shape, BF16),
@@ -1537,9 +1663,9 @@
             pltpu.VMEM((rows, out.shape[0]), BF16),
             pltpu.VMEM((rows, down.shape[0]), BF16),
             pltpu.SemaphoreType.DMA((4,)),
-            pltpu.SemaphoreType.DMA((6, 3)),
-            pltpu.SemaphoreType.DMA((6, 3)),
-            pltpu.SemaphoreType.DMA((6,)),
+            pltpu.SemaphoreType.DMA((7, 3)),
+            pltpu.SemaphoreType.DMA((7, 3)),
+            pltpu.SemaphoreType.DMA((7,)),
             pltpu.SemaphoreType.DMA((2, planes - 1, 2)),
             pltpu.SemaphoreType.DMA((2, planes - 1, 2)),
         ],
@@ -1590,7 +1716,9 @@
     sine = jnp.sin(theta)
     signed = jnp.tile(jnp.concatenate([-sine, sine], axis=1), (1, 2))
 
-    attn_w, gate_up, down_own = open_weights(w_query, w_key, w_value, w_out, w_gate, w_up, w_down)
+    attn_w, gate_up, lead_own, down_own = open_weights(
+        w_query, w_key, w_value, w_out, w_gate, w_up, w_down, w_down.shape[0] // parts // 8
+    )
     qkv_cols = q_cols + 2 * kv_cols
     w_qkv = attn_w[:, :qkv_cols]
     w_out_t = attn_w[:, qkv_cols:]
@@ -1614,10 +1742,11 @@
     hidden = inputs_f + product_scatter(1, attended, attn_w, qkv_cols, q_cols)[0]
     factor_two = rms_factor(hidden)
     normed_own = (hidden * factor_two * gain_two).astype(BF16)
-    normed_two = plane_gather(normed_own)[0]
-    all_cot, cots = along_ctx(cotangent, all_in, hidden)
+    normed_two, down_lead = plane_gather(normed_own, shard=lead_own)
+    cots = along_ctx(cotangent, all_in, hidden)
 
     product, gate_slope, up_slope = ffn(normed_two, gate_up)
+    all_cot = lay_along((after(cots[0], product),) + cots[1:])
     down_grad = matmul_t(all_cot, product).astype(BF16)
     down_sum = lax.psum_scatter(down_grad, "dp", scatter_dimension=0, tiled=True)
     hidden_grad, hidden_own, ffn_term, gate_grad, up_grad = ffn_back(
@@ -1625,6 +1754,7 @@
         cots,
         after(gate_slope, down_grad),
         up_slope,
+        down_lead,
         down_w,
         gate_up,
         (hidden, factor_two, gain_two[None], own_cot),
@@ -1645,6 +1775,7 @@
         signed,
         seqs,
         product,
+        down_lead,
         down_w,
         hidden,
         down_sum,

time: 613 us -> 610 us (level)
  Pallas kernels: 493 us -> 500 us
  local copies, waits for them, and re-layouts: 17.4 us -> 10.6 us
    unnamed x34 -> x22, local copies, waits for them, and re-layouts: 9.4 us -> 2.98 us
  transfers between devices with their start and end apart: 11 -> 11, of which waited for: 2 -> 1; matrix products, arithmetic and copies ran while one was open for 13% -> 13% of each run, Pallas kernels for 70% -> 72%
where the time goes in v6:
time: 610 us; the launch traced here: 603 us
  Pallas kernels  500 us (82%)
  matrix products  54.6 us (9%)
  other arithmetic  15.3 us (3%)
  between operations  14.9 us (2%)
  local copies, waits for them, and re-layouts  10.6 us (2%)
    pallas_call x3, Pallas kernels, plane_gather(): pl.pallas_call(functools.partial(gather_kernel, rows, 8 if pair is not No...  133 us
    pallas_call x2, Pallas kernels, product_scatter(): pl.pallas_call(functools.partial(scatter_kernel, rows, swap is not None,...  103 us
    pallas_call x1, Pallas kernels, attend_back(): pl.pallas_call(functools.partial(attend_back_kernel, seqs, rows), out_sha...  61.4 us
    pallas_call x1, Pallas kernels, ffn_back(): pl.pallas_call(functools.partial(ffn_back_kernel, rows), out_shape=(jax.S...  58.9 us
    pallas_call x1, Pallas kernels, open_weights(): pl.pallas_call(functools.partial(open_kernel, planes), out_shape=(jax.Sha...  50 us
    dot_general x4, matrix products, matmul_t(): lax.dot_general(left_op, right_op, (((0,), (0,)), ((), ())), preferred_el...  37.4 us
    pallas_call x1, Pallas kernels, ffn(): pl.pallas_call(ffn_kernel, grid=(total // rows,), out_shape=(jax.ShapeDty...  25.2 us
    pallas_call x1, Pallas kernels, attend(): pl.pallas_call(functools.partial(attend_kernel, length), grid=(seqs, pair...  21.6 us
  transfers between devices with their start and end apart: 11, of which 1 were waited for; matrix products, arithmetic and copies ran while one was open for 13% of the time, Pallas kernels for 72%

profile of v6, /device:TPU:0, one launch (start us, length us, event | category | flops | bytes accessed | tf_op | source)
XLA Modules:
  0.0 602.8 jit_solution(13764913366783495798)
XLA Ops:
  7.3 50.0 %open_weights.1 = (bf16[2048,640]{1,0:T(8,128)(2,1)}, bf16[512,2048]{1,0:T(8,128)(2,1)}, bf16[512,128]{1,0:T(8,128)(2,1)}, bf16[512,896]{1,0:T(8,128)(2,1)}) custom-call(bf16[128,1024]{1,0:T(8,128)(2,1)} %q_ref.1, bf16[128,256]{1,0:T(8,128)(2,1)} %key_ref.1, bf16[128,256]{1,0:T(8,128)(2,1)} %value_ref.1, bf16[1024,128]{1,0:T(8,128)(2,1)} %out_ref.1, ...), custom_call_target="tpu_custom_call" | custom-call | bytes 1024 | tf_op jit(solution)/shard_map/open_weights/pallas_call | solution.py:1647
  57.3 1.6 collective-permute-start.1
  58.9 2.4 multiply_reduce_fusion
  62.0 44.4 %plane_gather.3 = (bf16[2048,2048]{1,0:T(8,128)(2,1)}, f32[16,8,128]{2,1,0:T(8,128)}) custom-call(bf16[256,2048]{1,0:T(8,128)(2,1)} %get-tuple-element.67.block_ref, f32[8,128]{1,0:T(8,128)} %maximum_convert_fusion.refs_0_), custom_call_target="tpu_custom_call" | custom-call | bytes 1024 | tf_op jit(solution)/shard_map/plane_gather/pallas_call | solution.py:527
  107.2 5.2 fusion
  112.3 1.5 slice_bitcast_fusion.3
  116.5 10.1 %fusion.4.q_ref.kv_ref = f32[2048,384]{1,0:T(8,128)} fusion(bf16[2048,2048]{1,0:T(8,128)(2,1)} %get-tuple-element.68, f32[2048]{0:T(1024)S(1)} %bitcast.35, f32[2048]{0:T(1024)S(1)} %add_rsqrt_fusion, bf16[2048,640]{1,0:T(8,128)(2,1)} %get-tuple-element.70.right), kind=kOutput, calls=%fused_computation.11 | convolution fusion | flops 3238002688 | bytes 13123584 | tf_op jit(solution)/shard_map/dot_general | solution.py:1738
  126.6 21.6 %attend.1 = (bf16[2048,256]{1,0:T(8,128)(2,1)}, bf16[2048,256]{1,0:T(8,128)(2,1)}, bf16[2048,128]{1,0:T(8,128)(2,1)}, f32[2048,256]{1,0:T(8,128)}) custom-call(f32[2048,384]{1,0:T(8,128)} %fusion.4.q_ref.kv_ref, f32[2048,384]{1,0:T(8,128)} %fusion.4.q_ref.kv_ref, f32[1024,128]{1,0:T(8,128)} %copy.24.cos_ref, f32[1024,128]{1,0:T(8,128)} %copy.25.sin_ref), custom_call_target="tpu_custom_call" | custom-call | flops 4294967296 | bytes 6291456 | tf_op jit(solution)/shard_map/attend/pallas_call | solution.py:1050
  148.2 43.9 %product_scatter.2 = f32[256,2048]{1,0:T(8,128)} custom-call(bf16[2048,256]{1,0:T(8,128)(2,1)} %get-tuple-element.74.left, bf16[2048,640]{1,0:T(8,128)(2,1)} %get-tuple-element.70.right), custom_call_target="tpu_custom_call" | custom-call | bytes 1024 | tf_op jit(solution)/shard_map/product_scatter/pallas_call | solution.py:772
  192.1 1.9 multiply_reduce_fusion.1
  195.4 1.2 multiply_convert_fusion.block_ref
  196.6 42.9 %plane_gather.4 = (bf16[2048,2048]{1,0:T(8,128)(2,1)}, bf16[2048,128]{1,0:T(8,128)(2,1)}) custom-call(bf16[256,2048]{1,0:T(8,128)(2,1)} %multiply_convert_fusion.block_ref, bf16[512,128]{1,0:T(8,128)(2,1)} %get-tuple-element.76.refs_0_), custom_call_target="tpu_custom_call" | custom-call | bytes 1024 | tf_op jit(solution)/shard_map/plane_gather/pallas_call | solution.py:527
  239.5 25.2 %ffn.1 = (bf16[2048,1024]{1,0:T(8,128)(2,1)}, bf16[2048,1024]{1,0:T(8,128)(2,1)}, bf16[2048,1024]{1,0:T(8,128)(2,1)}) custom-call(bf16[2048,2048]{1,0:T(8,128)(2,1)} %get-tuple-element.77.in_ref.refs_0_, bf16[2048,2048]{1,0:T(8,128)(2,1)} %all-gather.3.cloned.1.call-done.w_ref.right_ref), custom_call_target="tpu_custom_call" | custom-call | bytes 1024 | tf_op jit(solution)/shard_map/ffn/pallas_call | solution.py:965
  264.8 3.3 lay.1
  268.9 10.9 %convolution_convert_fusion.1 = bf16[2048,1024]{1,0:T(8,128)(2,1)} fusion(bf16[2048,2048]{1,0:T(8,128)(2,1)S(1)} %bitcast.30, bf16[2048,1024]{1,0:T(8,128)(2,1)S(1)} %copy-done.3), kind=kOutput, calls=%fused_computation.6 | convolution fusion | flops 8592031744 | bytes 16777216 | tf_op jit(solution)/shard_map/dot_general | solution.py:55
  281.7 2.3 all-gather.5.cloned.1.call-done.down_ref.right_ref
  284.0 58.9 %ffn_back.1 = (f32[256,2048]{1,0:T(8,128)}, bf16[256,2048]{1,0:T(8,128)(2,1)}, f32[8,2048]{1,0:T(8,128)}, bf16[2048,1024]{1,0:T(8,128)(2,1)}, bf16[2048,1024]{1,0:T(8,128)(2,1)}) custom-call(bf16[2,256,2048]{2,1,0:T(8,128)(2,1)} %own_ref.2, bf16[2,256,2048]{2,1,0:T(8,128)(2,1)} %collective-permute-done.far_ref, ...), custom_call_target="tpu_custom_call" | custom-call | bytes 1024 | tf_op jit(solution)/shard_map/ffn_back/pallas_call | solution.py:914
  342.9 14.0 %convolution_convert_fusion = bf16[2048,1024]{1,0:T(8,128)(2,1)} fusion(bf16[2048,2048]{1,0:T(8,128)(2,1)} %get-tuple-element.77.in_ref.refs_0_, bf16[2048,1024]{1,0:T(8,128)(2,1)} %get-tuple-element.86), kind=kOutput, calls=%fused_computation.5 | convolution fusion | flops 8592031744 | bytes 16777216 | tf_op jit(solution)/shard_map/dot_general | solution.py:55
  357.0 45.8 %plane_gather.5 = (bf16[2048,2048]{1,0:T(8,128)(2,1)}, bf16[2048,1024]{1,0:T(8,128)(2,1)}) custom-call(bf16[256,2048]{1,0:T(8,128)(2,1)} %get-tuple-element.87.block_ref, bf16[2048,2048]{1,0:T(8,128)(2,1)} %get-tuple-element.77.in_ref.refs_0_, bf16[2048,1024]{1,0:T(8,128)(2,1)} %get-tuple-element.88.refs_1_), custom_call_target="tpu_custom_call" | custom-call | bytes 1024 | tf_op jit(solution)/shard_map/plane_gather/pallas_call | solution.py:527
  403.0 7.1 %convolution_convert_fusion.4.up_ref = bf16[2048,256]{1,0:T(8,128)(2,1)} fusion(bf16[2048,2048]{1,0:T(8,128)(2,1)} %get-tuple-element.89, bf16[2048,640]{1,0:T(8,128)(2,1)} %get-tuple-element.70.right), kind=kOutput, calls=%fused_computation.10 | convolution fusion | flops 2148007936 | bytes 10485760 | tf_op jit(solution)/shard_map/dot_general | solution.py:1766
  410.1 3.6 convolution_convert_fusion.3
  413.8 61.4 %attend_back.1 = (bf16[2048,384]{1,0:T(8,128)(2,1)}, bf16[256,2048]{1,0:T(8,128)(2,1)}, bf16[4096,128]{1,0:T(8,128)(2,1)}) custom-call(bf16[2048,256]{1,0:T(8,128)(2,1)} %get-tuple-element.71.q_ref, bf16[2048,128]{1,0:T(8,128)(2,1)} %get-tuple-element.72.kv_ref, bf16[2048,256]{1,0:T(8,128)(2,1)} %convolution_convert_fusion.4.up_ref, ...), custom_call_target="tpu_custom_call" | custom-call | bytes 1024 | tf_op jit(solution)/shard_map/attend_back/pallas_call | solution.py:1210
  475.2 8.9 %convolution_convert_fusion.2 = bf16[2048,384]{1,0:T(8,128)(2,1)S(1)} fusion(bf16[2048,384]{1,0:T(8,128)(2,1)} %get-tuple-element.93.left, bf16[2048,2048]{1,0:T(8,128)(2,1)} %get-tuple-element.68, f32[2048]{0:T(1024)S(1)} %bitcast.36, f32[2048]{0:T(1024)S(1)} %add_rsqrt_fusion), kind=kOutput, calls=%fused_computation.7 | convolution fusion | flops 3238789120 | bytes 11550720 | tf_op jit(solution)/shard_map/dot_general | solution.py:55
  484.1 1.8 pad_maximum_fusion
  485.9 1.2 collective-permute-start.3
  487.1 1.6 convert_element_type.61.refs_1_
  489.5 58.8 %product_scatter.3 = (bf16[256,2048]{1,0:T(8,128)(2,1)}, f32[8,2048]{1,0:T(8,128)}, bf16[128,4096]{1,0:T(8,128)(2,1)}) custom-call(bf16[2048,384]{1,0:T(8,128)(2,1)} %get-tuple-element.93.left, bf16[2048,640]{1,0:T(8,128)(2,1)} %get-tuple-element.70.right, bf16[512,1024]{1,0:T(8,128)(2,1)} %reduce-scatter.7.cloned.1.call-done.refs_0_, ...), custom_call_target="tpu_custom_call" | custom-call | bytes 1024 | tf_op jit(solution)/shard_map/product_scatter/pallas_call | solution.py:772
  550.5 5.3 final_forms.2
  555.8 21.4 %gain_sum.1 = (f32[8,128]{1,0:T(8,128)}, bf16[128,4096]{1,0:T(8,128)(2,1)}) custom-call(f32[8,2048]{1,0:T(8,128)} %get-tuple-element.101.attn_term_ref, f32[8,2048]{1,0:T(8,128)} %get-tuple-element.102.ffn_term_ref, bf16[512,1024]{1,0:T(8,128)(2,1)} %reduce-scatter.9.cloned.1.call-done.up_ref), custom_call_target="tpu_custom_call" | custom-call | bytes 1024 | tf_op jit(solution)/shard_map/gain_sum/pallas_call | solution.py:1312
  577.2 1.3 slice_bitcast_fusion
  578.5 11.2 %last_swap.1 = (bf16[128,1024]{1,0:T(8,128)(2,1)}, bf16[128,256]{1,0:T(8,128)(2,1)}, bf16[128,256]{1,0:T(8,128)(2,1)}, bf16[1024,128]{1,0:T(8,128)(2,1)}) custom-call(bf16[512,640]{1,0:T(8,128)(2,1)} %reduce-scatter.11.cloned.1.call-done.attn_ref), custom_call_target="tpu_custom_call" | custom-call | bytes 1024 | tf_op jit(solution)/shard_map/last_swap/pallas_call | solution.py:1363
  589.7 5.7 final_forms.3
  (64 shorter events, 11.7 us)
Async XLA Ops:
  7.2 50.1 %copy-start = (bf16[2,256,2048]{2,1,0:T(8,128)(2,1)S(1)}, bf16[2,256,2048]{2,1,0:T(8,128)(2,1)}, u32[]{:S(2)}) copy-start(bf16[2,256,2048]{2,1,0:T(8,128)(2,1)} %own_ref.2) | copy-start | bytes 6291460
  7.2 54.2 %copy-start.9 = (bf16[128]{0:T(256)(128)(2,1)S(1)}, bf16[128]{0:T(256)(128)(2,1)}, u32[]{:S(2)}) copy-start(bf16[128]{0:T(256)(128)(2,1)} %param.12) | copy-start | bytes 772
  7.2 54.2 %copy-start.8 = (bf16[128]{0:T(256)(128)(2,1)S(1)}, bf16[128]{0:T(256)(128)(2,1)}, u32[]{:S(2)}) copy-start(bf16[128]{0:T(256)(128)(2,1)} %param.17) | copy-start | bytes 772
  7.2 232.3 %all-gather.3.cloned.1.call-start = ((), (), s32[]{:S(2)}) async-start(), calls=%async_computation.4 | async-start | bytes 10485760 | tf_op jit(solution)/shard_map/all_gather | solution.py:1733
  57.3 226.7 %all-gather.5.cloned.1.call-start = ((), (), s32[]{:S(2)}) async-start(), calls=%async_computation.5 | async-start | bytes 4587520 | tf_op jit(solution)/shard_map/all_gather | solution.py:1734
  57.3 207.4 %collective-permute-start.1 = (bf16[2,256,2048]{2,1,0:T(8,128)(2,1)S(1)}, bf16[2,256,2048]{2,1,0:T(8,128)(2,1)}, u32[]{:S(2)}, u32[]{:S(2)}) collective-permute-start(bf16[2,256,2048]{2,1,0:T(8,128)(2,1)S(1)} %copy-done), channel_id=1, source_target_pairs={{0,2},{2,0},{4,6},{6,4},{1,3},{3,1},{5,7},{7,5},{8,10},{10,8},{12,... | collective-permute-start | bytes 6291464 | tf_op jit(solution)/shard_map/ppermute | solution.py:1443
  106.4 87.7 %collective-permute-start = (bf16[2,256,2048]{2,1,0:T(8,128)(2,1)S(1)}, bf16[2,256,2048]{2,1,0:T(8,128)(2,1)}, u32[]{:S(2)}, u32[]{:S(2)}) collective-permute-start(bf16[2,256,2048]{2,1,0:T(8,128)(2,1)S(1)} %copy-done), channel_id=1, source_target_pairs={{0,4},{2,6},{4,0},{6,2},{1,5},{3,7},{5,1},{7,3},{8,12},{10,14},{12... | collective-permute-start | bytes 6291464 | tf_op jit(solution)/shard_map/ppermute | solution.py:1441
  107.1 306.6 %reduce-scatter.5.cloned.1.call-start = ((), (), s32[]{:S(2)}) async-start(), calls=%async_computation.6 | async-start | bytes 5242880 | tf_op jit(solution)/shard_map/reduce_scatter | solution.py:1751
  148.2 43.9 %copy-start.2 = (bf16[256,2048]{1,0:T(8,128)(2,1)S(1)}, bf16[256,2048]{1,0:T(8,128)(2,1)}, u32[]{:S(2)}) copy-start(bf16[256,2048]{1,0:T(8,128)(2,1)} %get-tuple-element.67.block_ref) | copy-start | bytes 3145732
  194.1 1.3 copy-start.1
  194.1 70.7 %collective-permute-start.2 = (bf16[2,256,2048]{2,1,0:T(8,128)(2,1)}, bf16[2,256,2048]{2,1,0:T(8,128)(2,1)}, u32[]{:S(2)}, u32[]{:S(2)}) collective-permute-start(bf16[2,256,2048]{2,1,0:T(8,128)(2,1)} %collective-permute-done.far_ref), channel_id=1, source_target_pairs={{0,2},{2,0},{4,6},{6,4},{1,3},{3,1},{5,7},{7,5},{8,10},{10,8},{12,... | collective-permute-start | bytes 6291464 | tf_op jit(solution)/shard_map/ppermute | solution.py:1443
  264.8 4.1 copy-start.3
  279.8 209.7 %reduce-scatter.7.cloned.1.call-start = ((), (), s32[]{:S(2)}) async-start(), calls=%async_computation.7 | async-start | bytes 5242880 | tf_op jit(solution)/shard_map/reduce_scatter | solution.py:1763
  356.9 198.9 %reduce-scatter.9.cloned.1.call-start = ((), (), s32[]{:S(2)}) async-start(), calls=%async_computation.8 | async-start | bytes 5242880 | tf_op jit(solution)/shard_map/reduce_scatter | solution.py:1765
  402.8 175.7 %reduce-scatter.11.cloned.1.call-start = ((), (), s32[]{:S(2)}) async-start(), calls=%async_computation.9 | async-start | bytes 3276800 | tf_op jit(solution)/shard_map/reduce_scatter | solution.py:1786
  403.0 7.1 %copy-start.5 = (bf16[2048,256]{1,0:T(8,128)(2,1)S(1)}, bf16[2048,256]{1,0:T(8,128)(2,1)}, u32[]{:S(2)}) copy-start(bf16[2048,256]{1,0:T(8,128)(2,1)} %get-tuple-element.74.left) | copy-start | bytes 3145732
  403.0 7.1 %copy-start.10 = (bf16[2048,2048]{1,0:T(8,128)(2,1)S(1)}, bf16[2048,2048]{1,0:T(8,128)(2,1)}, u32[]{:S(2)}) copy-start(bf16[2048,2048]{1,0:T(8,128)(2,1)} %get-tuple-element.89) | copy-start | bytes 25165828
  475.2 8.9 %copy-start.4 = (bf16[2048,256]{1,0:T(8,128)(2,1)S(1)}, bf16[2048,256]{1,0:T(8,128)(2,1)}, u32[]{:S(2)}) copy-start(bf16[2048,256]{1,0:T(8,128)(2,1)} %convolution_convert_fusion.3) | copy-start | bytes 3145732
  485.9 63.6 %collective-permute-start.3 = (bf16[256,2048]{1,0:T(8,128)(2,1)}, bf16[256,2048]{1,0:T(8,128)(2,1)S(1)}, u32[]{:S(2)}, u32[]{:S(2)}) collective-permute-start(bf16[256,2048]{1,0:T(8,128)(2,1)} %get-tuple-element.91.own_ref), channel_id=1, source_target_pairs={{0,1},{1,0},{2,3},{3,2},{4,5},{5,4},{6,7},{7,6},{8,9},{9,8},{10,11... | collective-permute-start | bytes 3145736 | tf_op jit(solution)/shard_map/ppermute | solution.py:1689
  548.3 28.9 %collective-permute-start.4 = (bf16[256,2048]{1,0:T(8,128)(2,1)}, bf16[256,2048]{1,0:T(8,128)(2,1)S(1)}, u32[]{:S(2)}, u32[]{:S(2)}) collective-permute-start(bf16[256,2048]{1,0:T(8,128)(2,1)} %get-tuple-element.95.own_ref), channel_id=1, source_target_pairs={{0,1},{1,0},{2,3},{3,2},{4,5},{5,4},{6,7},{7,6},{8,9},{9,8},{10,11... | collective-permute-start | bytes 3145736 | tf_op jit(solution)/shard_map/ppermute | solution.py:1689
  549.5 1.0 copy-start.7
  577.2 12.5 %copy-start.6 = (bf16[256,2048]{1,0:T(8,128)(2,1)}, bf16[256,2048]{1,0:T(8,128)(2,1)S(1)}, u32[]{:S(2)}) copy-start(bf16[256,2048]{1,0:T(8,128)(2,1)S(1)} %collective-permute-done.4.other_ref) | copy-start | bytes 3145732
Sparse Core Ops, SparseCore 0:
  57.4 153.7 all-gather.2
  212.7 71.2 all-gather.4
  286.3 76.7 reduce-scatter.4
  365.3 77.2 reduce-scatter.6
  444.8 77.2 reduce-scatter.8
  524.9 52.8 reduce-scatter.10

commit v7 on v6

--- a/solution.py
+++ b/solution.py
@@ -478,7 +478,7 @@
     core_side = send(7, spot(1 - side, row, core), spot(1 - side, row, core), near_core)
     row_b.wait_recv()
     core_row = send(8, spot(side, 1 - row, core), spot(side, 1 - row, core), near_core)
-    for far in range(1, lines - 1):
+    for far in range(1, lines - 2):
         line.take(far)
     away_a.wait_recv()
     core_away_a = send(
@@ -488,6 +488,8 @@
     core_away_b = send(
         10, spot(1 - side, 1 - row, core, 1), spot(1 - side, 1 - row, core, 1), near_core
     )
+    if lines > 2:
+        line.take(lines - 2)
     for copy in (core_own, core_side, core_row, core_away_a, core_away_b):
         copy.wait_recv()
     for copy in copies:
@@ -1388,7 +1390,7 @@
 
 
 def final_forms(own, other, dtype, *grads):
-    steps = 4
+    steps = 2
     rows, width = own.shape
     halves = pl.BlockSpec((rows // steps, width), lambda i: (i, 0))
     whole = pl.BlockSpec((2, rows // steps, width), lambda i: (0, i, 0))

time: 610 us -> 609 us (level)
  transfers between devices with their start and end apart: 11 -> 11, of which waited for: 1 -> 2; matrix products, arithmetic and copies ran while one was open for 13% -> 13% of each run, Pallas kernels for 72% -> 71%
where the time goes in v7:
time: 609 us; the launch traced here: 601 us
  Pallas kernels  496 us (81%)
  matrix products  54.6 us (9%)
  other arithmetic  15.3 us (3%)
  between operations  14.9 us (2%)
  local copies, waits for them, and re-layouts  10.7 us (2%)
    pallas_call x3, Pallas kernels, plane_gather(): pl.pallas_call(functools.partial(gather_kernel, rows, 8 if pair is not No...  131 us
    pallas_call x2, Pallas kernels, product_scatter(): pl.pallas_call(functools.partial(scatter_kernel, rows, swap is not None,...  103 us
    pallas_call x1, Pallas kernels, attend_back(): pl.pallas_call(functools.partial(attend_back_kernel, seqs, rows), out_sha...  61.4 us
    pallas_call x1, Pallas kernels, ffn_back(): pl.pallas_call(functools.partial(ffn_back_kernel, rows), out_shape=(jax.S...  58.9 us
    pallas_call x1, Pallas kernels, open_weights(): pl.pallas_call(functools.partial(open_kernel, planes), out_shape=(jax.Sha...  50 us
    dot_general x4, matrix products, matmul_t(): lax.dot_general(left_op, right_op, (((0,), (0,)), ((), ())), preferred_el...  37.4 us
    pallas_call x1, Pallas kernels, ffn(): pl.pallas_call(ffn_kernel, grid=(total // rows,), out_shape=(jax.ShapeDty...  25.2 us
    pallas_call x1, Pallas kernels, attend(): pl.pallas_call(functools.partial(attend_kernel, length), grid=(seqs, pair...  21.6 us
  transfers between devices with their start and end apart: 11, of which 2 were waited for; matrix products, arithmetic and copies ran while one was open for 13% of the time, Pallas kernels for 71%

profile of v7, /device:TPU:0, one launch (start us, length us, event | category | flops | bytes accessed | tf_op | source)
XLA Modules:
  0.0 601.3 jit_solution(8600108656192092632)
XLA Ops:
  7.3 50.0 %open_weights.1 = (bf16[2048,640]{1,0:T(8,128)(2,1)}, bf16[512,2048]{1,0:T(8,128)(2,1)}, bf16[512,128]{1,0:T(8,128)(2,1)}, bf16[512,896]{1,0:T(8,128)(2,1)}) custom-call(bf16[128,1024]{1,0:T(8,128)(2,1)} %q_ref.1, bf16[128,256]{1,0:T(8,128)(2,1)} %key_ref.1, bf16[128,256]{1,0:T(8,128)(2,1)} %value_ref.1, bf16[1024,128]{1,0:T(8,128)(2,1)} %out_ref.1, ...), custom_call_target="tpu_custom_call" | custom-call | bytes 1024 | tf_op jit(solution)/shard_map/open_weights/pallas_call | solution.py:1649
  57.3 1.6 collective-permute-start.1
  58.9 2.4 multiply_reduce_fusion
  62.0 44.4 %plane_gather.3 = (bf16[2048,2048]{1,0:T(8,128)(2,1)}, f32[16,8,128]{2,1,0:T(8,128)}) custom-call(bf16[256,2048]{1,0:T(8,128)(2,1)} %get-tuple-element.67.block_ref, f32[8,128]{1,0:T(8,128)} %maximum_convert_fusion.refs_0_), custom_call_target="tpu_custom_call" | custom-call | bytes 1024 | tf_op jit(solution)/shard_map/plane_gather/pallas_call | solution.py:529
  107.2 5.2 fusion
  112.3 1.5 slice_bitcast_fusion.3
  116.5 10.1 %fusion.4.q_ref.kv_ref = f32[2048,384]{1,0:T(8,128)} fusion(bf16[2048,2048]{1,0:T(8,128)(2,1)} %get-tuple-element.68, f32[2048]{0:T(1024)S(1)} %bitcast.35, f32[2048]{0:T(1024)S(1)} %add_rsqrt_fusion, bf16[2048,640]{1,0:T(8,128)(2,1)} %get-tuple-element.70.right), kind=kOutput, calls=%fused_computation.11 | convolution fusion | flops 3238002688 | bytes 13123584 | tf_op jit(solution)/shard_map/dot_general | solution.py:1740
  126.6 21.6 %attend.1 = (bf16[2048,256]{1,0:T(8,128)(2,1)}, bf16[2048,256]{1,0:T(8,128)(2,1)}, bf16[2048,128]{1,0:T(8,128)(2,1)}, f32[2048,256]{1,0:T(8,128)}) custom-call(f32[2048,384]{1,0:T(8,128)} %fusion.4.q_ref.kv_ref, f32[2048,384]{1,0:T(8,128)} %fusion.4.q_ref.kv_ref, f32[1024,128]{1,0:T(8,128)} %copy.24.cos_ref, f32[1024,128]{1,0:T(8,128)} %copy.25.sin_ref), custom_call_target="tpu_custom_call" | custom-call | flops 4294967296 | bytes 6291456 | tf_op jit(solution)/shard_map/attend/pallas_call | solution.py:1052
  148.2 43.9 %product_scatter.2 = f32[256,2048]{1,0:T(8,128)} custom-call(bf16[2048,256]{1,0:T(8,128)(2,1)} %get-tuple-element.74.left, bf16[2048,640]{1,0:T(8,128)(2,1)} %get-tuple-element.70.right), custom_call_target="tpu_custom_call" | custom-call | bytes 1024 | tf_op jit(solution)/shard_map/product_scatter/pallas_call | solution.py:774
  192.1 1.9 multiply_reduce_fusion.1
  195.4 1.2 multiply_convert_fusion.block_ref
  196.6 40.6 %plane_gather.4 = (bf16[2048,2048]{1,0:T(8,128)(2,1)}, bf16[2048,128]{1,0:T(8,128)(2,1)}) custom-call(bf16[256,2048]{1,0:T(8,128)(2,1)} %multiply_convert_fusion.block_ref, bf16[512,128]{1,0:T(8,128)(2,1)} %get-tuple-element.76.refs_0_), custom_call_target="tpu_custom_call" | custom-call | bytes 1024 | tf_op jit(solution)/shard_map/plane_gather/pallas_call | solution.py:529
  237.3 25.2 %ffn.1 = (bf16[2048,1024]{1,0:T(8,128)(2,1)}, bf16[2048,1024]{1,0:T(8,128)(2,1)}, bf16[2048,1024]{1,0:T(8,128)(2,1)}) custom-call(bf16[2048,2048]{1,0:T(8,128)(2,1)} %get-tuple-element.77.in_ref.refs_0_, bf16[2048,2048]{1,0:T(8,128)(2,1)} %all-gather.3.cloned.1.call-done.w_ref.right_ref), custom_call_target="tpu_custom_call" | custom-call | bytes 1024 | tf_op jit(solution)/shard_map/ffn/pallas_call | solution.py:967
  262.4 3.2 lay.1
  266.5 10.9 %convolution_convert_fusion.1 = bf16[2048,1024]{1,0:T(8,128)(2,1)} fusion(bf16[2048,2048]{1,0:T(8,128)(2,1)S(1)} %bitcast.30, bf16[2048,1024]{1,0:T(8,128)(2,1)S(1)} %copy-done.3), kind=kOutput, calls=%fused_computation.6 | convolution fusion | flops 8592031744 | bytes 16777216 | tf_op jit(solution)/shard_map/dot_general | solution.py:55
  279.4 4.6 all-gather.5.cloned.1.call-done.down_ref.right_ref
  284.0 58.9 %ffn_back.1 = (f32[256,2048]{1,0:T(8,128)}, bf16[256,2048]{1,0:T(8,128)(2,1)}, f32[8,2048]{1,0:T(8,128)}, bf16[2048,1024]{1,0:T(8,128)(2,1)}, bf16[2048,1024]{1,0:T(8,128)(2,1)}) custom-call(bf16[2,256,2048]{2,1,0:T(8,128)(2,1)} %own_ref.2, bf16[2,256,2048]{2,1,0:T(8,128)(2,1)} %collective-permute-done.far_ref, ...), custom_call_target="tpu_custom_call" | custom-call | bytes 1024 | tf_op jit(solution)/shard_map/ffn_back/pallas_call | solution.py:916
  342.9 14.0 %convolution_convert_fusion = bf16[2048,1024]{1,0:T(8,128)(2,1)} fusion(bf16[2048,2048]{1,0:T(8,128)(2,1)} %get-tuple-element.77.in_ref.refs_0_, bf16[2048,1024]{1,0:T(8,128)(2,1)} %get-tuple-element.86), kind=kOutput, calls=%fused_computation.5 | convolution fusion | flops 8592031744 | bytes 16777216 | tf_op jit(solution)/shard_map/dot_general | solution.py:55
  357.0 45.8 %plane_gather.5 = (bf16[2048,2048]{1,0:T(8,128)(2,1)}, bf16[2048,1024]{1,0:T(8,128)(2,1)}) custom-call(bf16[256,2048]{1,0:T(8,128)(2,1)} %get-tuple-element.87.block_ref, bf16[2048,2048]{1,0:T(8,128)(2,1)} %get-tuple-element.77.in_ref.refs_0_, bf16[2048,1024]{1,0:T(8,128)(2,1)} %get-tuple-element.88.refs_1_), custom_call_target="tpu_custom_call" | custom-call | bytes 1024 | tf_op jit(solution)/shard_map/plane_gather/pallas_call | solution.py:529
  403.0 7.1 %convolution_convert_fusion.4.up_ref = bf16[2048,256]{1,0:T(8,128)(2,1)} fusion(bf16[2048,2048]{1,0:T(8,128)(2,1)} %get-tuple-element.89, bf16[2048,640]{1,0:T(8,128)(2,1)} %get-tuple-element.70.right), kind=kOutput, calls=%fused_computation.10 | convolution fusion | flops 2148007936 | bytes 10485760 | tf_op jit(solution)/shard_map/dot_general | solution.py:1768
  410.1 3.6 convolution_convert_fusion.3
  413.8 61.4 %attend_back.1 = (bf16[2048,384]{1,0:T(8,128)(2,1)}, bf16[256,2048]{1,0:T(8,128)(2,1)}, bf16[4096,128]{1,0:T(8,128)(2,1)}) custom-call(bf16[2048,256]{1,0:T(8,128)(2,1)} %get-tuple-element.71.q_ref, bf16[2048,128]{1,0:T(8,128)(2,1)} %get-tuple-element.72.kv_ref, bf16[2048,256]{1,0:T(8,128)(2,1)} %convolution_convert_fusion.4.up_ref, ...), custom_call_target="tpu_custom_call" | custom-call | bytes 1024 | tf_op jit(solution)/shard_map/attend_back/pallas_call | solution.py:1212
  475.2 8.9 %convolution_convert_fusion.2 = bf16[2048,384]{1,0:T(8,128)(2,1)S(1)} fusion(bf16[2048,384]{1,0:T(8,128)(2,1)} %get-tuple-element.93.left, bf16[2048,2048]{1,0:T(8,128)(2,1)} %get-tuple-element.68, f32[2048]{0:T(1024)S(1)} %bitcast.36, f32[2048]{0:T(1024)S(1)} %add_rsqrt_fusion), kind=kOutput, calls=%fused_computation.7 | convolution fusion | flops 3238789120 | bytes 11550720 | tf_op jit(solution)/shard_map/dot_general | solution.py:55
  484.1 1.8 pad_maximum_fusion
  485.9 1.2 collective-permute-start.3
  487.1 1.6 convert_element_type.61.refs_1_
  489.5 58.8 %product_scatter.3 = (bf16[256,2048]{1,0:T(8,128)(2,1)}, f32[8,2048]{1,0:T(8,128)}, bf16[128,4096]{1,0:T(8,128)(2,1)}) custom-call(bf16[2048,384]{1,0:T(8,128)(2,1)} %get-tuple-element.93.left, bf16[2048,640]{1,0:T(8,128)(2,1)} %get-tuple-element.70.right, bf16[512,1024]{1,0:T(8,128)(2,1)} %reduce-scatter.7.cloned.1.call-done.refs_0_, ...), custom_call_target="tpu_custom_call" | custom-call | bytes 1024 | tf_op jit(solution)/shard_map/product_scatter/pallas_call | solution.py:774
  550.5 4.4 final_forms.2
  554.9 21.4 %gain_sum.1 = (f32[8,128]{1,0:T(8,128)}, bf16[128,4096]{1,0:T(8,128)(2,1)}) custom-call(f32[8,2048]{1,0:T(8,128)} %get-tuple-element.101.attn_term_ref, f32[8,2048]{1,0:T(8,128)} %get-tuple-element.102.ffn_term_ref, bf16[512,1024]{1,0:T(8,128)(2,1)} %reduce-scatter.9.cloned.1.call-done.up_ref), custom_call_target="tpu_custom_call" | custom-call | bytes 1024 | tf_op jit(solution)/shard_map/gain_sum/pallas_call | solution.py:1314
  576.4 1.3 slice_bitcast_fusion
  577.8 11.1 %last_swap.1 = (bf16[128,1024]{1,0:T(8,128)(2,1)}, bf16[128,256]{1,0:T(8,128)(2,1)}, bf16[128,256]{1,0:T(8,128)(2,1)}, bf16[1024,128]{1,0:T(8,128)(2,1)}) custom-call(bf16[512,640]{1,0:T(8,128)(2,1)} %reduce-scatter.11.cloned.1.call-done.attn_ref), custom_call_target="tpu_custom_call" | custom-call | bytes 1024 | tf_op jit(solution)/shard_map/last_swap/pallas_call | solution.py:1365
  589.0 5.0 final_forms.3
  (64 shorter events, 11.9 us)
Async XLA Ops:
  7.2 50.1 %copy-start = (bf16[2,256,2048]{2,1,0:T(8,128)(2,1)S(1)}, bf16[2,256,2048]{2,1,0:T(8,128)(2,1)}, u32[]{:S(2)}) copy-start(bf16[2,256,2048]{2,1,0:T(8,128)(2,1)} %own_ref.2) | copy-start | bytes 6291460
  7.2 54.2 %copy-start.9 = (bf16[128]{0:T(256)(128)(2,1)S(1)}, bf16[128]{0:T(256)(128)(2,1)}, u32[]{:S(2)}) copy-start(bf16[128]{0:T(256)(128)(2,1)} %param.12) | copy-start | bytes 772
  7.2 54.2 %copy-start.8 = (bf16[128]{0:T(256)(128)(2,1)S(1)}, bf16[128]{0:T(256)(128)(2,1)}, u32[]{:S(2)}) copy-start(bf16[128]{0:T(256)(128)(2,1)} %param.17) | copy-start | bytes 772
  7.2 230.0 %all-gather.3.cloned.1.call-start = ((), (), s32[]{:S(2)}) async-start(), calls=%async_computation.4 | async-start | bytes 10485760 | tf_op jit(solution)/shard_map/all_gather | solution.py:1735
  57.3 226.7 %all-gather.5.cloned.1.call-start = ((), (), s32[]{:S(2)}) async-start(), calls=%async_computation.5 | async-start | bytes 4587520 | tf_op jit(solution)/shard_map/all_gather | solution.py:1736
  57.3 205.1 %collective-permute-start.1 = (bf16[2,256,2048]{2,1,0:T(8,128)(2,1)S(1)}, bf16[2,256,2048]{2,1,0:T(8,128)(2,1)}, u32[]{:S(2)}, u32[]{:S(2)}) collective-permute-start(bf16[2,256,2048]{2,1,0:T(8,128)(2,1)S(1)} %copy-done), channel_id=1, source_target_pairs={{0,2},{2,0},{4,6},{6,4},{1,3},{3,1},{5,7},{7,5},{8,10},{10,8},{12,... | collective-permute-start | bytes 6291464 | tf_op jit(solution)/shard_map/ppermute | solution.py:1445
  106.4 87.7 %collective-permute-start = (bf16[2,256,2048]{2,1,0:T(8,128)(2,1)S(1)}, bf16[2,256,2048]{2,1,0:T(8,128)(2,1)}, u32[]{:S(2)}, u32[]{:S(2)}) collective-permute-start(bf16[2,256,2048]{2,1,0:T(8,128)(2,1)S(1)} %copy-done), channel_id=1, source_target_pairs={{0,4},{2,6},{4,0},{6,2},{1,5},{3,7},{5,1},{7,3},{8,12},{10,14},{12... | collective-permute-start | bytes 6291464 | tf_op jit(solution)/shard_map/ppermute | solution.py:1443
  107.1 306.6 %reduce-scatter.5.cloned.1.call-start = ((), (), s32[]{:S(2)}) async-start(), calls=%async_computation.6 | async-start | bytes 5242880 | tf_op jit(solution)/shard_map/reduce_scatter | solution.py:1753
  148.2 43.9 %copy-start.2 = (bf16[256,2048]{1,0:T(8,128)(2,1)S(1)}, bf16[256,2048]{1,0:T(8,128)(2,1)}, u32[]{:S(2)}) copy-start(bf16[256,2048]{1,0:T(8,128)(2,1)} %get-tuple-element.67.block_ref) | copy-start | bytes 3145732
  194.1 1.3 copy-start.1
  194.1 68.3 %collective-permute-start.2 = (bf16[2,256,2048]{2,1,0:T(8,128)(2,1)}, bf16[2,256,2048]{2,1,0:T(8,128)(2,1)}, u32[]{:S(2)}, u32[]{:S(2)}) collective-permute-start(bf16[2,256,2048]{2,1,0:T(8,128)(2,1)} %collective-permute-done.far_ref), channel_id=1, source_target_pairs={{0,2},{2,0},{4,6},{6,4},{1,3},{3,1},{5,7},{7,5},{8,10},{10,8},{12,... | collective-permute-start | bytes 6291464 | tf_op jit(solution)/shard_map/ppermute | solution.py:1445
  262.4 4.1 copy-start.3
  277.4 212.1 %reduce-scatter.7.cloned.1.call-start = ((), (), s32[]{:S(2)}) async-start(), calls=%async_computation.7 | async-start | bytes 5242880 | tf_op jit(solution)/shard_map/reduce_scatter | solution.py:1765
  356.9 198.0 %reduce-scatter.9.cloned.1.call-start = ((), (), s32[]{:S(2)}) async-start(), calls=%async_computation.8 | async-start | bytes 5242880 | tf_op jit(solution)/shard_map/reduce_scatter | solution.py:1767
  402.8 175.1 %reduce-scatter.11.cloned.1.call-start = ((), (), s32[]{:S(2)}) async-start(), calls=%async_computation.9 | async-start | bytes 3276800 | tf_op jit(solution)/shard_map/reduce_scatter | solution.py:1788
  403.0 7.1 %copy-start.5 = (bf16[2048,256]{1,0:T(8,128)(2,1)S(1)}, bf16[2048,256]{1,0:T(8,128)(2,1)}, u32[]{:S(2)}) copy-start(bf16[2048,256]{1,0:T(8,128)(2,1)} %get-tuple-element.74.left) | copy-start | bytes 3145732
  403.0 7.1 %copy-start.10 = (bf16[2048,2048]{1,0:T(8,128)(2,1)S(1)}, bf16[2048,2048]{1,0:T(8,128)(2,1)}, u32[]{:S(2)}) copy-start(bf16[2048,2048]{1,0:T(8,128)(2,1)} %get-tuple-element.89) | copy-start | bytes 25165828
  475.2 8.9 %copy-start.4 = (bf16[2048,256]{1,0:T(8,128)(2,1)S(1)}, bf16[2048,256]{1,0:T(8,128)(2,1)}, u32[]{:S(2)}) copy-start(bf16[2048,256]{1,0:T(8,128)(2,1)} %convolution_convert_fusion.3) | copy-start | bytes 3145732
  485.9 63.6 %collective-permute-start.3 = (bf16[256,2048]{1,0:T(8,128)(2,1)}, bf16[256,2048]{1,0:T(8,128)(2,1)S(1)}, u32[]{:S(2)}, u32[]{:S(2)}) collective-permute-start(bf16[256,2048]{1,0:T(8,128)(2,1)} %get-tuple-element.91.own_ref), channel_id=1, source_target_pairs={{0,1},{1,0},{2,3},{3,2},{4,5},{5,4},{6,7},{7,6},{8,9},{9,8},{10,11... | collective-permute-start | bytes 3145736 | tf_op jit(solution)/shard_map/ppermute | solution.py:1691
  548.3 28.0 %collective-permute-start.4 = (bf16[256,2048]{1,0:T(8,128)(2,1)}, bf16[256,2048]{1,0:T(8,128)(2,1)S(1)}, u32[]{:S(2)}, u32[]{:S(2)}) collective-permute-start(bf16[256,2048]{1,0:T(8,128)(2,1)} %get-tuple-element.95.own_ref), channel_id=1, source_target_pairs={{0,1},{1,0},{2,3},{3,2},{4,5},{5,4},{6,7},{7,6},{8,9},{9,8},{10,11... | collective-permute-start | bytes 3145736 | tf_op jit(solution)/shard_map/ppermute | solution.py:1691
  549.5 1.0 copy-start.7
  576.4 12.6 %copy-start.6 = (bf16[256,2048]{1,0:T(8,128)(2,1)}, bf16[256,2048]{1,0:T(8,128)(2,1)S(1)}, u32[]{:S(2)}) copy-start(bf16[256,2048]{1,0:T(8,128)(2,1)S(1)} %collective-permute-done.4.other_ref) | copy-start | bytes 3145732
Sparse Core Ops, SparseCore 0:
  57.4 153.7 all-gather.2
  212.7 71.2 all-gather.4
  286.3 76.7 reduce-scatter.4
  365.3 77.2 reduce-scatter.6
  444.8 77.2 reduce-scatter.8
  524.9 52.8 reduce-scatter.10
